TPU v7x, 32 devices: a whole 2x2x4 slice. The times are simulated.
32 devices in a mesh: dp: 4 (over y, core), fsdp: 8 (over z, x).
Axes of the slice: x: 2, y: 2, z: 4, core: 2. Of those that a mesh axis runs over, the one named last changes fastest.
Arguments:
- tokens: bfloat16 [64, 512, 768], P(('dp', 'fsdp')), may hold values from -6 to 6
- cotangent: bfloat16 [64, 512, 768], P(('dp', 'fsdp')), may hold values from -6 to 6
- lengths: int32 [4, 16], P('dp'), may hold values from 1 to 512, 6144 in all within a row
- deal: int32 [4, 16], P('dp'), may hold values from 0 to 15, each once within a row
- w_query: bfloat16 [768, 768], P(('dp', 'fsdp')), may hold values from -0.21875 to 0.21875
- b_query: bfloat16 [768], P(('dp', 'fsdp')), may hold values from -1 to 1
- w_key: bfloat16 [768, 768], P(('dp', 'fsdp')), may hold values from -0.21875 to 0.21875
- w_value: bfloat16 [768, 768], P(('dp', 'fsdp')), may hold values from -0.21875 to 0.21875
- b_value: bfloat16 [768], P(('dp', 'fsdp')), may hold values from -1 to 1
- w_out: bfloat16 [768, 768], P(('dp', 'fsdp')), may hold values from -1.25 to 1.25
- b_out: bfloat16 [768], P(('dp', 'fsdp')), may hold values from -1 to 1
- norm1_gain: bfloat16 [768], P(('dp', 'fsdp')), may hold values from 0.5 to 1.5
- norm1_bias: bfloat16 [768], P(('dp', 'fsdp')), may hold values from -1 to 1
- w_in: bfloat16 [768, 3072], P(('dp', 'fsdp')), may hold values from -0.21875 to 0.21875
- b_in: bfloat16 [3072], P(('dp', 'fsdp')), may hold values from -1 to 1
- w_down: bfloat16 [3072, 768], P(('dp', 'fsdp')), may hold values from -0.109375 to 0.109375
- b_down: bfloat16 [768], P(('dp', 'fsdp')), may hold values from -1 to 1
- norm2_gain: bfloat16 [768], P(('dp', 'fsdp')), may hold values from 0.5 to 1.5
- norm2_bias: bfloat16 [768], P(('dp', 'fsdp')), may hold values from -1 to 1
Outputs:
- layer_out: bfloat16 [64, 512, 768], P(('dp', 'fsdp'))
- input_grad: bfloat16 [64, 512, 768], P(('dp', 'fsdp'))
- grad_w_query: float32 [768, 768], P(('dp', 'fsdp'))
- grad_b_query: float32 [768], P(('dp', 'fsdp'))
- grad_w_key: float32 [768, 768], P(('dp', 'fsdp'))
- grad_w_value: float32 [768, 768], P(('dp', 'fsdp'))
- grad_b_value: float32 [768], P(('dp', 'fsdp'))
- grad_w_out: float32 [768, 768], P(('dp', 'fsdp'))
- grad_b_out: float32 [768], P(('dp', 'fsdp'))
- grad_norm1_gain: float32 [768], P(('dp', 'fsdp'))
- grad_norm1_bias: float32 [768], P(('dp', 'fsdp'))
- grad_w_in: float32 [768, 3072], P(('dp', 'fsdp'))
- grad_b_in: float32 [3072], P(('dp', 'fsdp'))
- grad_w_down: float32 [3072, 768], P(('dp', 'fsdp'))
- grad_b_down: float32 [768], P(('dp', 'fsdp'))
- grad_norm2_gain: float32 [768], P(('dp', 'fsdp'))
- grad_norm2_bias: float32 [768], P(('dp', 'fsdp'))
Inputs may be any that keep to these rules, and one draw needn't show every extreme that they name: A row holds the lengths of one group's 16 sequences in the given order; it sums to 6144 and its longest is exactly 512. `deal`: each row is a permutation; bucket b of a group is slot b % 2 of the group's device b // 2 along fsdp.
All inputs are finite; a program needn't handle non-finite values.
Results may differ from a plain program's by a relative error of at most 0.014.
Values may be sent and summed in bfloat16 or wider, within the bound.
No kernel may reach another device: no remote copies, remote signals or barrier semaphores. Data moves between devices by JAX's collectives and lax.ppermute only.
A program may use at most 192 MiB of HBM per device.

v0:
```python
import jax
import jax.numpy as jnp
from jax import lax
from jax.sharding import PartitionSpec as P

HD = 64


norm_eps = 1e-12
half_root = 0.7071067811865476
slope_scale = 0.3989422804014327


def standardize(values):
    centre = values - jnp.mean(values, axis=-1, keepdims=True)
    spread = lax.rsqrt(jnp.mean(centre * centre, axis=-1, keepdims=True) + norm_eps)
    return (centre * spread, spread)


def norm_back(d_normed, normed, spread):
    return spread * (
        d_normed
        - jnp.mean(d_normed, axis=-1, keepdims=True)
        - normed * jnp.mean(d_normed * normed, axis=-1, keepdims=True)
    )


def gelu_value(values):
    return 0.5 * values * (1.0 + lax.erf(values * half_root))


def gelu_slope(values):
    return (
        0.5 * (1.0 + lax.erf(values * half_root))
        + values * jnp.exp(-0.5 * values * values) * slope_scale
    )


def matmul(left, right):
    return jnp.dot(left, right, preferred_element_type=jnp.float32)


def left_times(left, right):
    return jnp.einsum("ti,to->io", left, right, preferred_element_type=jnp.float32)


def right_times(grads, weight):
    return jnp.einsum("to,io->ti", grads, weight, preferred_element_type=jnp.float32)


def scores_of(query, key_rows, valid):
    rows = query.shape[0]
    raw = jnp.einsum(
        "qhd,khd->hqk",
        query.reshape(rows, -1, HD),
        key_rows.reshape(rows, -1, HD),
        preferred_element_type=jnp.float32,
    )
    return jnp.where(valid[None, None, :], raw * HD ** (-0.5), -1e30)


def forward_slot(inputs, length, weights):
    (
        w_query,
        b_query,
        w_key,
        w_value,
        b_value,
        w_out,
        b_out,
        gain_one,
        shift_one,
        w_in,
        b_in,
        w_down,
        b_down,
        gain_two,
        shift_two,
    ) = weights
    rows = inputs.shape[0]
    valid = jnp.arange(rows) < length
    query = (matmul(inputs, w_query) + b_query.astype(jnp.float32)).astype(jnp.bfloat16)
    key_rows = matmul(inputs, w_key).astype(jnp.bfloat16)
    value_rows = (matmul(inputs, w_value) + b_value.astype(jnp.float32)).astype(jnp.bfloat16)
    scores = scores_of(query, key_rows, valid)
    top = jnp.max(scores, axis=-1, keepdims=True)
    total = jnp.log(jnp.sum(jnp.exp(scores - top), axis=-1, keepdims=True)) + top
    probs = jnp.exp(scores - total).astype(jnp.bfloat16)
    context = (
        jnp.einsum(
            "hqk,khd->qhd",
            probs,
            value_rows.reshape(rows, -1, HD),
            preferred_element_type=jnp.float32,
        )
        .reshape(rows, -1)
        .astype(jnp.bfloat16)
    )
    attended = matmul(context, w_out) + b_out.astype(jnp.float32)
    middle_norm, middle_spread = standardize(inputs.astype(jnp.float32) + attended)
    middle = middle_norm * gain_one.astype(jnp.float32) + shift_one.astype(jnp.float32)
    middle_low = middle.astype(jnp.bfloat16)
    hidden = matmul(middle_low, w_in) + b_in.astype(jnp.float32)
    active = gelu_value(hidden).astype(jnp.bfloat16)
    branch = matmul(active, w_down) + b_down.astype(jnp.float32)
    final_norm, final_spread = standardize(middle + branch)
    result = final_norm * gain_two.astype(jnp.float32) + shift_two.astype(jnp.float32)
    output = jnp.where(valid[:, None], result, 0.0).astype(jnp.bfloat16)
    saved = (
        inputs,
        query,
        key_rows,
        value_rows,
        total,
        context,
        middle_norm,
        middle_spread,
        middle_low,
        hidden,
        active,
        final_norm,
        final_spread,
        valid,
    )
    return (output, saved)


def backward_slot(saved, upstream, weights):
    (
        w_query,
        b_query,
        w_key,
        w_value,
        b_value,
        w_out,
        b_out,
        gain_one,
        shift_one,
        w_in,
        b_in,
        w_down,
        b_down,
        gain_two,
        shift_two,
    ) = weights
    (
        inputs,
        query,
        key_rows,
        value_rows,
        total,
        context,
        middle_norm,
        middle_spread,
        middle_low,
        hidden,
        active,
        final_norm,
        final_spread,
        valid,
    ) = saved
    rows = inputs.shape[0]
    d_result = jnp.where(valid[:, None], upstream.astype(jnp.float32), 0.0)
    grad_gain_two = jnp.sum(d_result * final_norm, axis=0)
    grad_shift_two = jnp.sum(d_result, axis=0)
    d_final = norm_back(d_result * gain_two.astype(jnp.float32), final_norm, final_spread)
    d_branch = d_final.astype(jnp.bfloat16)
    grad_b_down = jnp.sum(d_branch.astype(jnp.float32), axis=0)
    grad_w_down = left_times(active, d_branch)
    d_hidden = (right_times(d_branch, w_down) * gelu_slope(hidden)).astype(jnp.bfloat16)
    grad_b_in = jnp.sum(d_hidden.astype(jnp.float32), axis=0)
    grad_w_in = left_times(middle_low, d_hidden)
    d_middle = d_final + right_times(d_hidden, w_in)
    grad_gain_one = jnp.sum(d_middle * middle_norm, axis=0)
    grad_shift_one = jnp.sum(d_middle, axis=0)
    d_sum = norm_back(d_middle * gain_one.astype(jnp.float32), middle_norm, middle_spread)
    d_attended = d_sum.astype(jnp.bfloat16)
    grad_b_out = jnp.sum(d_attended.astype(jnp.float32), axis=0)
    grad_w_out = left_times(context, d_attended)
    d_context = right_times(d_attended, w_out).astype(jnp.bfloat16).reshape(rows, -1, HD)
    scores = scores_of(query, key_rows, valid)
    probs = jnp.exp(scores - total)
    d_probs = jnp.einsum(
        "qhd,khd->hqk",
        d_context,
        value_rows.reshape(rows, -1, HD),
        preferred_element_type=jnp.float32,
    )
    d_value = (
        jnp.einsum(
            "hqk,qhd->khd",
            probs.astype(jnp.bfloat16),
            d_context,
            preferred_element_type=jnp.float32,
        )
        .reshape(rows, -1)
        .astype(jnp.bfloat16)
    )
    d_scores = (probs * (d_probs - jnp.sum(probs * d_probs, axis=-1, keepdims=True))).astype(
        jnp.bfloat16
    )
    scale = HD ** (-0.5)
    d_query = (
        (
            jnp.einsum(
                "hqk,khd->qhd",
                d_scores,
                key_rows.reshape(rows, -1, HD),
                preferred_element_type=jnp.float32,
            )
            * scale
        )
        .reshape(rows, -1)
        .astype(jnp.bfloat16)
    )
    d_key = (
        (
            jnp.einsum(
                "hqk,qhd->khd",
                d_scores,
                query.reshape(rows, -1, HD),
                preferred_element_type=jnp.float32,
            )
            * scale
        )
        .reshape(rows, -1)
        .astype(jnp.bfloat16)
    )
    grad_b_query = jnp.sum(d_query.astype(jnp.float32), axis=0)
    grad_b_value = jnp.sum(d_value.astype(jnp.float32), axis=0)
    grad_w_query = left_times(inputs, d_query)
    grad_w_key = left_times(inputs, d_key)
    grad_w_value = left_times(inputs, d_value)
    d_inputs = (
        d_sum
        + right_times(d_query, w_query)
        + right_times(d_key, w_key)
        + right_times(d_value, w_value)
    )
    grads = (
        grad_w_query,
        grad_b_query,
        grad_w_key,
        grad_w_value,
        grad_b_value,
        grad_w_out,
        grad_b_out,
        grad_gain_one,
        grad_shift_one,
        grad_w_in,
        grad_b_in,
        grad_w_down,
        grad_b_down,
        grad_gain_two,
        grad_shift_two,
    )
    return (grads, d_inputs)


def per_device(
    tokens,
    cotangent,
    lengths,
    deal,
    w_query,
    b_query,
    w_key,
    w_value,
    b_value,
    w_out,
    b_out,
    norm1_gain,
    norm1_bias,
    w_in,
    b_in,
    w_down,
    b_down,
    norm2_gain,
    norm2_bias,
):
    slots = tokens.shape[0]
    position = lax.axis_index("fsdp")
    deal_row = deal[0]
    length_row = lengths[0]
    owned = position * slots + jnp.arange(slots, dtype=jnp.int32)
    chosen = deal_row[None, :] == owned[:, None]
    my_lengths = jnp.sum(jnp.where(chosen, length_row[None, :], 0), axis=1)
    select = (deal_row[None, :] == owned[:, None]).astype(jnp.bfloat16)
    moved = jnp.einsum(
        "ms,scd->mcd",
        select,
        lax.all_gather(tokens, "fsdp", axis=0, tiled=True),
        preferred_element_type=jnp.float32,
    )
    mine = moved.astype(jnp.bfloat16)
    saved_list = []
    outputs = []
    for slot in range(slots):
        weights = (
            lax.all_gather(w_query, ("dp", "fsdp"), axis=0, tiled=True),
            lax.all_gather(b_query, ("dp", "fsdp"), axis=0, tiled=True),
            lax.all_gather(w_key, ("dp", "fsdp"), axis=0, tiled=True),
            lax.all_gather(w_value, ("dp", "fsdp"), axis=0, tiled=True),
            lax.all_gather(b_value, ("dp", "fsdp"), axis=0, tiled=True),
            lax.all_gather(w_out, ("dp", "fsdp"), axis=0, tiled=True),
            lax.all_gather(b_out, ("dp", "fsdp"), axis=0, tiled=True),
            lax.all_gather(norm1_gain, ("dp", "fsdp"), axis=0, tiled=True),
            lax.all_gather(norm1_bias, ("dp", "fsdp"), axis=0, tiled=True),
            lax.all_gather(w_in, ("dp", "fsdp"), axis=0, tiled=True),
            lax.all_gather(b_in, ("dp", "fsdp"), axis=0, tiled=True),
            lax.all_gather(w_down, ("dp", "fsdp"), axis=0, tiled=True),
            lax.all_gather(b_down, ("dp", "fsdp"), axis=0, tiled=True),
            lax.all_gather(norm2_gain, ("dp", "fsdp"), axis=0, tiled=True),
            lax.all_gather(norm2_bias, ("dp", "fsdp"), axis=0, tiled=True),
        )
        output, saved = forward_slot(mine[slot], my_lengths[slot], weights)
        outputs.append(output)
        saved_list.append(saved)
    grad_totals = None
    grad_shards = None
    input_grads = [None] * slots
    for slot in reversed(range(slots)):
        weights = (
            lax.all_gather(w_query, ("dp", "fsdp"), axis=0, tiled=True),
            lax.all_gather(b_query, ("dp", "fsdp"), axis=0, tiled=True),
            lax.all_gather(w_key, ("dp", "fsdp"), axis=0, tiled=True),
            lax.all_gather(w_value, ("dp", "fsdp"), axis=0, tiled=True),
            lax.all_gather(b_value, ("dp", "fsdp"), axis=0, tiled=True),
            lax.all_gather(w_out, ("dp", "fsdp"), axis=0, tiled=True),
            lax.all_gather(b_out, ("dp", "fsdp"), axis=0, tiled=True),
            lax.all_gather(norm1_gain, ("dp", "fsdp"), axis=0, tiled=True),
            lax.all_gather(norm1_bias, ("dp", "fsdp"), axis=0, tiled=True),
            lax.all_gather(w_in, ("dp", "fsdp"), axis=0, tiled=True),
            lax.all_gather(b_in, ("dp", "fsdp"), axis=0, tiled=True),
            lax.all_gather(w_down, ("dp", "fsdp"), axis=0, tiled=True),
            lax.all_gather(b_down, ("dp", "fsdp"), axis=0, tiled=True),
            lax.all_gather(norm2_gain, ("dp", "fsdp"), axis=0, tiled=True),
            lax.all_gather(norm2_bias, ("dp", "fsdp"), axis=0, tiled=True),
        )
        grads, d_inputs = backward_slot(saved_list[slot], cotangent[slot], weights)
        input_grads[slot] = d_inputs.astype(jnp.bfloat16)
        grad_totals = grads if grad_totals is None else jax.tree.map(jnp.add, grad_totals, grads)
    grad_shards = (
        lax.psum_scatter(grad_totals[0], ("dp", "fsdp"), scatter_dimension=0, tiled=True),
        lax.psum_scatter(grad_totals[1], ("dp", "fsdp"), scatter_dimension=0, tiled=True),
        lax.psum_scatter(grad_totals[2], ("dp", "fsdp"), scatter_dimension=0, tiled=True),
        lax.psum_scatter(grad_totals[3], ("dp", "fsdp"), scatter_dimension=0, tiled=True),
        lax.psum_scatter(grad_totals[4], ("dp", "fsdp"), scatter_dimension=0, tiled=True),
        lax.psum_scatter(grad_totals[5], ("dp", "fsdp"), scatter_dimension=0, tiled=True),
        lax.psum_scatter(grad_totals[6], ("dp", "fsdp"), scatter_dimension=0, tiled=True),
        lax.psum_scatter(grad_totals[7], ("dp", "fsdp"), scatter_dimension=0, tiled=True),
        lax.psum_scatter(grad_totals[8], ("dp", "fsdp"), scatter_dimension=0, tiled=True),
        lax.psum_scatter(grad_totals[9], ("dp", "fsdp"), scatter_dimension=0, tiled=True),
        lax.psum_scatter(grad_totals[10], ("dp", "fsdp"), scatter_dimension=0, tiled=True),
        lax.psum_scatter(grad_totals[11], ("dp", "fsdp"), scatter_dimension=0, tiled=True),
        lax.psum_scatter(grad_totals[12], ("dp", "fsdp"), scatter_dimension=0, tiled=True),
        lax.psum_scatter(grad_totals[13], ("dp", "fsdp"), scatter_dimension=0, tiled=True),
        lax.psum_scatter(grad_totals[14], ("dp", "fsdp"), scatter_dimension=0, tiled=True),
    )
    grad_stack = jnp.stack(input_grads)
    given_targets = lax.dynamic_slice_in_dim(deal_row, position * slots, slots)
    piece = lax.all_gather(grad_stack, "fsdp", axis=0, tiled=True)
    places = jnp.arange(piece.shape[0], dtype=jnp.int32)
    select = (given_targets[:, None] == places[None, :]).astype(jnp.bfloat16)
    moved = jnp.einsum("ms,scd->mcd", select, piece, preferred_element_type=jnp.float32)
    input_grad = moved.astype(jnp.bfloat16)
    layer_out = jnp.stack(outputs)
    return (layer_out, input_grad) + tuple(grad_shards)


def solution(mesh):
    placed = (
        P(("dp", "fsdp"), None, None),
        P(("dp", "fsdp"), None, None),
        P("dp", None),
        P("dp", None),
        P(("dp", "fsdp"), None),
        P(("dp", "fsdp")),
        P(("dp", "fsdp"), None),
        P(("dp", "fsdp"), None),
        P(("dp", "fsdp")),
        P(("dp", "fsdp"), None),
        P(("dp", "fsdp")),
        P(("dp", "fsdp")),
        P(("dp", "fsdp")),
        P(("dp", "fsdp"), None),
        P(("dp", "fsdp")),
        P(("dp", "fsdp"), None),
        P(("dp", "fsdp")),
        P(("dp", "fsdp")),
        P(("dp", "fsdp")),
    )
    return jax.shard_map(
        per_device,
        mesh=mesh,
        in_specs=placed,
        out_specs=(
            P(("dp", "fsdp"), None, None),
            P(("dp", "fsdp"), None, None),
            P(("dp", "fsdp"), None),
            P(("dp", "fsdp")),
            P(("dp", "fsdp"), None),
            P(("dp", "fsdp"), None),
            P(("dp", "fsdp")),
            P(("dp", "fsdp"), None),
            P(("dp", "fsdp")),
            P(("dp", "fsdp")),
            P(("dp", "fsdp")),
            P(("dp", "fsdp"), None),
            P(("dp", "fsdp")),
            P(("dp", "fsdp"), None),
            P(("dp", "fsdp")),
            P(("dp", "fsdp")),
            P(("dp", "fsdp")),
        ),
        check_vma=False,
    )
```

profile of v0, /device:TPU:0, one launch (start us, length us, event | category | flops | bytes accessed | tf_op | source)
XLA Modules:
  0.0 1539.1 jit_solution(7384203677610678772)
XLA Ops:
  16.8 47.1 %all-reduce.19 = (bf16[768]{0:T(1024)(128)(2,1)S(1)}, bf16[768]{0:T(1024)(128)(2,1)S(1)}, bf16[768]{0:T(1024)(128)(2,1)S(1)}, bf16[768]{0:T(1024)(128)(2,1)S(1)}...) all-reduce(bf16[768]{0:T(1024)(128)(2,1)S(1)} %dynamic-update-slice, ...), channel_id=1, replica_groups=mesh['dp'=4,'fsdp'=8] {'dp','fsdp'}, use_global_device_ids=true, to_apply=%add | all-reduce | flops 9216 | bytes 36864
  66.9 123.1 %all-gather.9.cloned.1.call-done = bf16[16,512,768]{2,1,0:T(8,128)(2,1)} async-done(((bf16[2,512,768]{2,1,0:T(8,128)(2,1)}), bf16[16,512,768]{2,1,0:T(8,128)(2,1)}) %all-gather.9.cloned.1.call-update) | async-done | bytes 12582928 | tf_op jit(solution)/shard_map/all_gather | solution.py:292
  190.1 11.9 fusion.20
  204.8 40.6 %all-gather.11.cloned.1.call-done = bf16[768,768]{1,0:T(8,128)(2,1)} async-done(((bf16[24,768]{1,0:T(8,128)(2,1)}), bf16[768,768]{1,0:T(8,128)(2,1)}) %all-gather.11.cloned.1.call-update) | async-done | bytes 1179664 | tf_op jit(solution)/shard_map/all_gather | solution.py:303
  253.6 47.7 %all-gather.13.cloned.1.call-done = bf16[768,768]{1,0:T(8,128)(2,1)} async-done(((bf16[24,768]{1,0:T(8,128)(2,1)}), bf16[768,768]{1,0:T(8,128)(2,1)}) %all-gather.13.cloned.1.call-update) | async-done | bytes 1179664 | tf_op jit(solution)/shard_map/all_gather | solution.py:300
  311.9 45.4 %all-gather.15.cloned.1.call-done = bf16[768,768]{1,0:T(8,128)(2,1)} async-done(((bf16[24,768]{1,0:T(8,128)(2,1)}), bf16[768,768]{1,0:T(8,128)(2,1)}) %all-gather.15.cloned.1.call-update) | async-done | bytes 1179664 | tf_op jit(solution)/shard_map/all_gather | solution.py:302
  377.1 9.9 fusion.6
  391.8 21.3 %all-gather.17.cloned.1.call-done = bf16[768,768]{1,0:T(8,128)(2,1)} async-done(((bf16[24,768]{1,0:T(8,128)(2,1)}), bf16[768,768]{1,0:T(8,128)(2,1)}) %all-gather.17.cloned.1.call-update) | async-done | bytes 1179664 | tf_op jit(solution)/shard_map/all_gather | solution.py:305
  425.1 9.9 fusion.7
  441.1 37.3 %all-gather.19.cloned.1.call-done = bf16[768,3072]{1,0:T(8,128)(2,1)} async-done(((bf16[24,3072]{1,0:T(8,128)(2,1)}), bf16[768,3072]{1,0:T(8,128)(2,1)}) %all-gather.19.cloned.1.call-update) | async-done | bytes 4718608 | tf_op jit(solution)/shard_map/all_gather | solution.py:309
  486.5 7.7 multiply_convert_fusion.3
  494.2 49.2 %all-gather.21.cloned.1.call-done = bf16[3072,768]{1,0:T(8,128)(2,1)} async-done(((bf16[96,768]{1,0:T(8,128)(2,1)}), bf16[3072,768]{1,0:T(8,128)(2,1)}) %all-gather.21.cloned.1.call-update) | async-done | bytes 4718608 | tf_op jit(solution)/shard_map/all_gather | solution.py:311
  559.7 7.9 convert_reduce_fusion
  594.3 10.3 multiply_reduce_fusion
  626.0 10.6 multiply_reduce_fusion.1
  697.3 41.7 %all-reduce.18 = (f32[768]{0:T(1024)S(1)}, f32[768]{0:T(1024)S(1)}, f32[768]{0:T(1024)S(1)}, f32[768]{0:T(1024)S(1)}, f32[768]{0:T(1024)S(1)}, /*index=5*/f32[30...) all-reduce(f32[768]{0:T(1024)S(1)} %add.338, ...), channel_id=3, replica_groups=mesh['dp'=4,'fsdp'=8] {'dp','fsdp'}, use_global_device_ids=true, to_apply=%region_26.27.clone | all-reduce | flops 9216 | bytes 73728
  745.6 86.1 %all-gather.23.cloned.1.call-done = bf16[16,512,768]{2,1,0:T(8,128)(2,1)} async-done(((bf16[2,512,768]{2,1,0:T(8,128)(2,1)}), bf16[16,512,768]{2,1,0:T(8,128)(2,1)}) %all-gather.23.cloned.1.call-update) | async-done | bytes 12582928 | tf_op jit(solution)/shard_map/all_gather | solution.py:362
  831.7 12.0 fusion.23
  845.0 90.3 %reduce-scatter.13.cloned.1.call-done = f32[24,768]{1,0:T(8,128)} async-done(((f32[768,768]{1,0:T(8,128)}), f32[24,768]{1,0:T(8,128)}) %reduce-scatter.13.cloned.1.call-update) | async-done | bytes 73744 | tf_op jit(solution)/shard_map/reduce_scatter | solution.py:349
  935.3 104.4 %reduce-scatter.11.cloned.1.call-done = f32[24,768]{1,0:T(8,128)} async-done(((f32[768,768]{1,0:T(8,128)}), f32[24,768]{1,0:T(8,128)}) %reduce-scatter.11.cloned.1.call-update) | async-done | bytes 73744 | tf_op jit(solution)/shard_map/reduce_scatter | solution.py:347
  1039.8 104.6 %reduce-scatter.7.cloned.1.call-done = f32[24,768]{1,0:T(8,128)} async-done(((f32[768,768]{1,0:T(8,128)}), f32[24,768]{1,0:T(8,128)}) %reduce-scatter.7.cloned.1.call-update) | async-done | bytes 73744 | tf_op jit(solution)/shard_map/reduce_scatter | solution.py:344
  1144.3 104.3 %reduce-scatter.9.cloned.1.call-done = f32[24,768]{1,0:T(8,128)} async-done(((f32[768,768]{1,0:T(8,128)}), f32[24,768]{1,0:T(8,128)}) %reduce-scatter.9.cloned.1.call-update) | async-done | bytes 73744 | tf_op jit(solution)/shard_map/reduce_scatter | solution.py:346
  1248.7 141.7 %reduce-scatter.15.cloned.1.call-done = f32[24,3072]{1,0:T(8,128)} async-done(((f32[768,3072]{1,0:T(8,128)}), f32[24,3072]{1,0:T(8,128)}) %reduce-scatter.15.cloned.1.call-update) | async-done | bytes 294928 | tf_op jit(solution)/shard_map/reduce_scatter | solution.py:353
  1390.4 141.8 %reduce-scatter.17.cloned.1.call-done = f32[96,768]{1,0:T(8,128)} async-done(((f32[3072,768]{1,0:T(8,128)}), f32[96,768]{1,0:T(8,128)}) %reduce-scatter.17.cloned.1.call-update) | async-done | bytes 294928 | tf_op jit(solution)/shard_map/reduce_scatter | solution.py:355
  (347 shorter events, 216.7 us)
Async XLA Ops:
  7.3 182.8 %all-gather.9.cloned.1.call-start = ((), (), s32[]{:S(2)}) async-start(), calls=%async_computation.6 | async-start | bytes 14155776 | tf_op jit(solution)/shard_map/all_gather | solution.py:292
  8.0 237.3 %all-gather.11.cloned.1.call-start = ((), (), s32[]{:S(2)}) async-start(), calls=%async_computation.7 | async-start | bytes 1216512 | tf_op jit(solution)/shard_map/all_gather | solution.py:303
  8.8 292.6 %all-gather.13.cloned.1.call-start = ((), (), s32[]{:S(2)}) async-start(), calls=%async_computation.8 | async-start | bytes 1216512 | tf_op jit(solution)/shard_map/all_gather | solution.py:300
  9.5 347.7 %all-gather.15.cloned.1.call-start = ((), (), s32[]{:S(2)}) async-start(), calls=%async_computation.9 | async-start | bytes 1216512 | tf_op jit(solution)/shard_map/all_gather | solution.py:302
  10.1 403.0 %all-gather.17.cloned.1.call-start = ((), (), s32[]{:S(2)}) async-start(), calls=%async_computation.10 | async-start | bytes 1216512 | tf_op jit(solution)/shard_map/all_gather | solution.py:305
  10.7 467.7 %all-gather.19.cloned.1.call-start = ((), (), s32[]{:S(2)}) async-start(), calls=%async_computation.11 | async-start | bytes 4866048 | tf_op jit(solution)/shard_map/all_gather | solution.py:309
  11.3 532.1 %all-gather.21.cloned.1.call-start = ((), (), s32[]{:S(2)}) async-start(), calls=%async_computation.12 | async-start | bytes 4866048 | tf_op jit(solution)/shard_map/all_gather | solution.py:311
  12.0 819.7 %all-gather.23.cloned.1.call-start = ((), (), s32[]{:S(2)}) async-start(), calls=%async_computation.13 | async-start | bytes 14155776 | tf_op jit(solution)/shard_map/all_gather | solution.py:362
  63.9 181.4 %copy-start.55 = (f32[768]{0:T(1024)}, f32[768]{0:T(1024)S(1)}, u32[]{:S(2)}) copy-start(f32[768]{0:T(1024)S(1)} %convert_element_type.270) | copy-start | bytes 9220
  204.6 208.5 %copy-start.2 = (bf16[1,512,768]{2,1,0:T(8,128)(2,1)}, bf16[1,512,768]{2,1,0:T(8,128)(2,1)S(1)}, u32[]{:S(2)}) copy-start(bf16[1,512,768]{2,1,0:T(8,128)(2,1)S(1)} %copy.129) | copy-start | bytes 2359300
  249.8 185.2 %copy-start.4 = (bf16[512,768]{0,1:T(8,128)(2,1)}, bf16[512,768]{0,1:T(8,128)(2,1)S(1)}, u32[]{:S(2)}) copy-start(bf16[512,768]{0,1:T(8,128)(2,1)S(1)} %copy.107) | copy-start | bytes 2359300
  252.2 49.2 %copy-start.54 = (f32[768]{0:T(1024)S(1)}, f32[768]{0:T(1024)}, u32[]{:S(2)}) copy-start(f32[768]{0:T(1024)} %convert_element_type.272) | copy-start | bytes 9220
  441.1 45.3 %copy-start.10 = (f32[512,768]{1,0:T(8,128)S(1)}, f32[512,768]{1,0:T(8,128)}, u32[]{:S(2)}) copy-start(f32[512,768]{1,0:T(8,128)} %copy-done.9) | copy-start | bytes 4718596
  441.1 45.3 %copy-start.51 = (f32[3072]{0:T(1024)S(1)}, f32[3072]{0:T(1024)}, u32[]{:S(2)}) copy-start(f32[3072]{0:T(1024)} %convert_element_type.283) | copy-start | bytes 36868
  486.5 56.9 %copy-start.52 = (f32[768]{0:T(1024)S(1)}, f32[768]{0:T(1024)}, u32[]{:S(2)}) copy-start(f32[768]{0:T(1024)} %convert_element_type.285) | copy-start | bytes 9220
  626.0 27.3 %copy-start.14 = (bf16[12,64,512]{2,1,0:T(8,128)(2,1)}, bf16[12,64,512]{2,1,0:T(8,128)(2,1)S(1)}, u32[]{:S(2)}) copy-start(bf16[12,64,512]{2,1,0:T(8,128)(2,1)S(1)} %get-tuple-element.171) | copy-start | bytes 2359300
  656.0 279.3 %reduce-scatter.13.cloned.1.call-start = ((), (), s32[]{:S(2)}) async-start(), calls=%async_computation.17 | async-start | bytes 2433024 | tf_op jit(solution)/shard_map/reduce_scatter | solution.py:349
  660.4 379.4 %reduce-scatter.11.cloned.1.call-start = ((), (), s32[]{:S(2)}) async-start(), calls=%async_computation.16 | async-start | bytes 2433024 | tf_op jit(solution)/shard_map/reduce_scatter | solution.py:347
  664.2 480.2 %reduce-scatter.7.cloned.1.call-start = ((), (), s32[]{:S(2)}) async-start(), calls=%async_computation.14 | async-start | bytes 2433024 | tf_op jit(solution)/shard_map/reduce_scatter | solution.py:344
  668.5 580.2 %reduce-scatter.9.cloned.1.call-start = ((), (), s32[]{:S(2)}) async-start(), calls=%async_computation.15 | async-start | bytes 2433024 | tf_op jit(solution)/shard_map/reduce_scatter | solution.py:346
  672.7 717.7 %reduce-scatter.15.cloned.1.call-start = ((), (), s32[]{:S(2)}) async-start(), calls=%async_computation.18 | async-start | bytes 9732096 | tf_op jit(solution)/shard_map/reduce_scatter | solution.py:353
  684.8 847.3 %reduce-scatter.17.cloned.1.call-start = ((), (), s32[]{:S(2)}) async-start(), calls=%async_computation.19 | async-start | bytes 9732096 | tf_op jit(solution)/shard_map/reduce_scatter | solution.py:355
  696.4 47.9 %copy-start.43 = (bf16[1,512,768]{2,1,0:T(8,128)(2,1)S(1)}, bf16[1,512,768]{2,1,0:T(8,128)(2,1)}, u32[]{:S(2)}) copy-start(bf16[1,512,768]{2,1,0:T(8,128)(2,1)} %get-tuple-element.131) | copy-start | bytes 2359300
  696.4 47.9 %copy-start.44 = (bf16[1,512,768]{2,1,0:T(8,128)(2,1)S(1)}, bf16[1,512,768]{2,1,0:T(8,128)(2,1)}, u32[]{:S(2)}) copy-start(bf16[1,512,768]{2,1,0:T(8,128)(2,1)} %get-tuple-element.132) | copy-start | bytes 2359300
  (78 other events, 423.3 us)
Sparse Core Ops, SparseCore 0:
  10.3 179.7 all-gather.8
  193.1 52.2 all-gather.10
  248.4 52.9 all-gather.12
  304.2 52.9 all-gather.14
  360.1 52.9 all-gather.16
  415.9 62.4 all-gather.18
  481.4 61.9 all-gather.20
  656.1 175.4 all-gather.22
  837.5 97.7 reduce-scatter.12
  941.1 98.6 reduce-scatter.10
  1045.6 98.6 reduce-scatter.6
  1150.1 98.5 reduce-scatter.8
  1255.2 135.1 reduce-scatter.14
  1396.7 135.3 reduce-scatter.16
where the time goes:
time: 1540 us
  waiting for transfers between devices  1140 us (74%)
  matrix products  189 us (12%)
  blocking collectives  88.8 us (6%)
  other arithmetic  53.3 us (3%)
  local copies, waits for them, and re-layouts  49.2 us (3%)
  between operations  15.5 us (1%)
    reduce_scatter x1, waiting for transfers between devices, per_device(): lax.psum_scatter(grad_totals[11], ('dp', 'fsdp'), scatter_dimension=0, ti...  142 us
    reduce_scatter x1, waiting for transfers between devices, per_device(): lax.psum_scatter(grad_totals[9], ('dp', 'fsdp'), scatter_dimension=0, til...  142 us
    all_gather x1, waiting for transfers between devices, per_device(): lax.all_gather(tokens, 'fsdp', axis=0, tiled=True)  123 us
    reduce_scatter x1, waiting for transfers between devices, per_device(): lax.psum_scatter(grad_totals[0], ('dp', 'fsdp'), scatter_dimension=0, til...  105 us
    reduce_scatter x1, waiting for transfers between devices, per_device(): lax.psum_scatter(grad_totals[3], ('dp', 'fsdp'), scatter_dimension=0, til...  104 us
    reduce_scatter x1, waiting for transfers between devices, per_device(): lax.psum_scatter(grad_totals[2], ('dp', 'fsdp'), scatter_dimension=0, til...  104 us
    reduce_scatter x1, waiting for transfers between devices, per_device(): lax.psum_scatter(grad_totals[5], ('dp', 'fsdp'), scatter_dimension=0, til...  90.3 us
    unnamed x2, blocking collectives  88.8 us
  transfers between devices with their start and end apart: 14, of which 14 were waited for; matrix products, arithmetic and copies ran while one was open for 11% of the time, Pallas kernels for 0%

commit v1 on v0

v1 whole, which is shorter than its diff:
```python
import jax
import jax.numpy as jnp
from jax import lax
from jax.sharding import PartitionSpec as P

HD = 64
LINE = 4
BOTH = ("dp", "fsdp")
bf16 = jnp.bfloat16
f32 = jnp.float32

norm_eps = 1e-12
half_root = 0.7071067811865476
slope_scale = 0.3989422804014327


class Grid:
    def __init__(self, mesh):
        self.dp = mesh.shape["dp"]
        self.fsdp = mesh.shape["fsdp"]
        self.total = self.dp * self.fsdp
        nx = self.fsdp // LINE
        ny = self.dp // 2
        self.size = {"y": ny, "core": 2, "z": LINE, "x": nx}
        self.stride = {"x": 1, "z": nx, "core": self.fsdp, "y": 2 * self.fsdp}

    def place(self, axis):
        me = lax.axis_index("dp") * self.fsdp + lax.axis_index("fsdp")
        return (me // self.stride[axis]) % self.size[axis]

    def swap(self, array, axis, step):
        mask = self.stride[axis] * step
        return lax.ppermute(array, BOTH, [(i, i ^ mask) for i in range(self.total)])


AXES = ("y", "core", "z", "x")


def gather(grid, shard, order):
    held = shard
    have = []
    for axis in order:
        size = grid.size[axis]
        me = grid.place(axis)
        parts = [held] + [grid.swap(held, axis, step) for step in range(1, size)]
        bit = 1
        while bit < size:
            flip = (me & bit) != 0
            parts = [jnp.where(flip, parts[j ^ bit], parts[j]) for j in range(size)]
            bit *= 2
        at = sum(AXES.index(other) < AXES.index(axis) for other in have)
        held = jnp.stack(parts, axis=at)
        have.append(axis)
    return held.reshape((-1,) + shard.shape[1:])


def scatter_sum(grid, terms, order):
    rows = terms.shape[0] // grid.total
    held = terms.reshape(tuple(grid.size[axis] for axis in AXES) + (rows,) + terms.shape[1:])
    have = list(AXES)
    for axis in order:
        size = grid.size[axis]
        me = grid.place(axis)
        at = have.index(axis)
        kept = lax.dynamic_index_in_dim(held, me, at, keepdims=False)
        got = [
            grid.swap(
                lax.dynamic_index_in_dim(held, me ^ step, at, keepdims=False).astype(bf16),
                axis,
                step,
            )
            for step in range(1, size)
        ]
        held = kept
        for one in got:
            held = held + one.astype(f32)
        have.remove(axis)
    return held


def standardize(values):
    centre = values - jnp.mean(values, axis=-1, keepdims=True)
    spread = lax.rsqrt(jnp.mean(centre * centre, axis=-1, keepdims=True) + norm_eps)
    return (centre * spread, spread)


def norm_back(d_normed, normed, spread):
    return spread * (
        d_normed
        - jnp.mean(d_normed, axis=-1, keepdims=True)
        - normed * jnp.mean(d_normed * normed, axis=-1, keepdims=True)
    )


def gelu_value(values):
    return 0.5 * values * (1.0 + lax.erf(values * half_root))


def gelu_slope(values):
    return (
        0.5 * (1.0 + lax.erf(values * half_root))
        + values * jnp.exp(-0.5 * values * values) * slope_scale
    )


def matmul(left, right):
    return jnp.dot(left, right, preferred_element_type=f32)


def left_times(left, right):
    return jnp.einsum("ti,to->io", left, right, preferred_element_type=f32)


def right_times(grads, weight):
    return jnp.einsum("to,io->ti", grads, weight, preferred_element_type=f32)


def pieces_out(array, count):
    slots, rows, width = array.shape
    return array.reshape(slots, count, rows // count, width).transpose(1, 0, 2, 3)


def reorder(array, source):
    count = lax.axis_size("fsdp")
    slots, rows, width = array.shape
    spread = lax.all_to_all(pieces_out(array, count), "fsdp", 0, 0, tiled=True)
    spread = spread.reshape(count * slots, rows // count, width)
    spread = jnp.take(spread, source, axis=0, mode="clip").reshape(count, slots, rows // count, width)
    joined = lax.all_to_all(spread, "fsdp", 0, 0, tiled=True)
    return joined.transpose(1, 0, 2, 3).reshape(slots, rows, width)


def per_device(grid, *args):
    (
        tokens,
        cotangent,
        lengths,
        deal,
        w_query,
        b_query,
        w_key,
        w_value,
        b_value,
        w_out,
        b_out,
        gain_one,
        shift_one,
        w_in,
        b_in,
        w_down,
        b_down,
        gain_two,
        shift_two,
    ) = args
    slots, rows, width = tokens.shape
    hidden_width = w_in.shape[1]
    position = lax.axis_index("fsdp")
    deal_row = deal[0]
    my_lengths = lax.dynamic_slice_in_dim(lengths[0], position * slots, slots)
    spots = jnp.arange(deal_row.shape[0], dtype=jnp.int32)
    inverse = jnp.sum(
        jnp.where(deal_row[None, :] == spots[:, None], spots[None, :], 0), axis=1
    )

    own = jnp.concatenate([w_query, w_key, w_value], axis=1)
    third = own.shape[1] // 3
    qkv = jnp.concatenate(
        [
            gather(grid, own[:, :third], ("z", "x", "y", "core")),
            gather(grid, own[:, third : 2 * third], ("x", "y", "z", "core")),
            gather(grid, own[:, 2 * third :], ("y", "z", "x", "core")),
        ],
        axis=1,
    )
    singles = (b_query, b_value, b_out, gain_one, shift_one, b_in, b_down, gain_two, shift_two)
    small = jnp.concatenate(singles)
    small = lax.all_to_all(
        jnp.broadcast_to(small[None, :], (grid.total, small.shape[0])), BOTH, 0, 0, tiled=True
    )
    vectors = []
    at = 0
    for one in singles:
        vectors.append(small[:, at : at + one.shape[0]].reshape(-1).astype(f32))
        at += one.shape[0]
    bq, bv, bo, g1, s1, bi, bd, g2, s2 = vectors

    wo = gather(grid, w_out, ("z", "x", "y", "core"))
    wi = gather(grid, w_in, ("z", "x", "y", "core"))
    wd = gather(grid, w_down, ("z", "x", "y", "core"))

    upstream = reorder(cotangent, deal_row)

    total_rows = slots * rows
    inputs = tokens.reshape(total_rows, width)
    valid = jnp.arange(rows)[None, :] < my_lengths[:, None]
    valid_row = valid.reshape(total_rows)[:, None]

    no_bias = jnp.zeros_like(bq)
    fused = (matmul(inputs, qkv) + jnp.concatenate([bq, no_bias, bv])).astype(bf16)
    query, key_rows, value_rows = (
        fused[:, i * width : (i + 1) * width].reshape(slots, rows, -1, HD) for i in range(3)
    )

    def scores_of():
        raw = jnp.einsum("sqhd,skhd->shqk", query, key_rows, preferred_element_type=f32)
        return jnp.where(valid[:, None, None, :], raw * HD ** (-0.5), -1e30)

    scores = scores_of()
    top = jnp.max(scores, axis=-1, keepdims=True)
    total = jnp.log(jnp.sum(jnp.exp(scores - top), axis=-1, keepdims=True)) + top
    probs = jnp.exp(scores - total).astype(bf16)
    context = (
        jnp.einsum("shqk,skhd->sqhd", probs, value_rows, preferred_element_type=f32)
        .reshape(total_rows, width)
        .astype(bf16)
    )
    middle_norm, middle_spread = standardize(inputs.astype(f32) + matmul(context, wo) + bo)
    middle = middle_norm * g1 + s1
    middle_low = middle.astype(bf16)
    hidden = matmul(middle_low, wi) + bi
    active = gelu_value(hidden).astype(bf16)
    final_norm, final_spread = standardize(middle + matmul(active, wd) + bd)
    output = jnp.where(valid_row, final_norm * g2 + s2, 0.0).astype(bf16)
    layer_out = reorder(output.reshape(slots, rows, width), inverse)

    d_result = jnp.where(valid_row, upstream.reshape(total_rows, width).astype(f32), 0.0)
    grad_g2 = jnp.sum(d_result * final_norm, axis=0)
    grad_s2 = jnp.sum(d_result, axis=0)
    d_final = norm_back(d_result * g2, final_norm, final_spread)
    d_branch = d_final.astype(bf16)
    grad_bd = jnp.sum(d_branch.astype(f32), axis=0)
    shard_wd = scatter_sum(grid, left_times(active, d_branch), ("core", "y", "x", "z"))
    d_hidden = (right_times(d_branch, wd) * gelu_slope(hidden)).astype(bf16)
    grad_bi = jnp.sum(d_hidden.astype(f32), axis=0)
    shard_wi = scatter_sum(grid, left_times(middle_low, d_hidden), ("core", "y", "x", "z"))
    d_middle = d_final + right_times(d_hidden, wi)
    grad_g1 = jnp.sum(d_middle * middle_norm, axis=0)
    grad_s1 = jnp.sum(d_middle, axis=0)
    d_sum = norm_back(d_middle * g1, middle_norm, middle_spread)
    d_attended = d_sum.astype(bf16)
    grad_bo = jnp.sum(d_attended.astype(f32), axis=0)
    shard_wo = scatter_sum(grid, left_times(context, d_attended), ("core", "y", "x", "z"))
    d_context = right_times(d_attended, wo).astype(bf16).reshape(slots, rows, -1, HD)
    probs = jnp.exp(scores_of() - total)
    d_probs = jnp.einsum("sqhd,skhd->shqk", d_context, value_rows, preferred_element_type=f32)
    d_value = jnp.einsum(
        "shqk,sqhd->skhd", probs.astype(bf16), d_context, preferred_element_type=f32
    )
    d_scores = (probs * (d_probs - jnp.sum(probs * d_probs, axis=-1, keepdims=True))).astype(bf16)
    scale = HD ** (-0.5)
    d_query = (
        jnp.einsum("shqk,skhd->sqhd", d_scores, key_rows, preferred_element_type=f32) * scale
    )
    d_key = jnp.einsum("shqk,sqhd->skhd", d_scores, query, preferred_element_type=f32) * scale
    d_fused = jnp.concatenate(
        [one.reshape(total_rows, width).astype(bf16) for one in (d_query, d_key, d_value)], axis=1
    )
    grad_fused = jnp.sum(d_fused.astype(f32), axis=0)
    shard_qkv = scatter_sum(grid, left_times(inputs, d_fused), ("core", "y", "x", "z"))
    input_grad = (d_sum + right_times(d_fused, qkv)).astype(bf16).reshape(slots, rows, width)

    grads = (
        grad_fused[:width],
        grad_fused[2 * width :],
        grad_bo,
        grad_g1,
        grad_s1,
        grad_bi,
        grad_bd,
        grad_g2,
        grad_s2,
    )
    small = jnp.concatenate([one.reshape(grid.total, -1) for one in grads], axis=1)
    small = jnp.sum(lax.all_to_all(small, BOTH, 0, 0, tiled=True), axis=0)
    parts = []
    at = 0
    for one in singles:
        parts.append(small[at : at + one.shape[0]])
        at += one.shape[0]
    pbq, pbv, pbo, pg1, ps1, pbi, pbd, pg2, ps2 = parts
    return (
        layer_out,
        input_grad,
        shard_qkv[:, :width],
        pbq,
        shard_qkv[:, width : 2 * width],
        shard_qkv[:, 2 * width :],
        pbv,
        shard_wo,
        pbo,
        pg1,
        ps1,
        shard_wi,
        pbi,
        shard_wd,
        pbd,
        pg2,
        ps2,
    )


def solution(mesh):
    grid = Grid(mesh)
    rows3 = P(BOTH, None, None)
    rows2 = P(BOTH, None)
    rows1 = P(BOTH)
    table = P("dp", None)
    kinds = (2, 1, 2, 2, 1, 2, 1, 1, 1, 2, 1, 2, 1, 1, 1)
    placed = tuple(rows2 if kind == 2 else rows1 for kind in kinds)

    def step(*args):
        return per_device(grid, *args)

    return jax.shard_map(
        step,
        mesh=mesh,
        in_specs=(rows3, rows3, table, table) + placed,
        out_specs=(rows3, rows3) + placed,
        check_vma=False,
    )
```

time: 1540 us -> 578 us (0.38)
  waiting for transfers between devices: 1140 us -> 173 us
  starting transfers between devices: 0.77 us -> 94.9 us
  blocking collectives: 88.8 us -> 0 us
  matrix products: 189 us -> 140 us
  other arithmetic: 53.3 us -> 85.3 us
  local copies, waits for them, and re-layouts: 49.2 us -> 72.8 us
    reduce_scatter x6 -> x0, waiting for transfers between devices: 687 us -> none  [the longest x1 142 us: per_device(): lax.psum_scatter(grad_totals[11], ('dp', 'fsdp'), scatter_dimension=0, ti...]
    all_gather x8 -> x0, waiting for transfers between devices: 451 us -> none  [the longest x1 123 us: per_device(): lax.all_gather(tokens, 'fsdp', axis=0, tiled=True)]
    ppermute x0 -> x60, waiting for transfers between devices: none -> 156 us  [swap(): return lax.ppermute(array, BOTH, [(i, i ^ mask) for i in range(self.total)])]
    unnamed x2 -> x0, blocking collectives: 88.8 us -> none
    ppermute x0 -> x60, starting transfers between devices: none -> 69.6 us  [swap(): return lax.ppermute(array, BOTH, [(i, i ^ mask) for i in range(self.total)])]
    dot_general x50 -> x18, matrix products: 189 us -> 140 us  [the longest x4 24.6 us: right_times(): return jnp.einsum('to,io->ti', grads, weight, preferred_element_type=f32)]
    all_to_all x0 -> x6, starting transfers between devices: none -> 25.3 us  [the longest x2 10.1 us: reorder(): joined = lax.all_to_all(spread, 'fsdp', 0, 0, tiled=True)]
    add x12 -> x17, other arithmetic: 0.06 us -> 17.9 us  [the longest x16 17.9 us: scatter_sum(): held = held + one.astype(f32)]
  transfers between devices with their start and end apart: 14 -> 66, of which waited for: 14 -> 21; matrix products, arithmetic and copies ran while one was open for 11% -> 25% of each run, Pallas kernels for 0% -> 0%
where the time goes in v1:
time: 578 us; the launch traced here: 569 us
  waiting for transfers between devices  173 us (30%)
  matrix products  140 us (24%)
  starting transfers between devices  94.9 us (16%)
  other arithmetic  85.3 us (15%)
  local copies, waits for them, and re-layouts  72.8 us (13%)
    ppermute x60, waiting for transfers between devices, swap(): return lax.ppermute(array, BOTH, [(i, i ^ mask) for i in range(self.total)])  156 us
    ppermute x60, starting transfers between devices, swap(): return lax.ppermute(array, BOTH, [(i, i ^ mask) for i in range(self.total)])  69.6 us
    dot_general x4, matrix products, right_times(): return jnp.einsum('to,io->ti', grads, weight, preferred_element_type=f32)  24.6 us
    dot_general x4, matrix products, left_times(): return jnp.einsum('ti,to->io', left, right, preferred_element_type=f32)  24.1 us
    convert_element_type x1, other arithmetic, per_device(): (probs * (d_probs - jnp.sum(probs * d_probs, axis=-1, keepdims=True))).as...  22.1 us
    dot_general x4, matrix products, matmul(): return jnp.dot(left, right, preferred_element_type=f32)  21.5 us
    another operation x46, other arithmetic, gather(): held = jnp.stack(parts, axis=at)  19.8 us
    dot_general x1, matrix products, per_device(): jnp.einsum('sqhd,skhd->shqk', d_context, value_rows, preferred_element_ty...  19.7 us
  transfers between devices with their start and end apart: 66, of which 21 were waited for; matrix products, arithmetic and copies ran while one was open for 25% of the time, Pallas kernels for 0%

profile of v1, /device:TPU:0, one launch (start us, length us, event | category | flops | bytes accessed | tf_op | source)
XLA Modules:
  0.0 569.0 jit_solution(17518119879794219521)
XLA Ops:
  9.4 6.1 %concatenate.16 = bf16[288]{0:T(512)(128)(2,1)S(1)} concatenate(bf16[24]{0:T(256)(128)(2,1)} %param.24, bf16[24]{0:T(256)(128)(2,1)} %param.27, bf16[24]{0:T(256)(128)(2,1)} %param.29, bf16[24]{0:T(256)(128)(2,1)} %param.30, bf16[24]{0:T(256)(128)(2,1)} %param.31, bf16[96]{0:T(256)(128)(2,1)} %param.33, bf16[24]{0:T(256)(128)(2,1)} %param.35, bf16[24]{0:T(256)(128)(2,1)} %param.36, ...), dimensions={0} | concatenate | bytes 1152 | tf_op jit(solution)/shard_map/concatenate | solution.py:176
  43.0 36.3 %collective-permute-done.19 = bf16[24,768]{1,0:T(8,128)(2,1)S(1)} collective-permute-done((bf16[24,768]{1,0:T(8,128)(2,1)S(1)}, bf16[24,768]{1,0:T(8,128)(2,1)S(1)}, u32[]{:S(2)}, u32[]{:S(2)}) %collective-permute-start.19) | collective-permute-done | bytes 36896 | tf_op jit(solution)/shard_map/ppermute | solution.py:33
  119.0 7.5 %collective-permute-done.4 = bf16[4,2,24,768]{3,2,1,0:T(8,128)(2,1)S(1)} collective-permute-done((bf16[4,2,24,768]{3,2,1,0:T(8,128)(2,1)S(1)}, bf16[4,2,24,768]{3,2,1,0:T(8,128)(2,1)S(1)}, u32[]{:S(2)}, u32[]{:S(2)}) %collective-permute-start.4) | collective-permute-done | bytes 294944 | tf_op jit(solution)/shard_map/ppermute | solution.py:33
  133.2 7.1 %collective-permute-done.33 = bf16[4,96,768]{2,1,0:T(8,128)(2,1)S(1)} collective-permute-done((bf16[4,96,768]{2,1,0:T(8,128)(2,1)S(1)}, bf16[4,96,768]{2,1,0:T(8,128)(2,1)S(1)}, u32[]{:S(2)}, u32[]{:S(2)}) %collective-permute-start.33) | collective-permute-done | bytes 589856 | tf_op jit(solution)/shard_map/ppermute | solution.py:33
  163.4 11.4 %fusion = (f32[2,12,512]{2,1,0:T(8,128)S(1)}, f32[2,12,512,512]{2,3,1,0:T(8,128)}) fusion(pred[2,512]{1,0:T(4,128)(4,1)S(1)} %iota_compare_fusion.1, bf16[2,512,12,64]{1,0,3,2:T(2,128)(2,1)S(1)} %reshape.369, bf16[2,512,12,64]{1,0,3,2:T(2,128)(2,1)S(1)} %reshape.368), kind=kOutput, calls=%fused_computation.7 | convolution fusion | flops 824168448 | bytes 28361728 | tf_op jit(solution)/shard_map/sqhd,skhd->shqk/dot_general | solution.py:205
  174.8 11.2 %exponential_reduce_fusion = f32[2,12,512]{2,1,0:T(8,128)S(1)} fusion(f32[2,12,512,512]{2,3,1,0:T(8,128)} %get-tuple-element.127, f32[2,12,512]{2,1,0:T(8,128)S(1)} %get-tuple-element.126, pred[2,512]{1,0:T(4,128)(4,1)S(1)} %iota_compare_fusion.1), kind=kLoop, calls=%fused_computation.5 | loop fusion | flops 25153536 | bytes 25265152 | tf_op jit(solution)/shard_map/reduce_sum | solution.py:210
  190.1 11.2 %fusion.16 = bf16[2,512,12,64]{1,3,2,0:T(8,128)(2,1)S(1)} fusion(bf16[2,512,12,64]{1,0,3,2:T(2,128)(2,1)S(1)} %copy-done.17, f32[2,12,512,512]{2,3,1,0:T(8,128)} %get-tuple-element.127, f32[2,12,512]{2,1,0:T(8,128)S(1)} %log_add_fusion, pred[2,512]{1,0:T(4,128)(4,1)S(1)} %iota_compare_fusion.1), kind=kOutput, calls=%fused_computation.79 | convolution fusion | flops 831258624 | bytes 28361728 | tf_op jit(solution)/shard_map/shqk,skhd->sqhd/dot_general | solution.py:213
  223.4 9.3 %multiply_convert_fusion.1 = (bf16[1024,3072]{1,0:T(8,128)(2,1)S(1)}, f32[1024,3072]{1,0:T(8,128)}) fusion(f32[3072]{0:T(1024)S(1)} %reshape.398, bf16[768,3072]{1,0:T(8,128)(2,1)S(1)} %bitcast.376, f32[1024,768]{1,0:T(8,128)S(1)} %get-tuple-element.129, f32[768]{0:T(1024)S(1)} %reshape.397, f32[768]{0:T(1024)S(1)} %reshape.396, ...), kind=kOutput, calls=%fused_computation.17 | convolution fusion | flops 4854644736 | bytes 26765312 | tf_op jit(solution)/shard_map/dot_general | solution.py:107
  237.2 5.5 fusion.82
  244.8 13.0 %all-to-all-done.4 = bf16[8,2,64,768]{3,2,1,0:T(8,128)(2,1)} async-done(((bf16[8,2,64,768]{3,2,1,0:T(8,128)(2,1)}), bf16[8,2,64,768]{3,2,1,0:T(8,128)(2,1)}, u32[]{:S(2)}, u32[]{:S(2)}) %all-to-all-start.4) | async-done | bytes 1572896 | tf_op jit(solution)/shard_map/all_to_all | solution.py:129
  268.2 12.0 %convert_reduce_fusion = (f32[3072]{0:T(1024)S(1)}, bf16[1024,3072]{1,0:T(8,128)(2,1)S(1)}) fusion(f32[1024,3072]{1,0:T(8,128)} %get-tuple-element.131, f32[3072]{0:T(1024)S(1)} %reshape.398, bf16[3072,768]{1,0:T(8,128)(2,1)S(1)} %bitcast.383, f32[1024,768]{1,0:T(8,128)S(1)} %get-tuple-element.26), kind=kOutput, calls=%fused_computation.16 | convolution fusion | flops 4873516032 | bytes 26763264 | tf_op jit(solution)/shard_map/to,io->ti/dot_general | solution.py:115
  280.2 5.9 %multiply_reduce_fusion.2 = (f32[768]{0:T(1024)S(1)}, f32[1024]{0:T(1024)S(1)}, f32[1024]{0:T(1024)S(1)}, f32[768]{0:T(1024)S(1)}, f32[1024,768]{1,0:T(8,128)S(1)}) fusion(f32[1024,768]{1,0:T(8,128)S(1)} %get-tuple-element.129, f32[1024]{0:T(1024)S(1)} %add_rsqrt_fusion.1, f32[1024]{0:T(1024)S(1)} %broadcast_multiply_fusion.4, f32[768]{0:T(1024)S(1)} %reshape.396, ...), kind=kOutput, calls=%fused_computation.35 | convolution fusion | flops 4839698432 | bytes 20472832 | tf_op jit(solution)/shard_map/to,io->ti/dot_general | solution.py:115
  286.1 8.4 %fusion.73 = f32[768,3072]{1,0:T(8,128)} fusion(bf16[1024,3072]{1,0:T(8,128)(2,1)S(1)} %get-tuple-element.138, f32[1024,768]{1,0:T(8,128)S(1)} %get-tuple-element.129, f32[768]{0:T(1024)S(1)} %reshape.397, f32[768]{0:T(1024)S(1)} %reshape.396, f32[1024]{0:T(1024)S(1)} %add_rsqrt_fusion.1, f32[1024]{0:T(1024)S(1)} %broadcast_multiply_fusion.4), kind=kOutput, calls=%fused_computation.298 | convolution fusion | flops 4835770368 | bytes 18888704 | tf_op jit(solution)/shard_map/ti,to->io/dot_general | solution.py:111
  294.5 10.2 %fusion.66 = f32[3072,768]{1,0:T(8,128)} fusion(bf16[1024,3072]{1,0:T(8,128)(2,1)} %copy-done.55, f32[1024,768]{1,0:T(8,128)S(1)} %get-tuple-element.26), kind=kOutput, calls=%fused_computation.291 | convolution fusion | flops 4832624640 | bytes 18874368 | tf_op jit(solution)/shard_map/ti,to->io/dot_general | solution.py:111
  310.9 12.6 %fusion.17 = bf16[2,512,12,64]{1,3,2,0:T(8,128)(2,1)} fusion(bf16[2,512,12,64]{1,0,3,2:T(2,128)(2,1)S(1)} %reshape.379, f32[2,12,512,512]{2,3,1,0:T(8,128)} %get-tuple-element.127, f32[2,12,512]{2,1,0:T(8,128)S(1)} %log_add_fusion, pred[2,512]{1,0:T(4,128)(4,1)S(1)} %iota_compare_fusion.1), kind=kOutput, calls=%fused_computation.80 | convolution fusion | flops 831258624 | bytes 28361728 | tf_op jit(solution)/shard_map/shqk,sqhd->skhd/dot_general | solution.py:246
  323.5 19.7 %multiply_reduce_fusion = (f32[2,12,512]{2,1,0:T(8,128)S(1)}, f32[2,12,512,512]{2,3,1,0:T(8,128)}) fusion(f32[2,12,512,512]{2,3,1,0:T(8,128)} %get-tuple-element.127, f32[2,12,512]{2,1,0:T(8,128)S(1)} %log_add_fusion, pred[2,512]{1,0:T(4,128)(4,1)S(1)} %iota_compare_fusion.1, bf16[2,512,12,64]{1,0,3,2:T(2,128)(2,1)S(1)} %copy-done.18, ...), kind=kOutput, calls=%fused_computation.3 | convolution fusion | flops 836751360 | bytes 53576704 | tf_op jit(solution)/shard_map/sqhd,skhd->shqk/dot_general | solution.py:245
  343.1 22.1 %multiply_convert_fusion = bf16[2,12,512,512]{2,3,1,0:T(8,128)(2,1)} fusion(f32[2,12,512,512]{2,3,1,0:T(8,128)} %get-tuple-element.136, f32[2,12,512,512]{2,3,1,0:T(8,128)} %get-tuple-element.127, f32[2,12,512]{2,1,0:T(8,128)S(1)} %get-tuple-element.135, f32[2,12,512]{2,1,0:T(8,128)S(1)} %log_add_fusion, pred[2,512]{1,0:T(4,128)(4,1)S(1)} %iota_compare_fusion.1), kind=kLoop, calls=%fused_computation.2 | loop fusion | flops 37748736 | bytes 63013888 | tf_op jit(solution)/shard_map/convert_element_type | solution.py:249
  365.2 8.6 %fusion.19 = bf16[2,512,12,64]{1,3,2,0:T(8,128)(2,1)S(1)} fusion(bf16[2,12,512,512]{2,3,1,0:T(8,128)(2,1)} %multiply_convert_fusion, bf16[2,512,12,64]{1,0,3,2:T(2,128)(2,1)S(1)} %copy-done.9), kind=kOutput, calls=%fused_computation.82 | convolution fusion | flops 806879232 | bytes 15728640 | tf_op jit(solution)/shard_map/shqk,sqhd->skhd/dot_general | solution.py:254
  373.9 6.8 %fusion.18 = bf16[2,512,12,64]{1,3,2,0:T(8,128)(2,1)S(1)} fusion(bf16[2,12,512,512]{2,3,1,0:T(8,128)(2,1)} %multiply_convert_fusion, bf16[2,512,12,64]{1,0,3,2:T(2,128)(2,1)S(1)} %copy-done.5), kind=kOutput, calls=%fused_computation.81 | convolution fusion | flops 806879232 | bytes 15728640 | tf_op jit(solution)/shard_map/shqk,skhd->sqhd/dot_general | solution.py:252
  431.5 13.1 %collective-permute-done.44 = bf16[4,24,768]{2,1,0:T(8,128)(2,1)S(1)} collective-permute-done((bf16[4,24,768]{2,1,0:T(8,128)(2,1)S(1)}, bf16[4,24,768]{2,1,0:T(8,128)(2,1)S(1)}, u32[]{:S(2)}, u32[]{:S(2)}) %collective-permute-start.44) | collective-permute-done | bytes 147488 | tf_op jit(solution)/shard_map/ppermute | solution.py:33
  457.8 13.7 %collective-permute-done.37 = bf16[4,2,24,2304]{3,2,0,1:T(8,128)(2,1)S(1)} collective-permute-done((bf16[4,2,24,2304]{3,2,0,1:T(8,128)(2,1)S(1)}, bf16[4,2,24,2304]{3,2,0,1:T(8,128)(2,1)S(1)}, u32[]{:S(2)}, u32[]{:S(2)}) %collective-permute-start.37) | collective-permute-done | bytes 884768 | tf_op jit(solution)/shard_map/ppermute | solution.py:33
  491.0 5.4 all-to-all-start.2
  497.5 25.5 %collective-permute-done.55 = bf16[4,2,96,768]{3,2,0,1:T(8,128)(2,1)} collective-permute-done((bf16[4,2,96,768]{3,2,0,1:T(8,128)(2,1)}, bf16[4,2,96,768]{3,2,0,1:T(8,128)(2,1)}, u32[]{:S(2)}, u32[]{:S(2)}) %collective-permute-start.55) | collective-permute-done | bytes 1179680 | tf_op jit(solution)/shard_map/ppermute | solution.py:33
  530.3 11.7 %collective-permute-done.56 = bf16[4,96,768]{2,1,0:T(8,128)(2,1)S(1)} collective-permute-done((bf16[4,96,768]{2,1,0:T(8,128)(2,1)S(1)}, bf16[4,96,768]{2,1,0:T(8,128)(2,1)S(1)}, u32[]{:S(2)}, u32[]{:S(2)}) %collective-permute-start.56) | collective-permute-done | bytes 589856 | tf_op jit(solution)/shard_map/ppermute | solution.py:33
  (427 shorter events, 272.3 us)
Async XLA Ops:
  0.7 37.8 %collective-permute-start.1 = (bf16[24,768]{1,0:T(8,128)(2,1)}, bf16[24,768]{1,0:T(8,128)(2,1)S(1)}, u32[]{:S(2)}, u32[]{:S(2)}) collective-permute-start(bf16[24,768]{1,0:T(8,128)(2,1)} %param.23), channel_id=1, source_target_pairs={{0,4},{1,5},{2,6},{3,7},{4,0},{5,1},{6,2},{7,3},{8,12},{9,13},{10,... | collective-permute-start | bytes 110600 | tf_op jit(solution)/shard_map/ppermute | solution.py:33
  4.8 33.8 %collective-permute-start = (bf16[24,768]{1,0:T(8,128)(2,1)}, bf16[24,768]{1,0:T(8,128)(2,1)S(1)}, u32[]{:S(2)}, u32[]{:S(2)}) collective-permute-start(bf16[24,768]{1,0:T(8,128)(2,1)} %param.23), channel_id=1, source_target_pairs={{0,6},{1,7},{2,4},{3,5},{4,2},{5,3},{6,0},{7,1},{8,14},{9,15},{10,... | collective-permute-start | bytes 110600 | tf_op jit(solution)/shard_map/ppermute | solution.py:33
  6.2 35.4 %collective-permute-start.2 = (bf16[24,768]{1,0:T(8,128)(2,1)}, bf16[24,768]{1,0:T(8,128)(2,1)S(1)}, u32[]{:S(2)}, u32[]{:S(2)}) collective-permute-start(bf16[24,768]{1,0:T(8,128)(2,1)} %param.23), channel_id=1, source_target_pairs={{0,2},{1,3},{2,0},{3,1},{4,6},{5,7},{6,4},{7,5},{8,10},{9,11},{10,... | collective-permute-start | bytes 110600 | tf_op jit(solution)/shard_map/ppermute | solution.py:33
  28.0 184.4 %all-to-all-start.3 = ((bf16[8,2,64,768]{3,2,1,0:T(8,128)(2,1)}), bf16[8,2,64,768]{3,2,1,0:T(8,128)(2,1)}, u32[]{:S(2)}, u32[]{:S(2)}) async-start(bf16[8,2,64,768]{3,2,1,0:T(8,128)(2,1)} %copy.323), calls=%async_computation.3 | async-start | bytes 3145728 | tf_op jit(solution)/shard_map/all_to_all | solution.py:126
  34.0 45.3 %collective-permute-start.19 = (bf16[24,768]{1,0:T(8,128)(2,1)S(1)}, bf16[24,768]{1,0:T(8,128)(2,1)S(1)}, u32[]{:S(2)}, u32[]{:S(2)}) collective-permute-start(bf16[24,768]{1,0:T(8,128)(2,1)S(1)} %copy-done.47), channel_id=1, source_target_pairs={{0,4},{1,5},{2,6},{3,7},{4,0},{5,1},{6,2},{7,3},{8,12},{9,13},{10,... | collective-permute-start | bytes 110600 | tf_op jit(solution)/shard_map/ppermute | solution.py:33
  36.9 42.4 %collective-permute-start.18 = (bf16[24,768]{1,0:T(8,128)(2,1)S(1)}, bf16[24,768]{1,0:T(8,128)(2,1)S(1)}, u32[]{:S(2)}, u32[]{:S(2)}) collective-permute-start(bf16[24,768]{1,0:T(8,128)(2,1)S(1)} %copy-done.47), channel_id=1, source_target_pairs={{0,6},{1,7},{2,4},{3,5},{4,2},{5,3},{6,0},{7,1},{8,14},{9,15},{10,... | collective-permute-start | bytes 110600 | tf_op jit(solution)/shard_map/ppermute | solution.py:33
  38.5 42.9 %collective-permute-start.20 = (bf16[24,768]{1,0:T(8,128)(2,1)S(1)}, bf16[24,768]{1,0:T(8,128)(2,1)S(1)}, u32[]{:S(2)}, u32[]{:S(2)}) collective-permute-start(bf16[24,768]{1,0:T(8,128)(2,1)S(1)} %copy-done.47), channel_id=1, source_target_pairs={{0,2},{1,3},{2,0},{3,1},{4,6},{5,7},{6,4},{7,5},{8,10},{9,11},{10,... | collective-permute-start | bytes 110600 | tf_op jit(solution)/shard_map/ppermute | solution.py:33
  38.6 56.5 %collective-permute-start.25 = (bf16[24,3072]{1,0:T(8,128)(2,1)S(1)}, bf16[24,3072]{1,0:T(8,128)(2,1)S(1)}, u32[]{:S(2)}, u32[]{:S(2)}) collective-permute-start(bf16[24,3072]{1,0:T(8,128)(2,1)S(1)} %copy-done.45), channel_id=1, source_target_pairs={{0,4},{1,5},{2,6},{3,7},{4,0},{5,1},{6,2},{7,3},{8,12},{9,13},{10,... | collective-permute-start | bytes 442376 | tf_op jit(solution)/shard_map/ppermute | solution.py:33
  41.6 54.1 %collective-permute-start.24 = (bf16[24,3072]{1,0:T(8,128)(2,1)S(1)}, bf16[24,3072]{1,0:T(8,128)(2,1)S(1)}, u32[]{:S(2)}, u32[]{:S(2)}) collective-permute-start(bf16[24,3072]{1,0:T(8,128)(2,1)S(1)} %copy-done.45), channel_id=1, source_target_pairs={{0,6},{1,7},{2,4},{3,5},{4,2},{5,3},{6,0},{7,1},{8,14},{9,15},{10,... | collective-permute-start | bytes 442376 | tf_op jit(solution)/shard_map/ppermute | solution.py:33
  110.0 30.4 %collective-permute-start.33 = (bf16[4,96,768]{2,1,0:T(8,128)(2,1)S(1)}, bf16[4,96,768]{2,1,0:T(8,128)(2,1)S(1)}, u32[]{:S(2)}, u32[]{:S(2)}) collective-permute-start(bf16[4,96,768]{2,1,0:T(8,128)(2,1)S(1)} %pad_maximum_fusion.18), channel_id=1, source_target_pairs={{0,1},{1,0},{2,3},{3,2},{4,5},{5,4},{6,7},{7,6},{8,9},{9,8},{10,11... | collective-permute-start | bytes 1769480 | tf_op jit(solution)/shard_map/ppermute | solution.py:33
  131.4 69.9 %collective-permute-start.23 = (bf16[2,4,2,24,768]{4,3,1,2,0:T(8,128)(2,1)}, bf16[2,4,2,24,768]{4,3,1,2,0:T(8,128)(2,1)}, u32[]{:S(2)}, u32[]{:S(2)}) collective-permute-start(bf16[2,4,2,24,768]{4,3,1,2,0:T(8,128)(2,1)} %pad_maximum_fusion.16), channel_id=1, source_target_pairs={{0,8},{1,9},{2,10},{3,11},{4,12},{5,13},{6,14},{7,15},{8,0},{9,1},... | collective-permute-start | bytes 1769480 | tf_op jit(solution)/shard_map/ppermute | solution.py:33
  140.4 45.7 %collective-permute-start.28 = (bf16[4,2,24,3072]{3,2,1,0:T(8,128)(2,1)}, bf16[4,2,24,3072]{3,2,1,0:T(8,128)(2,1)}, u32[]{:S(2)}, u32[]{:S(2)}) collective-permute-start(bf16[4,2,24,3072]{3,2,1,0:T(8,128)(2,1)} %pad_maximum_fusion.11), channel_id=1, source_target_pairs={{0,16},{1,17},{2,18},{3,19},{4,20},{5,21},{6,22},{7,23},{8,24},{9,... | collective-permute-start | bytes 3538952 | tf_op jit(solution)/shard_map/ppermute | solution.py:33
  143.3 63.9 %collective-permute-start.34 = (bf16[4,2,96,768]{3,2,1,0:T(8,128)(2,1)}, bf16[4,2,96,768]{3,2,1,0:T(8,128)(2,1)}, u32[]{:S(2)}, u32[]{:S(2)}) collective-permute-start(bf16[4,2,96,768]{3,2,1,0:T(8,128)(2,1)} %pad_maximum_fusion.12), channel_id=1, source_target_pairs={{0,16},{1,17},{2,18},{3,19},{4,20},{5,21},{6,22},{7,23},{8,24},{9,... | collective-permute-start | bytes 3538952 | tf_op jit(solution)/shard_map/ppermute | solution.py:33
  215.6 42.2 %all-to-all-start.4 = ((bf16[8,2,64,768]{3,2,1,0:T(8,128)(2,1)}), bf16[8,2,64,768]{3,2,1,0:T(8,128)(2,1)}, u32[]{:S(2)}, u32[]{:S(2)}) async-start(bf16[8,2,64,768]{3,2,1,0:T(8,128)(2,1)} %bitcast.371), calls=%async_computation.4 | async-start | bytes 3145728 | tf_op jit(solution)/shard_map/all_to_all | solution.py:129
  403.6 44.2 %collective-permute-start.36 = (bf16[2,4,2,24,2304]{4,3,1,2,0:T(8,128)(2,1)}, bf16[2,4,2,24,2304]{4,3,1,2,0:T(8,128)(2,1)}, u32[]{:S(2)}, u32[]{:S(2)}) collective-permute-start(bf16[2,4,2,24,2304]{4,3,1,2,0:T(8,128)(2,1)} %fusion.13), channel_id=1, source_target_pairs={{0,8},{1,9},{2,10},{3,11},{4,12},{5,13},{6,14},{7,15},{8,0},{9,1},... | collective-permute-start | bytes 5308424 | tf_op jit(solution)/shard_map/ppermute | solution.py:33
  408.3 42.8 %collective-permute-start.48 = (bf16[2,4,2,24,3072]{4,3,1,2,0:T(8,128)(2,1)}, bf16[2,4,2,24,3072]{4,3,1,2,0:T(8,128)(2,1)}, u32[]{:S(2)}, u32[]{:S(2)}) collective-permute-start(bf16[2,4,2,24,3072]{4,3,1,2,0:T(8,128)(2,1)} %fusion.11), channel_id=1, source_target_pairs={{0,8},{1,9},{2,10},{3,11},{4,12},{5,13},{6,14},{7,15},{8,0},{9,1},... | collective-permute-start | bytes 7077896 | tf_op jit(solution)/shard_map/ppermute | solution.py:33
  420.9 52.4 %collective-permute-start.54 = (bf16[2,4,2,96,768]{4,3,1,2,0:T(8,128)(2,1)}, bf16[2,4,2,96,768]{4,3,1,2,0:T(8,128)(2,1)}, u32[]{:S(2)}, u32[]{:S(2)}) collective-permute-start(bf16[2,4,2,96,768]{4,3,1,2,0:T(8,128)(2,1)} %fusion.12), channel_id=1, source_target_pairs={{0,8},{1,9},{2,10},{3,11},{4,12},{5,13},{6,14},{7,15},{8,0},{9,1},... | collective-permute-start | bytes 7077896 | tf_op jit(solution)/shard_map/ppermute | solution.py:33
  422.8 66.3 %all-to-all-start.1 = ((bf16[8,2,64,768]{3,2,1,0:T(8,128)(2,1)}), bf16[8,2,64,768]{3,2,1,0:T(8,128)(2,1)S(1)}, u32[]{:S(2)}, u32[]{:S(2)}) async-start(bf16[8,2,64,768]{3,2,1,0:T(8,128)(2,1)} %bitcast.354), calls=%async_computation.1 | async-start | bytes 3145728 | tf_op jit(solution)/shard_map/all_to_all | solution.py:126
  444.6 39.8 %collective-permute-start.45 = (bf16[24,768]{1,0:T(8,128)(2,1)S(1)}, bf16[24,768]{1,0:T(8,128)(2,1)S(1)}, u32[]{:S(2)}, u32[]{:S(2)}) collective-permute-start(bf16[24,768]{1,0:T(8,128)(2,1)S(1)} %get-tuple-element.80), channel_id=1, source_target_pairs={{0,2},{1,3},{2,0},{3,1},{4,6},{5,7},{6,4},{7,5},{8,10},{9,11},{10,... | collective-permute-start | bytes 110600 | tf_op jit(solution)/shard_map/ppermute | solution.py:33
  445.4 40.1 %collective-permute-start.47 = (bf16[24,768]{1,0:T(8,128)(2,1)S(1)}, bf16[24,768]{1,0:T(8,128)(2,1)S(1)}, u32[]{:S(2)}, u32[]{:S(2)}) collective-permute-start(bf16[24,768]{1,0:T(8,128)(2,1)S(1)} %get-tuple-element.81), channel_id=1, source_target_pairs={{0,6},{1,7},{2,4},{3,5},{4,2},{5,3},{6,0},{7,1},{8,14},{9,15},{10,... | collective-permute-start | bytes 110600 | tf_op jit(solution)/shard_map/ppermute | solution.py:33
  447.8 40.6 %collective-permute-start.46 = (bf16[24,768]{1,0:T(8,128)(2,1)S(1)}, bf16[24,768]{1,0:T(8,128)(2,1)S(1)}, u32[]{:S(2)}, u32[]{:S(2)}) collective-permute-start(bf16[24,768]{1,0:T(8,128)(2,1)S(1)} %get-tuple-element.82), channel_id=1, source_target_pairs={{0,4},{1,5},{2,6},{3,7},{4,0},{5,1},{6,2},{7,3},{8,12},{9,13},{10,... | collective-permute-start | bytes 110600 | tf_op jit(solution)/shard_map/ppermute | solution.py:33
  471.6 56.3 %collective-permute-start.49 = (bf16[4,2,24,3072]{3,2,0,1:T(8,128)(2,1)}, bf16[4,2,24,3072]{3,2,0,1:T(8,128)(2,1)}, u32[]{:S(2)}, u32[]{:S(2)}) collective-permute-start(bf16[4,2,24,3072]{3,2,0,1:T(8,128)(2,1)} %fusion.30), channel_id=1, source_target_pairs={{0,16},{1,17},{2,18},{3,19},{4,20},{5,21},{6,22},{7,23},{8,24},{9,... | collective-permute-start | bytes 3538952 | tf_op jit(solution)/shard_map/ppermute | solution.py:33
  483.8 39.2 %collective-permute-start.55 = (bf16[4,2,96,768]{3,2,0,1:T(8,128)(2,1)}, bf16[4,2,96,768]{3,2,0,1:T(8,128)(2,1)}, u32[]{:S(2)}, u32[]{:S(2)}) collective-permute-start(bf16[4,2,96,768]{3,2,0,1:T(8,128)(2,1)} %fusion.31), channel_id=1, source_target_pairs={{0,16},{1,17},{2,18},{3,19},{4,20},{5,21},{6,22},{7,23},{8,24},{9,... | collective-permute-start | bytes 3538952 | tf_op jit(solution)/shard_map/ppermute | solution.py:33
  491.0 76.5 %all-to-all-start.2 = ((bf16[8,2,64,768]{3,2,1,0:T(8,128)(2,1)}), bf16[8,2,64,768]{3,2,1,0:T(8,128)(2,1)S(1)}, u32[]{:S(2)}, u32[]{:S(2)}) async-start(bf16[8,2,64,768]{3,2,1,0:T(8,128)(2,1)} %bitcast.370), calls=%async_computation.2 | async-start | bytes 3145728 | tf_op jit(solution)/shard_map/all_to_all | solution.py:129
  (107 other events, 1235.3 us)

commit v2 on v1

v2 whole, which is shorter than its diff:
```python
import itertools

import jax
import jax.numpy as jnp
from jax import lax
from jax.experimental import pallas as pl
from jax.experimental.pallas import tpu as pltpu
from jax.sharding import PartitionSpec as P

HD = 64
WIDE = 2 * HD
NEG = -1e30
LINE = 4
BOTH = ("dp", "fsdp")
bf16 = jnp.bfloat16
f32 = jnp.float32

norm_eps = 1e-12
half_root = 0.7071067811865476
slope_scale = 0.3989422804014327


class Grid:
    def __init__(self, mesh):
        self.dp = mesh.shape["dp"]
        self.fsdp = mesh.shape["fsdp"]
        self.total = self.dp * self.fsdp
        nx = self.fsdp // LINE
        ny = self.dp // 2
        self.size = {"y": ny, "core": 2, "zh": 2, "zl": 2, "x": nx}
        self.stride = {"x": 1, "zl": nx, "zh": 2 * nx, "core": self.fsdp, "y": 2 * self.fsdp}

    def place(self, axis):
        me = lax.axis_index("dp") * self.fsdp + lax.axis_index("fsdp")
        return (me // self.stride[axis]) % self.size[axis]

    def spot(self):
        line = self.place("zh") * 2 + self.place("zl")
        return jnp.stack([self.place("y"), self.place("core"), line, self.place("x")]).astype(
            jnp.int32
        )

    def swap(self, array, axis, step):
        mask = self.stride[axis] * step
        return lax.ppermute(array, BOTH, [(i, i ^ mask) for i in range(self.total)])


AXES = ("y", "core", "zh", "zl", "x")


def place_kernel(spot, *refs, keys):
    out = refs[-1]
    for part, (y, core, x) in zip(refs, keys):
        out[spot[0] ^ y, spot[1] ^ core, 0, spot[3] ^ x] = part[0]


class Gather:
    def __init__(self, grid, shard):
        self.grid = grid
        self.held = shard

    def fetch(self, array, **steps):
        grid = self.grid
        mask = sum(grid.stride[axis] * step for axis, step in steps.items())
        return lax.ppermute(array, BOTH, [(k, k ^ mask) for k in range(grid.total)])

    def send_line(self):
        return [self.fetch(self.held, zl=step & 1, zh=step >> 1) for step in range(1, LINE)]

    def take_line(self, got):
        parts = [self.held] + list(got)
        me = self.grid.place("zh") * 2 + self.grid.place("zl")
        shape = (LINE,) + self.held.shape
        line = lax.broadcasted_iota(jnp.int32, shape, 0)
        held = parts[-1][None]
        for step in range(LINE - 2, -1, -1):
            held = jnp.where(line == (me ^ step), parts[step][None], held)
        self.held = held

    def send_plane(self):
        sizes = self.grid.size
        self.keys = [(y, x) for y in range(sizes["y"]) for x in range(sizes["x"])]
        return [self.fetch(self.held, y=y, x=x) for y, x in self.keys[1:]]

    def take_plane(self, got):
        self.parts = [self.held] + list(got)

    def send_core(self):
        return [self.fetch(part, core=1) for part in self.parts]

    def whole(self, got):
        grid = self.grid
        rows, wide = self.held.shape[1:]
        keys = [(y, core, x) for core in range(2) for y, x in self.keys]
        shape = (grid.size["y"], 2, LINE, grid.size["x"], rows, wide)
        out = pl.pallas_call(
            lambda *refs: place_kernel(*refs, keys=keys),
            grid_spec=pltpu.PrefetchScalarGridSpec(
                num_scalar_prefetch=1,
                grid=(LINE,),
                in_specs=[pl.BlockSpec((1, rows, wide), lambda i, _: (i, 0, 0))] * len(keys),
                out_specs=pl.BlockSpec(
                    shape[:2] + (1,) + shape[3:], lambda i, _: (0, 0, i, 0, 0, 0)
                ),
            ),
            out_shape=jax.ShapeDtypeStruct(shape, bf16),
            cost_estimate=pl.CostEstimate(
                flops=0, bytes_accessed=4 * grid.total * rows * wide, transcendentals=0
            ),
            name="place",
        )(grid.spot(), *self.parts, *got)
        return out.reshape(grid.total * rows, wide)


def join_kernel(query_ref, key_ref, value_ref, out_ref, in_ref, first_ref, up_ref):
    width = out_ref.shape[1]
    for pair in range(width // WIDE):
        for i, ref in enumerate((query_ref, key_ref, value_ref)):
            at = (pair * 3 + i) * WIDE
            first_ref[:, at : at + WIDE] = ref[:, pair * WIDE : (pair + 1) * WIDE]
    up_ref[:, :width] = out_ref[...]
    up_ref[:, width:] = in_ref[...]


def join(w_query, w_key, w_value, w_out, w_in):
    rows, width = w_query.shape
    return pl.pallas_call(
        join_kernel,
        out_shape=[
            jax.ShapeDtypeStruct((rows, 3 * width), bf16),
            jax.ShapeDtypeStruct((rows, width + w_in.shape[1]), bf16),
        ],
        name="join",
    )(w_query, w_key, w_value, w_out, w_in)


def grad_tall_kernel(spot, left_ref, right_ref, out_ref):
    out_ref[0] = tn(left_ref[...], right_ref[...]).astype(bf16)


def grad_tall(grid, left, right, other):
    rows, tall = left.shape
    wide = right.shape[1]
    ny = grid.size["y"]
    block = tall // (2 * ny)
    return pl.pallas_call(
        grad_tall_kernel,
        grid_spec=pltpu.PrefetchScalarGridSpec(
            num_scalar_prefetch=1,
            grid=(ny,),
            in_specs=[
                pl.BlockSpec((rows, block), lambda y, spot: (0, y * 2 + (spot[1] ^ other))),
                pl.BlockSpec((rows, wide), lambda y, _: (0, 0)),
            ],
            out_specs=pl.BlockSpec((1, block, wide), lambda y, _: (y, 0, 0)),
        ),
        out_shape=jax.ShapeDtypeStruct((ny, block, wide), bf16),
        cost_estimate=pl.CostEstimate(
            flops=rows * tall * wide * 2, bytes_accessed=rows * tall * 2, transcendentals=0
        ),
        name="grad_tall",
    )(grid.spot(), left, right)


STRIP = 384


def grad_wide_kernel(spot, left_ref, right_ref, *refs):
    own_ref, other_ref, turned, total = refs[-4:]

    @pl.when(pl.program_id(0) == 0)
    def _():
        turned[...] = left_ref[...].T

    total[...] = jnp.dot(turned[...], right_ref[...], preferred_element_type=f32)
    ny, block = own_ref.shape[:2]
    core = spot[1]
    for y in range(ny):
        at = pl.multiple_of((2 * y + core) * block, 16)
        own_ref[y] = total[pl.ds(at, block), :].astype(bf16)
        at = pl.multiple_of((2 * y + 1 - core) * block, 16)
        other_ref[y] = total[pl.ds(at, block), :].astype(bf16)


def grad_wide(grid, left, right, wide=None, first=0, base=None):
    rows, tall = left.shape
    wide = wide or right.shape[1]
    ny = grid.size["y"]
    block = tall // (2 * ny)
    at = first // STRIP
    made = pl.BlockSpec((ny, block, STRIP), lambda j, _: (0, 0, j + at))
    given = () if base is None else tuple(base)
    return pl.pallas_call(
        grad_wide_kernel,
        grid_spec=pltpu.PrefetchScalarGridSpec(
            num_scalar_prefetch=1,
            grid=(right.shape[1] // STRIP,),
            in_specs=[
                pl.BlockSpec((rows, tall), lambda j, _: (0, 0)),
                pl.BlockSpec((rows, STRIP), lambda j, _: (0, j)),
            ]
            + [pl.BlockSpec(memory_space=pl.ANY)] * len(given),
            out_specs=[made, made],
            scratch_shapes=[pltpu.VMEM((tall, rows), bf16), pltpu.VMEM((tall, STRIP), f32)],
        ),
        out_shape=[jax.ShapeDtypeStruct((ny, block, wide), bf16)] * 2,
        input_output_aliases={3: 0, 4: 1} if given else {},
        cost_estimate=pl.CostEstimate(
            flops=rows * tall * right.shape[1] * 2,
            bytes_accessed=2 * rows * (tall + right.shape[1]),
            transcendentals=0,
        ),
        name="grad_wide",
    )(grid.spot(), left, right, *given)


def fold_plane_kernel(spot, own_ref, got_ref, *outs, keys):
    for out, (y, x) in zip(outs, keys):
        at = (spot[0] ^ y, 0, spot[3] ^ x)
        out[0] = (own_ref[at].astype(f32) + got_ref[at].astype(f32)).astype(bf16)


def fold_line_kernel(spot, *refs):
    parts, outs = refs[:-LINE], refs[-LINE:]
    for step, out in enumerate(outs):
        total = parts[0][spot[2] ^ step].astype(f32)
        for part in parts[1:]:
            total = total + part[spot[2] ^ step].astype(f32)
        out[...] = total.astype(bf16)


class Scatter:
    def __init__(self, grid):
        self.grid = grid

    def fetch(self, array, **steps):
        grid = self.grid
        mask = sum(grid.stride[axis] * step for axis, step in steps.items())
        return lax.ppermute(array, BOTH, [(k, k ^ mask) for k in range(grid.total)])

    def send_core(self, other):
        return self.fetch(other, core=1)

    def send_plane(self, own, got):
        grid = self.grid
        ny, block, wide = own.shape
        nx = grid.size["x"]
        rows = block // (LINE * nx)
        shape = (ny, LINE, nx, rows, wide)
        keys = [(y, x) for y in range(ny) for x in range(nx)]
        whole = pl.BlockSpec((ny, 1, nx, rows, wide), lambda i, _: (0, i, 0, 0, 0))
        parts = pl.pallas_call(
            lambda *refs: fold_plane_kernel(*refs, keys=keys),
            grid_spec=pltpu.PrefetchScalarGridSpec(
                num_scalar_prefetch=1,
                grid=(LINE,),
                in_specs=[whole, whole],
                out_specs=[pl.BlockSpec((1, rows, wide), lambda i, _: (i, 0, 0))] * len(keys),
            ),
            out_shape=[jax.ShapeDtypeStruct((LINE, rows, wide), bf16)] * len(keys),
            cost_estimate=pl.CostEstimate(
                flops=0, bytes_accessed=6 * ny * block * wide, transcendentals=0
            ),
            name="fold_plane",
        )(grid.spot(), own.reshape(shape), got.reshape(shape))
        self.own = parts[0]
        return [self.fetch(part, y=y, x=x) for part, (y, x) in zip(parts[1:], keys[1:])]

    def send_line(self, got):
        rows, wide = self.own.shape[1:]
        parts = pl.pallas_call(
            fold_line_kernel,
            grid_spec=pltpu.PrefetchScalarGridSpec(
                num_scalar_prefetch=1,
                grid=(1,),
                in_specs=[pl.BlockSpec((LINE, rows, wide), lambda i, _: (0, 0, 0))]
                * (1 + len(got)),
                out_specs=[pl.BlockSpec((rows, wide), lambda i, _: (0, 0))] * LINE,
            ),
            out_shape=[jax.ShapeDtypeStruct((rows, wide), bf16)] * LINE,
            cost_estimate=pl.CostEstimate(
                flops=0, bytes_accessed=8 * LINE * rows * wide, transcendentals=0
            ),
            name="fold_line",
        )(self.grid.spot(), self.own, *got)
        self.own = parts[0]
        return [
            self.fetch(part, zl=step & 1, zh=step >> 1)
            for step, part in zip(range(1, LINE), parts[1:])
        ]

    def finish(self, got):
        total = self.own.astype(f32)
        for one in got:
            total = total + one.astype(f32)
        return total


def tie(values, after):
    return lax.optimization_barrier((values, after))


def standardize(values):
    centre = values - jnp.mean(values, axis=-1, keepdims=True)
    spread = lax.rsqrt(jnp.mean(centre * centre, axis=-1, keepdims=True) + norm_eps)
    return (centre * spread, spread)


def norm_back(d_normed, normed, spread):
    return spread * (
        d_normed
        - jnp.mean(d_normed, axis=-1, keepdims=True)
        - normed * jnp.mean(d_normed * normed, axis=-1, keepdims=True)
    )


def gelu_value(values):
    return 0.5 * values * (1.0 + lax.erf(values * half_root))


def gelu_slope(values):
    return (
        0.5 * (1.0 + lax.erf(values * half_root))
        + values * jnp.exp(-0.5 * values * values) * slope_scale
    )


def matmul(left, right):
    return jnp.dot(left, right, preferred_element_type=f32)


def left_times(left, right):
    return jnp.einsum("ti,to->io", left, right, preferred_element_type=f32)


def right_times(grads, weight):
    return jnp.einsum("to,io->ti", grads, weight, preferred_element_type=f32)


def nt(left, right):
    return lax.dot_general(left, right, (((1,), (1,)), ((), ())), preferred_element_type=f32)


def tn(left, right):
    return lax.dot_general(left, right, (((0,), (0,)), ((), ())), preferred_element_type=f32)


def head_lanes(shape, head):
    lane = lax.broadcasted_iota(jnp.int32, shape, 1)
    return (lane >= head * HD) & (lane < (head + 1) * HD)


def score_operands(query, key_rows, length, head):
    rows, wide = query.shape
    lane = lax.broadcasted_iota(jnp.int32, (rows, wide), 1)
    row = lax.broadcasted_iota(jnp.int32, (rows, wide), 0)
    spare = (1 - head) * HD
    mine = head_lanes((rows, wide), head)
    one = jnp.where(lane == spare, 1.0, 0.0).astype(bf16)
    mask = jnp.where(row < length, 0.0, NEG).astype(bf16)
    left = jnp.where(mine, query * bf16(HD ** (-0.5)), one)
    right = jnp.where(lane == spare, mask, key_rows)
    return left, right


def attend_kernel(lengths, fused_ref, context_ref, total_ref, *, first):
    length = lengths[first + pl.program_id(0)]
    query, key_rows, value = (fused_ref[:, i * WIDE : (i + 1) * WIDE] for i in range(3))
    weights, values, scales = [], [], []
    for head in range(2):
        left, right = score_operands(query, key_rows, length, head)
        scores = nt(right, left)
        top = jnp.max(scores, axis=0, keepdims=True)
        raised = jnp.exp(scores - top)
        amount = jnp.sum(raised, axis=0, keepdims=True)
        total_ref[0, 0, head : head + 1, :] = top + jnp.log(amount)
        scales.append(1.0 / amount)
        weights.append(raised.astype(bf16))
        values.append(jnp.where(head_lanes(value.shape, head), value, bf16(0)))
    context = tn(jnp.concatenate(values, axis=0), jnp.concatenate(weights, axis=0))
    context = jnp.concatenate([context[:HD] * scales[0], context[HD:] * scales[1]], axis=0)
    context_ref[...] = context.T.astype(bf16)


def attend(fused, lengths, slots, first, count):
    width = fused.shape[1] // 3
    rows = fused.shape[0] // slots
    pairs = width // WIDE
    return pl.pallas_call(
        lambda *refs: attend_kernel(*refs, first=first),
        grid_spec=pltpu.PrefetchScalarGridSpec(
            num_scalar_prefetch=1,
            grid=(count, pairs),
            in_specs=[pl.BlockSpec((rows, 3 * WIDE), lambda s, h, _: (s + first, h))],
            out_specs=[
                pl.BlockSpec((rows, WIDE), lambda s, h, _: (s, h)),
                pl.BlockSpec((1, 1, 2, rows), lambda s, h, _: (s, h, 0, 0)),
            ],
        ),
        out_shape=[
            jax.ShapeDtypeStruct((count * rows, width), bf16),
            jax.ShapeDtypeStruct((count, pairs, 2, rows), f32),
        ],
        cost_estimate=pl.CostEstimate(
            flops=4 * count * rows * rows * width * 4,
            bytes_accessed=8 * count * rows * width,
            transcendentals=count * pairs * 2 * rows * rows,
        ),
        name="attend",
    )(lengths, fused)


def attend_back_kernel(lengths, fused_ref, total_ref, up_ref, d_ref, sums_ref):
    length = lengths[pl.program_id(1)]
    query, key_rows, value = (fused_ref[:, i * WIDE : (i + 1) * WIDE] for i in range(3))
    up = up_ref[...]
    weights, slopes, ups, queries, keys = [], [], [], [], []
    for head in range(2):
        left, right = score_operands(query, key_rows, length, head)
        mine = head_lanes(query.shape, head)
        scores = nt(right, left)
        probs = jnp.exp(scores - total_ref[0, 0, head : head + 1, :])
        masked = jnp.where(mine, up, bf16(0))
        d_probs = nt(value, masked)
        product = probs * d_probs
        d_scores = product - probs * jnp.sum(product, axis=0, keepdims=True)
        weights.append(probs.astype(bf16))
        slopes.append(d_scores.astype(bf16))
        ups.append(masked)
        queries.append(jnp.where(mine, query * bf16(HD ** (-0.5)), bf16(0)))
        keys.append(jnp.where(mine, key_rows * bf16(HD ** (-0.5)), bf16(0)))
    d_value = jnp.dot(
        jnp.concatenate(weights, axis=1), jnp.concatenate(ups, axis=0), preferred_element_type=f32
    ).astype(bf16)
    d_key = jnp.dot(
        jnp.concatenate(slopes, axis=1), jnp.concatenate(queries, axis=0), preferred_element_type=f32
    ).astype(bf16)
    d_query = tn(jnp.concatenate(keys, axis=0), jnp.concatenate(slopes, axis=0)).T.astype(bf16)
    d_ref[:, 0:WIDE] = d_query
    d_ref[:, WIDE : 2 * WIDE] = d_key
    d_ref[:, 2 * WIDE :] = d_value
    sums_ref[0, 0:1, :] = jnp.sum(d_query.astype(f32), axis=0, keepdims=True)
    sums_ref[0, 1:2, :] = jnp.sum(d_value.astype(f32), axis=0, keepdims=True)


def attend_back(fused, totals, up, lengths, slots, first, count):
    width = fused.shape[1] // 3
    rows = fused.shape[0] // slots
    return pl.pallas_call(
        attend_back_kernel,
        grid_spec=pltpu.PrefetchScalarGridSpec(
            num_scalar_prefetch=1,
            grid=(count, slots),
            in_specs=[
                pl.BlockSpec((rows, 3 * WIDE), lambda h, s, _: (s, first + h)),
                pl.BlockSpec((1, 1, 2, rows), lambda h, s, _: (s, first + h, 0, 0)),
                pl.BlockSpec((rows, WIDE), lambda h, s, _: (s, first + h)),
            ],
            out_specs=[
                pl.BlockSpec((rows, 3 * WIDE), lambda h, s, _: (s, h)),
                pl.BlockSpec((1, 2, WIDE), lambda h, s, _: (s, 0, h)),
            ],
        ),
        out_shape=[
            jax.ShapeDtypeStruct((slots * rows, count * 3 * WIDE), bf16),
            jax.ShapeDtypeStruct((slots, 2, count * WIDE), f32),
        ],
        cost_estimate=pl.CostEstimate(
            flops=10 * slots * rows * rows * count * WIDE * 4,
            bytes_accessed=16 * slots * rows * count * WIDE,
            transcendentals=slots * count * 2 * rows * rows,
        ),
        name="attend_back",
    )(lengths, fused, totals, up)


def interleave(query, key_rows, value):
    lead = query.shape[0]
    return jnp.stack([one.reshape(lead, -1, WIDE) for one in (query, key_rows, value)], axis=2).reshape(
        lead, -1
    )


def pieces_out(array, count):
    slots, rows, width = array.shape
    return array.reshape(slots, count, rows // count, width).transpose(1, 0, 2, 3)


def spread_out(array):
    count = lax.axis_size("fsdp")
    return lax.all_to_all(pieces_out(array, count), "fsdp", 0, 0, tiled=True)


def bring_in(spread, source):
    count, slots, short, width = spread.shape
    spread = spread.reshape(count * slots, short, width)
    spread = jnp.take(spread, source, axis=0, mode="clip").reshape(count, slots, short, width)
    return lax.all_to_all(spread, "fsdp", 0, 0, tiled=True)


def joined(pieces):
    count, slots, short, width = pieces.shape
    return pieces.transpose(1, 0, 2, 3).reshape(slots, count * short, width)


def per_device(grid, *args):
    (
        tokens,
        cotangent,
        lengths,
        deal,
        w_query,
        b_query,
        w_key,
        w_value,
        b_value,
        w_out,
        b_out,
        gain_one,
        shift_one,
        w_in,
        b_in,
        w_down,
        b_down,
        gain_two,
        shift_two,
    ) = args
    slots, rows, width = tokens.shape
    pairs = width // WIDE
    position = lax.axis_index("fsdp")
    deal_row = deal[0]
    my_lengths = lax.dynamic_slice_in_dim(lengths[0], position * slots, slots)
    spots = jnp.arange(deal_row.shape[0], dtype=jnp.int32)
    inverse = jnp.sum(
        jnp.where(deal_row[None, :] == spots[:, None], spots[None, :], 0), axis=1
    )

    singles = (b_query, b_value, b_out, gain_one, shift_one, b_in, b_down, gain_two, shift_two)
    own, up_own = join(w_query, w_key, w_value, w_out, w_in)
    first = Gather(grid, own)
    up_weights = Gather(grid, up_own)
    down_weights = Gather(grid, w_down)

    got = first.send_line()
    got_up = up_weights.send_line()
    got_down = down_weights.send_line()
    first.take_line(got)
    got = first.send_plane()
    singles, first.held = tie(singles, first.held)
    small = jnp.concatenate(singles)
    small = lax.all_to_all(
        jnp.broadcast_to(small[None, :], (grid.total, small.shape[0])), BOTH, 0, 0, tiled=True
    )
    (cotangent, got), _ = tie((cotangent, got), ())
    first.take_plane(got)
    up_weights.take_line(got_up)
    down_weights.take_line(got_down)
    (up_weights.held, down_weights.held), _ = tie(
        (up_weights.held, down_weights.held), got
    )
    got = first.send_core()
    got_up = up_weights.send_plane()
    up_spread = spread_out(cotangent)
    qkv = first.whole(got)

    vectors = []
    at = 0
    for one in singles:
        vectors.append(small[:, at : at + one.shape[0]].reshape(-1).astype(f32))
        at += one.shape[0]
    bq, bv, bo, g1, s1, bi, bd, g2, s2 = vectors

    total_rows = slots * rows
    inputs = tokens.reshape(total_rows, width)
    valid = jnp.arange(rows)[None, :] < my_lengths[:, None]
    valid_row = valid.reshape(total_rows)[:, None]

    bias = interleave(bq[None], jnp.zeros_like(bq)[None], bv[None])
    fused = (matmul(inputs, qkv) + bias).astype(bf16)
    (down_weights.held, fused) = lax.optimization_barrier((down_weights.held, fused))
    got_down = down_weights.send_plane()
    halves = []
    for slot in range(slots):
        halves.append(attend(fused, my_lengths, slots, slot, 1))
        (fused, halves), _ = tie((fused, halves), ())
    (halves, up_spread), got_up = tie((halves, up_spread), got_up)
    up_weights.take_plane(got_up)
    got_up = up_weights.send_core()
    upstream = bring_in(up_spread, deal_row)
    context = jnp.concatenate([half[0] for half in halves], axis=0)
    totals = jnp.concatenate([half[1] for half in halves], axis=0)
    up_whole = up_weights.whole(got_up)
    wo, wi = up_whole[:, :width], up_whole[:, width:]

    middle_norm, middle_spread = standardize(inputs.astype(f32) + matmul(context, wo) + bo)
    middle = middle_norm * g1 + s1
    middle_low = middle.astype(bf16)
    hidden = matmul(middle_low, wi) + bi
    active = gelu_value(hidden).astype(bf16)
    active, got_down = tie(active, got_down)
    down_weights.take_plane(got_down)
    wd = down_weights.whole(down_weights.send_core())
    final_norm, final_spread = standardize(middle + matmul(active, wd) + bd)
    output = jnp.where(valid_row, final_norm * g2 + s2, 0.0).astype(bf16)

    upstream = joined(upstream).reshape(total_rows, width).astype(f32)
    d_result = jnp.where(valid_row, upstream, 0.0)
    grad_g2 = jnp.sum(d_result * final_norm, axis=0)
    grad_s2 = jnp.sum(d_result, axis=0)
    d_final = norm_back(d_result * g2, final_norm, final_spread)
    d_branch = d_final.astype(bf16)
    grad_bd = jnp.sum(d_branch.astype(f32), axis=0)

    plane, line = ("y", "x"), ("zh", "zl")
    sum_down, sum_up, sum_first, sum_second = (Scatter(grid) for _ in range(4))
    other = grad_tall(grid, active, d_branch, 1)
    got_down = sum_down.send_core(other)
    own_down = grad_tall(grid, active, d_branch, 0)
    output, d_branch = tie(output, d_branch)
    out_spread = spread_out(output.reshape(slots, rows, width))
    d_hidden = (right_times(d_branch, wd) * gelu_slope(hidden)).astype(bf16)
    grad_bi = jnp.sum(d_hidden.astype(f32), axis=0)
    d_hidden, got_down = tie(d_hidden, got_down)
    got_down = sum_down.send_plane(own_down, got_down)
    own_up, other = grad_wide(grid, middle_low, d_hidden)
    got_up = sum_up.send_core(other)
    d_middle = d_final + right_times(d_hidden, wi)
    grad_g1 = jnp.sum(d_middle * middle_norm, axis=0)
    grad_s1 = jnp.sum(d_middle, axis=0)
    d_sum = norm_back(d_middle * g1, middle_norm, middle_spread)
    d_attended = d_sum.astype(bf16)
    grad_bo = jnp.sum(d_attended.astype(f32), axis=0)
    d_attended, got_up = tie(d_attended, got_up)
    got_up = sum_up.send_plane(own_up, got_up)
    half = pairs // 2
    wide = width + half * 3 * WIDE
    begun = grad_wide(grid, context, d_attended, wide)
    d_context = right_times(d_attended, wo).astype(bf16)
    d_first, sums_first = attend_back(fused, totals, d_context, my_lengths, slots, 0, half)
    (d_first, d_context, out_spread), got_down = tie((d_first, d_context, out_spread), got_down)
    got_down = sum_down.send_line(got_down)
    out_pieces = bring_in(out_spread, inverse)
    own_first, other = grad_wide(grid, inputs, d_first, wide, width, begun)
    got_first = sum_first.send_core(other)
    d_second, sums_second = attend_back(
        fused, totals, d_context, my_lengths, slots, half, pairs - half
    )
    (d_second, d_sum), (got_up, got_first) = tie((d_second, d_sum), (got_up, got_first))
    got_first = sum_first.send_plane(own_first, got_first)
    own_second, other = grad_wide(grid, inputs, d_second)
    got_second = sum_second.send_core(other)
    got_up = sum_up.send_line(got_up)
    d_fused = jnp.concatenate([d_first, d_second], axis=1)
    (d_fused, d_sum), got_second = tie((d_fused, d_sum), got_second)
    got_second = sum_second.send_plane(own_second, got_second)
    input_grad = (d_sum + right_times(d_fused, qkv)).astype(bf16).reshape(slots, rows, width)
    input_grad, got_first = tie(input_grad, got_first)
    got_first = sum_first.send_line(got_first)
    got_second = sum_second.send_line(got_second)
    shard_first = sum_first.finish(got_first)
    shard_second = sum_second.finish(got_second)
    layer_out = joined(out_pieces)
    shard_qkv = jnp.concatenate([shard_first[:, width:], shard_second], axis=1).reshape(-1, pairs, 3, WIDE)
    shard_q, shard_k, shard_v = (shard_qkv[:, :, i].reshape(-1, width) for i in range(3))
    sums = jnp.sum(jnp.concatenate([sums_first, sums_second], axis=-1), axis=0)

    grads = (sums[0], sums[1], grad_bo, grad_g1, grad_s1, grad_bi, grad_bd, grad_g2, grad_s2)
    small = jnp.concatenate([one.reshape(grid.total, -1) for one in grads], axis=1)
    small = jnp.sum(lax.all_to_all(small, BOTH, 0, 0, tiled=True), axis=0)
    parts = []
    at = 0
    for one in singles:
        parts.append(small[at : at + one.shape[0]])
        at += one.shape[0]
    pbq, pbv, pbo, pg1, ps1, pbi, pbd, pg2, ps2 = parts
    return (
        layer_out,
        input_grad,
        shard_q,
        pbq,
        shard_k,
        shard_v,
        pbv,
        shard_first[:, :width],
        pbo,
        pg1,
        ps1,
        sum_up.finish(got_up),
        pbi,
        sum_down.finish(got_down),
        pbd,
        pg2,
        ps2,
    )


def solution(mesh):
    grid = Grid(mesh)
    rows3 = P(BOTH, None, None)
    rows2 = P(BOTH, None)
    rows1 = P(BOTH)
    table = P("dp", None)
    kinds = (2, 1, 2, 2, 1, 2, 1, 1, 1, 2, 1, 2, 1, 1, 1)
    placed = tuple(rows2 if kind == 2 else rows1 for kind in kinds)

    def step(*args):
        return per_device(grid, *args)

    return jax.shard_map(
        step,
        mesh=mesh,
        in_specs=(rows3, rows3, table, table) + placed,
        out_specs=(rows3, rows3) + placed,
        check_vma=False,
    )
```

time: 578 us -> 477 us (0.83)
  Pallas kernels: 0 us -> 142 us
  waiting for transfers between devices: 173 us -> 96.7 us
  matrix products: 140 us -> 64.9 us
  other arithmetic: 85.3 us -> 34.8 us
  local copies, waits for them, and re-layouts: 72.8 us -> 33.7 us
    pallas_call x0 -> x22, Pallas kernels: none -> 142 us  [the longest x4 33.6 us: grad_wide(): pl.pallas_call(grad_wide_kernel, grid_spec=pltpu.PrefetchScalarGridSpec(n...]
    dot_general x10 -> x0, matrix products: 94.3 us -> none  [the longest x4 24.1 us: left_times(): return jnp.einsum('ti,to->io', left, right, preferred_element_type=f32)]
    ppermute x60 -> x58, waiting for transfers between devices: 156 us -> 90.3 us  [fetch(): return lax.ppermute(array, BOTH, [(k, k ^ mask) for k in range(grid.total)])]
    convert_element_type x22 -> x1, local copies, waits for them, and re-layouts: 21 us -> 0.3 us  [per_device(): upstream = joined(upstream).reshape(total_rows, width).astype(f32)]
    another operation x46 -> x2, other arithmetic: 19.8 us -> 0.73 us  [the longest x1 0.66 us: spot(): jnp.stack([self.place('y'), self.place('core'), line, self.place('x')])]
    convert_element_type x2 -> x3, other arithmetic: 23.8 us -> 5.85 us  [the longest x1 3.56 us: per_device(): (d_sum + right_times(d_fused, qkv)).astype(bf16).reshape(slots, rows, width)]
    all_to_all x4, waiting for transfers between devices: 13 us -> 0.01 us  [the longest x2 0.01 us: bring_in(): return lax.all_to_all(spread, 'fsdp', 0, 0, tiled=True)]
    add x17 -> x4, other arithmetic: 17.9 us -> 5.42 us  [finish(): total = total + one.astype(f32)]
  transfers between devices with their start and end apart: 66 -> 64, of which waited for: 21 -> 13; matrix products, arithmetic and copies ran while one was open for 25% -> 24% of each run, Pallas kernels for 0% -> 26%
where the time goes in v2:
time: 477 us; the launch traced here: 469 us
  Pallas kernels  142 us (30%)
  waiting for transfers between devices  96.7 us (20%)
  starting transfers between devices  94.3 us (20%)
  matrix products  64.9 us (14%)
  other arithmetic  34.8 us (7%)
  local copies, waits for them, and re-layouts  33.7 us (7%)
    ppermute x58, waiting for transfers between devices, fetch(): return lax.ppermute(array, BOTH, [(k, k ^ mask) for k in range(grid.total)])  90.3 us
    ppermute x58, starting transfers between devices, fetch(): return lax.ppermute(array, BOTH, [(k, k ^ mask) for k in range(grid.total)])  66.1 us
    dot_general x4, matrix products, right_times(): return jnp.einsum('to,io->ti', grads, weight, preferred_element_type=f32)  34 us
    pallas_call x4, Pallas kernels, grad_wide(): pl.pallas_call(grad_wide_kernel, grid_spec=pltpu.PrefetchScalarGridSpec(n...  33.6 us
    dot_general x4, matrix products, matmul(): return jnp.dot(left, right, preferred_element_type=f32)  30.9 us
    pallas_call x2, Pallas kernels, attend_back(): pl.pallas_call(attend_back_kernel, grid_spec=pltpu.PrefetchScalarGridSpec...  26.6 us
    pallas_call x4, Pallas kernels, send_plane(): pl.pallas_call(lambda *refs: fold_plane_kernel(*refs, keys=keys), grid_sp...  19 us
    pallas_call x2, Pallas kernels, attend(): pl.pallas_call(lambda *refs: attend_kernel(*refs, first=first), grid_spec...  18.5 us
  transfers between devices with their start and end apart: 64, of which 13 were waited for; matrix products, arithmetic and copies ran while one was open for 24% of the time, Pallas kernels for 26%

profile of v2, /device:TPU:0, one launch (start us, length us, event | category | flops | bytes accessed | tf_op | source)
XLA Modules:
  0.0 468.5 jit_solution(8066587574775167568)
XLA Ops:
  12.0 7.7 %collective-permute-done.8 = bf16[24,2304]{1,0:T(8,128)(2,1)S(1)} collective-permute-done((bf16[24,2304]{1,0:T(8,128)(2,1)}, bf16[24,2304]{1,0:T(8,128)(2,1)S(1)}, u32[]{:S(2)}, u32[]{:S(2)}) %collective-permute-start.8) | collective-permute-done | bytes 110624 | tf_op jit(solution)/shard_map/ppermute | solution.py:65
  19.7 13.2 %collective-permute-done.7 = bf16[24,2304]{1,0:T(8,128)(2,1)S(1)} collective-permute-done((bf16[24,2304]{1,0:T(8,128)(2,1)}, bf16[24,2304]{1,0:T(8,128)(2,1)S(1)}, u32[]{:S(2)}, u32[]{:S(2)}) %collective-permute-start.7) | collective-permute-done | bytes 110624 | tf_op jit(solution)/shard_map/ppermute | solution.py:65
  38.1 6.1 %concatenate.21 = bf16[288]{0:T(512)(128)(2,1)S(1)} concatenate(bf16[24]{0:T(256)(128)(2,1)} %param.24, bf16[24]{0:T(256)(128)(2,1)} %param.27, bf16[24]{0:T(256)(128)(2,1)} %param.29, bf16[24]{0:T(256)(128)(2,1)} %param.30, bf16[24]{0:T(256)(128)(2,1)} %param.31, bf16[96]{0:T(256)(128)(2,1)} %param.33, bf16[24]{0:T(256)(128)(2,1)} %param.35, bf16[24]{0:T(256)(128)(2,1)} %param.36, ...), dimensions={0} | concatenate | bytes 1152 | tf_op jit(solution)/shard_map/concatenate | solution.py:550
  51.7 6.5 %all-to-all-done = bf16[32,2,144]{2,1,0:T(2,128)(2,1)S(1)} async-done(((bf16[32,2,144]{2,1,0:T(2,128)(2,1)}), bf16[32,2,144]{2,1,0:T(2,128)(2,1)S(1)}, u32[]{:S(2)}, u32[]{:S(2)}) %all-to-all-start) | async-done | bytes 18464 | tf_op jit(solution)/shard_map/all_to_all | solution.py:551
  78.8 21.9 %collective-permute-done = bf16[24,3840]{1,0:T(8,128)(2,1)S(1)} collective-permute-done((bf16[24,3840]{1,0:T(8,128)(2,1)S(1)}, bf16[24,3840]{1,0:T(8,128)(2,1)S(1)}, u32[]{:S(2)}, u32[]{:S(2)}) %collective-permute-start) | collective-permute-done | bytes 184352 | tf_op jit(solution)/shard_map/ppermute | solution.py:65
  111.5 8.6 %fusion.6.refs_1_.fused_ref = bf16[1024,2304]{1,0:T(8,128)(2,1)} fusion(bf16[1024,768]{1,0:T(8,128)(2,1)} %bitcast.95, bf16[768,2304]{1,0:T(8,128)(2,1)} %bitcast.89, f32[2304]{0:T(1024)S(1)} %copy-done.52), kind=kOutput, calls=%fused_computation.13 | convolution fusion | flops 3628597248 | bytes 9839616 | tf_op jit(solution)/shard_map/dot_general | solution.py:329
  120.1 9.2 %attend.2 = (bf16[512,768]{1,0:T(8,128)(2,1)}, f32[1,6,2,512]{3,2,1,0:T(2,128)}) custom-call(s32[2]{0:T(128)} %dynamic-slice_bitcast_fusion.refs_0_.lengths, bf16[1024,2304]{1,0:T(8,128)(2,1)} %fusion.6.refs_1_.fused_ref), custom_call_target="tpu_custom_call" | custom-call | flops 3221225472 | bytes 3145728 | tf_op jit(solution)/shard_map/attend/pallas_call | solution.py:389
  129.3 9.4 %attend.3 = (bf16[512,768]{1,0:T(8,128)(2,1)}, f32[1,6,2,512]{3,2,1,0:T(2,128)}) custom-call(s32[2]{0:T(128)} %dynamic-slice_bitcast_fusion.refs_0_.lengths, bf16[1024,2304]{1,0:T(8,128)(2,1)} %fusion.6.refs_1_.fused_ref), custom_call_target="tpu_custom_call" | custom-call | flops 3221225472 | bytes 3145728 | tf_op jit(solution)/shard_map/attend/pallas_call | solution.py:389
  151.3 6.4 %place.4 = bf16[2,2,4,2,24,3840]{5,4,3,2,1,0:T(8,128)(2,1)} custom-call(s32[4]{0:T(128)} %pad_add_fusion.refs_0_.spot, bf16[4,24,3840]{2,1,0:T(8,128)(2,1)} %copy-done.10, bf16[4,24,3840]{2,1,0:T(8,128)(2,1)} %collective-permute-done.16.refs_2_, bf16[4,24,3840]{2,1,0:T(8,128)(2,1)} %collective-permute-done.17.refs_3_, ...), custom_call_target="tpu_custom_call" | custom-call | bytes 11796480 | tf_op jit(solution)/shard_map/place/pallas_call | solution.py:96
  164.9 9.7 %multiply_convert_fusion = (bf16[1024,3072]{1,0:T(8,128)(2,1)}, f32[1024,3072]{1,0:T(8,128)}) fusion(f32[3072]{0:T(1024)S(1)} %reshape.339, bf16[1024,768]{1,0:T(8,128)(2,1)S(1)} %fusion.12.left_ref, bf16[768,3840]{1,0:T(8,128)(2,1)S(1)} %bitcast.86), kind=kOutput, calls=%fused_computation.10 | convolution fusion | flops 4850712576 | bytes 25178112 | tf_op jit(solution)/shard_map/dot_general | solution.py:329
  174.6 10.8 %collective-permute-done.25.refs_4_ = bf16[4,96,768]{2,1,0:T(8,128)(2,1)} collective-permute-done((bf16[4,96,768]{2,1,0:T(8,128)(2,1)S(1)}, bf16[4,96,768]{2,1,0:T(8,128)(2,1)}, u32[]{:S(2)}, u32[]{:S(2)}) %collective-permute-start.25) | collective-permute-done | bytes 589856 | tf_op jit(solution)/shard_map/ppermute | solution.py:65
  189.3 5.7 %place.5 = bf16[2,2,4,2,96,768]{5,4,3,2,1,0:T(8,128)(2,1)} custom-call(s32[4]{0:T(128)} %pad_add_fusion.refs_0_.spot, bf16[4,96,768]{2,1,0:T(8,128)(2,1)} %copy-done.11, bf16[4,96,768]{2,1,0:T(8,128)(2,1)} %copy-done.22, bf16[4,96,768]{2,1,0:T(8,128)(2,1)} %copy-done.23, bf16[4,96,768]{2,1,0:T(8,128)(2,1)} %collective-permute-done.25.refs_4_, ...), custom_call_target="tpu_custom_call" | custom-call | bytes 9437184 | tf_op jit(solution)/shard_map/place/pallas_call | solution.py:96
  195.0 9.3 %fusion.20 = (f32[1024]{0:T(1024)S(1)}, f32[1024,768]{1,0:T(8,128)S(1)}) fusion(f32[768]{0:T(1024)S(1)} %reshape.340, bf16[1024,3072]{1,0:T(8,128)(2,1)} %get-tuple-element.169.left_ref, bf16[3072,768]{1,0:T(8,128)(2,1)} %bitcast.87, f32[768]{0:T(1024)S(1)} %reshape.338, f32[768]{0:T(1024)S(1)} %reshape.337, f32[1024]{0:T(1024)S(1)} %add_rsqrt_fusion.1, ...), kind=kOutput, calls=%fused_computation.101 | convolution fusion | flops 4837342208 | bytes 17323008 | tf_op jit(solution)/shard_map/dot_general | solution.py:329
  216.4 6.5 %grad_tall.2 = bf16[2,768,768]{2,1,0:T(8,128)(2,1)} custom-call(s32[4]{0:T(128)} %pad_add_fusion.refs_0_.spot, bf16[1024,3072]{1,0:T(8,128)(2,1)} %get-tuple-element.169.left_ref, bf16[1024,768]{1,0:T(8,128)(2,1)} %get-tuple-element.174.right_ref), custom_call_target="tpu_custom_call" | custom-call | flops 4831838208 | bytes 6291456 | tf_op jit(solution)/shard_map/grad_tall/pallas_call | solution.py:146
  222.9 6.7 %grad_tall.3 = bf16[2,768,768]{2,1,0:T(8,128)(2,1)} custom-call(s32[4]{0:T(128)} %pad_add_fusion.refs_0_.spot, bf16[1024,3072]{1,0:T(8,128)(2,1)} %get-tuple-element.169.left_ref, bf16[1024,768]{1,0:T(8,128)(2,1)} %get-tuple-element.174.right_ref), custom_call_target="tpu_custom_call" | custom-call | flops 4831838208 | bytes 6291456 | tf_op jit(solution)/shard_map/grad_tall/pallas_call | solution.py:146
  235.5 13.6 %convert_reduce_fusion = (f32[3072]{0:T(1024)S(1)}, bf16[1024,3072]{1,0:T(8,128)(2,1)}) fusion(f32[1024,3072]{1,0:T(8,128)} %get-tuple-element.282, f32[3072]{0:T(1024)S(1)} %reshape.339, bf16[1024,768]{1,0:T(8,128)(2,1)S(1)} %copy-done.13, bf16[3072,768]{1,0:T(8,128)(2,1)} %bitcast.88), kind=kOutput, calls=%fused_computation.9 | convolution fusion | flops 4872729600 | bytes 25190400 | tf_op jit(solution)/shard_map/to,io->ti/dot_general | solution.py:337
  249.1 13.3 %grad_wide.4 = (bf16[2,192,3072]{2,1,0:T(8,128)(2,1)}, bf16[2,192,3072]{2,1,0:T(8,128)(2,1)}) custom-call(s32[4]{0:T(128)} %pad_add_fusion.refs_0_.spot, bf16[1024,768]{1,0:T(8,128)(2,1)} %copy-done.17, bf16[1024,3072]{1,0:T(8,128)(2,1)} %get-tuple-element.175.right_ref), custom_call_target="tpu_custom_call" | custom-call | flops 4831838208 | bytes 7864320 | tf_op jit(solution)/shard_map/grad_wide/pallas_call | solution.py:193
  262.8 11.1 %multiply_reduce_fusion.1 = (f32[768]{0:T(1024)S(1)}, f32[1024]{0:T(1024)S(1)}, f32[1024]{0:T(1024)S(1)}, f32[768]{0:T(1024)S(1)}, f32[1024,768]{1,0:T(8,128)}) fusion(f32[1024,768]{1,0:T(8,128)S(1)} %copy-done.4, f32[1024]{0:T(1024)S(1)} %add_rsqrt_fusion.1, f32[1024]{0:T(1024)S(1)} %broadcast_multiply_fusion.4, f32[768]{0:T(1024)S(1)} %reshape.337, ...), kind=kOutput, calls=%fused_computation.23 | convolution fusion | flops 4839698432 | bytes 20472832 | tf_op jit(solution)/shard_map/to,io->ti/dot_general | solution.py:337
  286.6 6.0 %grad_wide.5 = (bf16[2,192,1920]{2,1,0:T(8,128)(2,1)}, bf16[2,192,1920]{2,1,0:T(8,128)(2,1)}) custom-call(s32[4]{0:T(128)} %pad_add_fusion.refs_0_.spot, bf16[1024,768]{1,0:T(8,128)(2,1)} %copy-done.32, bf16[1024,768]{1,0:T(8,128)(2,1)} %get-tuple-element.177.right_ref), custom_call_target="tpu_custom_call" | custom-call | flops 1207959552 | bytes 3145728 | tf_op jit(solution)/shard_map/grad_wide/pallas_call | solution.py:193
  296.4 13.3 %attend_back.2 = (bf16[1024,1152]{1,0:T(8,128)(2,1)}, f32[2,2,384]{2,1,0:T(2,128)}) custom-call(s32[2]{0:T(128)} %dynamic-slice_bitcast_fusion.refs_0_.lengths, bf16[1024,2304]{1,0:T(8,128)(2,1)} %fusion.6.refs_1_.fused_ref, f32[2,6,2,512]{3,2,1,0:T(2,128)} %copy-done.51, bf16[1024,768]{1,0:T(8,128)(2,1)} %convolution_convert_fusion.up_ref), custom_call_target="tpu_custom_call" | custom-call | flops 8053063680 | bytes 6291456 | tf_op jit(solution)/shard_map/attend_back/pallas_call | solution.py:449
  309.7 7.1 %grad_wide.6 = (bf16[2,192,1920]{2,1,0:T(8,128)(2,1)}, bf16[2,192,1920]{2,1,0:T(8,128)(2,1)}) custom-call(s32[4]{0:T(128)} %pad_add_fusion.refs_0_.spot, bf16[1024,768]{1,0:T(8,128)(2,1)} %bitcast.96, bf16[1024,1152]{1,0:T(8,128)(2,1)} %get-tuple-element.185.right_ref, ...), custom_call_target="tpu_custom_call", output_to_operand_aliasing={{0}: (3, {}), {1}: (4, {})} | custom-call | flops 1811939328 | bytes 3932160 | tf_op jit(solution)/shard_map/grad_wide/pallas_call | solution.py:193
  326.3 13.3 %attend_back.3 = (bf16[1024,1152]{1,0:T(8,128)(2,1)}, f32[2,2,384]{2,1,0:T(2,128)}) custom-call(s32[2]{0:T(128)} %dynamic-slice_bitcast_fusion.refs_0_.lengths, bf16[1024,2304]{1,0:T(8,128)(2,1)} %fusion.6.refs_1_.fused_ref, f32[2,6,2,512]{3,2,1,0:T(2,128)} %copy-done.51, bf16[1024,768]{1,0:T(8,128)(2,1)} %convolution_convert_fusion.up_ref), custom_call_target="tpu_custom_call" | custom-call | flops 8053063680 | bytes 6291456 | tf_op jit(solution)/shard_map/attend_back/pallas_call | solution.py:449
  367.1 7.3 %grad_wide.7 = (bf16[2,192,1152]{2,1,0:T(8,128)(2,1)}, bf16[2,192,1152]{2,1,0:T(8,128)(2,1)}) custom-call(s32[4]{0:T(128)} %pad_add_fusion.refs_0_.spot, bf16[1024,768]{1,0:T(8,128)(2,1)} %bitcast.97, bf16[1024,1152]{1,0:T(8,128)(2,1)} %get-tuple-element.196.right_ref), custom_call_target="tpu_custom_call" | custom-call | flops 1811939328 | bytes 3932160 | tf_op jit(solution)/shard_map/grad_wide/pallas_call | solution.py:193
  375.1 29.6 %collective-permute-done.56 = bf16[96,768]{1,0:T(8,128)(2,1)} collective-permute-done((bf16[96,768]{1,0:T(8,128)(2,1)}, bf16[96,768]{1,0:T(8,128)(2,1)}, u32[]{:S(2)}, u32[]{:S(2)}) %collective-permute-start.56) | collective-permute-done | bytes 147488 | tf_op jit(solution)/shard_map/ppermute | solution.py:239
  (350 shorter events, 214.4 us)
Async XLA Ops:
  2.5 75.1 %collective-permute-start.2 = (bf16[24,3840]{1,0:T(8,128)(2,1)}, bf16[24,3840]{1,0:T(8,128)(2,1)S(1)}, u32[]{:S(2)}, u32[]{:S(2)}) collective-permute-start(bf16[24,3840]{1,0:T(8,128)(2,1)} %get-tuple-element.130), channel_id=1, source_target_pairs={{0,6},{1,7},{2,4},{3,5},{4,2},{5,3},{6,0},{7,1},{8,14},{9,15},{10,... | collective-permute-start | bytes 552968 | tf_op jit(solution)/shard_map/ppermute | solution.py:65
  7.6 70.5 %collective-permute-start.1 = (bf16[24,3840]{1,0:T(8,128)(2,1)}, bf16[24,3840]{1,0:T(8,128)(2,1)S(1)}, u32[]{:S(2)}, u32[]{:S(2)}) collective-permute-start(bf16[24,3840]{1,0:T(8,128)(2,1)} %get-tuple-element.130), channel_id=1, source_target_pairs={{0,4},{1,5},{2,6},{3,7},{4,0},{5,1},{6,2},{7,3},{8,12},{9,13},{10,... | collective-permute-start | bytes 552968 | tf_op jit(solution)/shard_map/ppermute | solution.py:65
  65.0 73.7 %all-to-all-start.1 = ((bf16[8,2,64,768]{3,2,1,0:T(8,128)(2,1)}), bf16[8,2,64,768]{3,2,1,0:T(8,128)(2,1)S(1)}, u32[]{:S(2)}, u32[]{:S(2)}) async-start(bf16[8,2,64,768]{3,2,1,0:T(8,128)(2,1)} %copy.77), calls=%async_computation.1 | async-start | bytes 3145728 | tf_op jit(solution)/shard_map/all_to_all | solution.py:491
  69.2 31.4 %collective-permute-start = (bf16[24,3840]{1,0:T(8,128)(2,1)S(1)}, bf16[24,3840]{1,0:T(8,128)(2,1)S(1)}, u32[]{:S(2)}, u32[]{:S(2)}) collective-permute-start(bf16[24,3840]{1,0:T(8,128)(2,1)S(1)} %copy-done.36), channel_id=1, source_target_pairs={{0,2},{1,3},{2,0},{3,1},{4,6},{5,7},{6,4},{7,5},{8,10},{9,11},{10,... | collective-permute-start | bytes 552968 | tf_op jit(solution)/shard_map/ppermute | solution.py:65
  78.1 28.3 %collective-permute-start.15 = (bf16[4,24,2304]{2,1,0:T(8,128)(2,1)}, bf16[4,24,2304]{2,1,0:T(8,128)(2,1)}, u32[]{:S(2)}, u32[]{:S(2)}) collective-permute-start(bf16[4,24,2304]{2,1,0:T(8,128)(2,1)} %collective-permute-done.11.refs_4_), channel_id=1, source_target_pairs={{0,8},{1,9},{2,10},{3,11},{4,12},{5,13},{6,14},{7,15},{8,0},{9,1},... | collective-permute-start | bytes 1327112 | tf_op jit(solution)/shard_map/ppermute | solution.py:65
  102.0 36.6 %collective-permute-start.16 = (bf16[4,24,3840]{2,1,0:T(8,128)(2,1)S(1)}, bf16[4,24,3840]{2,1,0:T(8,128)(2,1)}, u32[]{:S(2)}, u32[]{:S(2)}) collective-permute-start(bf16[4,24,3840]{2,1,0:T(8,128)(2,1)S(1)} %select_select_fusion.refs_1_), channel_id=1, source_target_pairs={{0,1},{1,0},{2,3},{3,2},{4,5},{5,4},{6,7},{7,6},{8,9},{9,8},{10,11... | collective-permute-start | bytes 2211848 | tf_op jit(solution)/shard_map/ppermute | solution.py:65
  102.1 36.5 %collective-permute-start.17 = (bf16[4,24,3840]{2,1,0:T(8,128)(2,1)S(1)}, bf16[4,24,3840]{2,1,0:T(8,128)(2,1)}, u32[]{:S(2)}, u32[]{:S(2)}) collective-permute-start(bf16[4,24,3840]{2,1,0:T(8,128)(2,1)S(1)} %select_select_fusion.refs_1_), channel_id=1, source_target_pairs={{0,16},{1,17},{2,18},{3,19},{4,20},{5,21},{6,22},{7,23},{8,24},{9,... | collective-permute-start | bytes 2211848 | tf_op jit(solution)/shard_map/ppermute | solution.py:65
  103.1 35.6 %collective-permute-start.18 = (bf16[4,24,3840]{2,1,0:T(8,128)(2,1)S(1)}, bf16[4,24,3840]{2,1,0:T(8,128)(2,1)}, u32[]{:S(2)}, u32[]{:S(2)}) collective-permute-start(bf16[4,24,3840]{2,1,0:T(8,128)(2,1)S(1)} %select_select_fusion.refs_1_), channel_id=1, source_target_pairs={{0,17},{1,16},{2,19},{3,18},{4,21},{5,20},{6,23},{7,22},{8,25},{9,... | collective-permute-start | bytes 2211848 | tf_op jit(solution)/shard_map/ppermute | solution.py:65
  105.6 42.1 %collective-permute-start.19 = (bf16[4,24,3840]{2,1,0:T(8,128)(2,1)S(1)}, bf16[4,24,3840]{2,1,0:T(8,128)(2,1)}, u32[]{:S(2)}, u32[]{:S(2)}) collective-permute-start(bf16[4,24,3840]{2,1,0:T(8,128)(2,1)S(1)} %select_select_fusion.refs_1_), channel_id=1, source_target_pairs={{0,8},{1,9},{2,10},{3,11},{4,12},{5,13},{6,14},{7,15},{8,0},{9,1},... | collective-permute-start | bytes 2211848 | tf_op jit(solution)/shard_map/ppermute | solution.py:65
  139.7 34.8 %collective-permute-start.23 = (bf16[4,96,768]{2,1,0:T(8,128)(2,1)S(1)}, bf16[4,96,768]{2,1,0:T(8,128)(2,1)S(1)}, u32[]{:S(2)}, u32[]{:S(2)}) collective-permute-start(bf16[4,96,768]{2,1,0:T(8,128)(2,1)S(1)} %select_select_fusion.1.refs_1_), channel_id=1, source_target_pairs={{0,1},{1,0},{2,3},{3,2},{4,5},{5,4},{6,7},{7,6},{8,9},{9,8},{10,11... | collective-permute-start | bytes 1769480 | tf_op jit(solution)/shard_map/ppermute | solution.py:65
  141.8 63.0 %all-to-all-start.2 = ((bf16[8,2,64,768]{3,2,1,0:T(8,128)(2,1)}), bf16[8,2,64,768]{3,2,1,0:T(8,128)(2,1)}, u32[]{:S(2)}, u32[]{:S(2)}) async-start(bf16[8,2,64,768]{3,2,1,0:T(8,128)(2,1)} %bitcast.14), calls=%async_computation.2 | async-start | bytes 3145728 | tf_op jit(solution)/shard_map/all_to_all | solution.py:498
  148.3 37.1 %collective-permute-start.25 = (bf16[4,96,768]{2,1,0:T(8,128)(2,1)S(1)}, bf16[4,96,768]{2,1,0:T(8,128)(2,1)}, u32[]{:S(2)}, u32[]{:S(2)}) collective-permute-start(bf16[4,96,768]{2,1,0:T(8,128)(2,1)S(1)} %select_select_fusion.1.refs_1_), channel_id=1, source_target_pairs={{0,17},{1,16},{2,19},{3,18},{4,21},{5,20},{6,23},{7,22},{8,25},{9,... | collective-permute-start | bytes 1769480 | tf_op jit(solution)/shard_map/ppermute | solution.py:65
  151.2 35.2 %collective-permute-start.26 = (bf16[4,96,768]{2,1,0:T(8,128)(2,1)S(1)}, bf16[4,96,768]{2,1,0:T(8,128)(2,1)}, u32[]{:S(2)}, u32[]{:S(2)}) collective-permute-start(bf16[4,96,768]{2,1,0:T(8,128)(2,1)S(1)} %select_select_fusion.1.refs_1_), channel_id=1, source_target_pairs={{0,8},{1,9},{2,10},{3,11},{4,12},{5,13},{6,14},{7,15},{8,0},{9,1},... | collective-permute-start | bytes 1769480 | tf_op jit(solution)/shard_map/ppermute | solution.py:65
  231.0 78.7 %all-to-all-start.3 = ((bf16[8,2,64,768]{3,2,1,0:T(8,128)(2,1)}), bf16[8,2,64,768]{3,2,1,0:T(8,128)(2,1)}, u32[]{:S(2)}, u32[]{:S(2)}) async-start(bf16[8,2,64,768]{3,2,1,0:T(8,128)(2,1)} %bitcast.75), calls=%async_computation.3 | async-start | bytes 3145728 | tf_op jit(solution)/shard_map/all_to_all | solution.py:491
  278.9 30.8 %collective-permute-start.32 = (bf16[4,96,768]{2,1,0:T(8,128)(2,1)}, bf16[4,96,768]{2,1,0:T(8,128)(2,1)}, u32[]{:S(2)}, u32[]{:S(2)}) collective-permute-start(bf16[4,96,768]{2,1,0:T(8,128)(2,1)} %get-tuple-element.181), channel_id=1, source_target_pairs={{0,1},{1,0},{2,3},{3,2},{4,5},{5,4},{6,7},{7,6},{8,9},{9,8},{10,11... | collective-permute-start | bytes 1769480 | tf_op jit(solution)/shard_map/ppermute | solution.py:239
  280.6 29.1 %collective-permute-start.33 = (bf16[4,96,768]{2,1,0:T(8,128)(2,1)}, bf16[4,96,768]{2,1,0:T(8,128)(2,1)}, u32[]{:S(2)}, u32[]{:S(2)}) collective-permute-start(bf16[4,96,768]{2,1,0:T(8,128)(2,1)} %get-tuple-element.182), channel_id=1, source_target_pairs={{0,16},{1,17},{2,18},{3,19},{4,20},{5,21},{6,22},{7,23},{8,24},{9,... | collective-permute-start | bytes 1769480 | tf_op jit(solution)/shard_map/ppermute | solution.py:239
  316.8 49.1 %collective-permute-start.38 = (bf16[2,192,1920]{2,1,0:T(8,128)(2,1)}, bf16[2,192,1920]{2,1,0:T(8,128)(2,1)S(1)}, u32[]{:S(2)}, u32[]{:S(2)}) collective-permute-start(bf16[2,192,1920]{2,1,0:T(8,128)(2,1)} %get-tuple-element.195), channel_id=1, source_target_pairs={{0,8},{1,9},{2,10},{3,11},{4,12},{5,13},{6,14},{7,15},{8,0},{9,1},... | collective-permute-start | bytes 4423688 | tf_op jit(solution)/shard_map/ppermute | solution.py:239
  322.8 38.9 %collective-permute-start.35 = (bf16[4,24,3072]{2,1,0:T(8,128)(2,1)}, bf16[4,24,3072]{2,1,0:T(8,128)(2,1)S(1)}, u32[]{:S(2)}, u32[]{:S(2)}) collective-permute-start(bf16[4,24,3072]{2,1,0:T(8,128)(2,1)} %get-tuple-element.190), channel_id=1, source_target_pairs={{0,1},{1,0},{2,3},{3,2},{4,5},{5,4},{6,7},{7,6},{8,9},{9,8},{10,11... | collective-permute-start | bytes 1769480 | tf_op jit(solution)/shard_map/ppermute | solution.py:239
  324.4 40.0 %collective-permute-start.36 = (bf16[4,24,3072]{2,1,0:T(8,128)(2,1)}, bf16[4,24,3072]{2,1,0:T(8,128)(2,1)S(1)}, u32[]{:S(2)}, u32[]{:S(2)}) collective-permute-start(bf16[4,24,3072]{2,1,0:T(8,128)(2,1)} %get-tuple-element.191), channel_id=1, source_target_pairs={{0,16},{1,17},{2,18},{3,19},{4,20},{5,21},{6,22},{7,23},{8,24},{9,... | collective-permute-start | bytes 1769480 | tf_op jit(solution)/shard_map/ppermute | solution.py:239
  325.6 40.4 %collective-permute-start.37 = (bf16[4,24,3072]{2,1,0:T(8,128)(2,1)}, bf16[4,24,3072]{2,1,0:T(8,128)(2,1)S(1)}, u32[]{:S(2)}, u32[]{:S(2)}) collective-permute-start(bf16[4,24,3072]{2,1,0:T(8,128)(2,1)} %get-tuple-element.192), channel_id=1, source_target_pairs={{0,17},{1,16},{2,19},{3,18},{4,21},{5,20},{6,23},{7,22},{8,25},{9,... | collective-permute-start | bytes 1769480 | tf_op jit(solution)/shard_map/ppermute | solution.py:239
  356.7 108.7 %all-to-all-start.4 = ((bf16[8,2,64,768]{3,2,1,0:T(8,128)(2,1)}), bf16[8,2,64,768]{3,2,1,0:T(8,128)(2,1)}, u32[]{:S(2)}, u32[]{:S(2)}) async-start(bf16[8,2,64,768]{3,2,1,0:T(8,128)(2,1)} %bitcast.22), calls=%async_computation.4 | async-start | bytes 3145728 | tf_op jit(solution)/shard_map/all_to_all | solution.py:498
  361.7 43.0 %collective-permute-start.56 = (bf16[96,768]{1,0:T(8,128)(2,1)}, bf16[96,768]{1,0:T(8,128)(2,1)}, u32[]{:S(2)}, u32[]{:S(2)}) collective-permute-start(bf16[96,768]{1,0:T(8,128)(2,1)} %get-tuple-element.241), channel_id=1, source_target_pairs={{0,4},{1,5},{2,6},{3,7},{4,0},{5,1},{6,2},{7,3},{8,12},{9,13},{10,... | collective-permute-start | bytes 442376 | tf_op jit(solution)/shard_map/ppermute | solution.py:239
  364.5 40.1 %collective-permute-start.55 = (bf16[96,768]{1,0:T(8,128)(2,1)}, bf16[96,768]{1,0:T(8,128)(2,1)}, u32[]{:S(2)}, u32[]{:S(2)}) collective-permute-start(bf16[96,768]{1,0:T(8,128)(2,1)} %get-tuple-element.240), channel_id=1, source_target_pairs={{0,2},{1,3},{2,0},{3,1},{4,6},{5,7},{6,4},{7,5},{8,10},{9,11},{10,... | collective-permute-start | bytes 442376 | tf_op jit(solution)/shard_map/ppermute | solution.py:239
  374.4 47.7 %collective-permute-start.39 = (bf16[2,192,1152]{2,1,0:T(8,128)(2,1)}, bf16[2,192,1152]{2,1,0:T(8,128)(2,1)S(1)}, u32[]{:S(2)}, u32[]{:S(2)}) collective-permute-start(bf16[2,192,1152]{2,1,0:T(8,128)(2,1)} %get-tuple-element.198), channel_id=1, source_target_pairs={{0,8},{1,9},{2,10},{3,11},{4,12},{5,13},{6,14},{7,15},{8,0},{9,1},... | collective-permute-start | bytes 2654216 | tf_op jit(solution)/shard_map/ppermute | solution.py:239
  (102 other events, 1485.3 us)

commit v3 on v2

--- a/solution.py
+++ b/solution.py
@@ -112,121 +112,150 @@
         return out.reshape(grid.total * rows, wide)
 
 
-def join_kernel(query_ref, key_ref, value_ref, out_ref, in_ref, first_ref, up_ref):
-    width = out_ref.shape[1]
+def join_kernel(query_ref, key_ref, value_ref, out_ref, in_ref, down_ref, first_ref, up_ref):
+    rows, width = out_ref.shape
     for pair in range(width // WIDE):
         for i, ref in enumerate((query_ref, key_ref, value_ref)):
             at = (pair * 3 + i) * WIDE
             first_ref[:, at : at + WIDE] = ref[:, pair * WIDE : (pair + 1) * WIDE]
-    up_ref[:, :width] = out_ref[...]
-    up_ref[:, width:] = in_ref[...]
-
-
-def join(w_query, w_key, w_value, w_out, w_in):
+    for i in range(down_ref.shape[0] // rows):
+        up_ref[:, i * width : (i + 1) * width] = down_ref[i * rows : (i + 1) * rows, :]
+    at = in_ref.shape[1]
+    up_ref[:, at : at + width] = out_ref[...]
+    up_ref[:, at + width :] = in_ref[...]
+
+
+def join(w_query, w_key, w_value, w_out, w_in, w_down):
     rows, width = w_query.shape
     return pl.pallas_call(
         join_kernel,
         out_shape=[
             jax.ShapeDtypeStruct((rows, 3 * width), bf16),
-            jax.ShapeDtypeStruct((rows, width + w_in.shape[1]), bf16),
+            jax.ShapeDtypeStruct((rows, width + 2 * w_in.shape[1]), bf16),
         ],
         name="join",
-    )(w_query, w_key, w_value, w_out, w_in)
-
-
-def grad_tall_kernel(spot, left_ref, right_ref, out_ref):
-    out_ref[0] = tn(left_ref[...], right_ref[...]).astype(bf16)
-
-
-def grad_tall(grid, left, right, other):
-    rows, tall = left.shape
-    wide = right.shape[1]
-    ny = grid.size["y"]
-    block = tall // (2 * ny)
+    )(w_query, w_key, w_value, w_out, w_in, w_down)
+
+
+def stack_kernel(wide_ref, out_ref):
+    count, rows, wide = wide_ref.shape
+    width = out_ref.shape[1]
+    folds = wide // width
+    for k in range(count):
+        for i in range(folds):
+            at = (k * folds + i) * rows
+            out_ref[at : at + rows, :] = wide_ref[k, :, i * width : (i + 1) * width]
+
+
+def stack(gathered, total, width):
+    rows = gathered.shape[0] // total
+    wide = (gathered.shape[1] - width) // 2
+    folds = wide // width
+    count = 4
     return pl.pallas_call(
-        grad_tall_kernel,
-        grid_spec=pltpu.PrefetchScalarGridSpec(
-            num_scalar_prefetch=1,
-            grid=(ny,),
-            in_specs=[
-                pl.BlockSpec((rows, block), lambda y, spot: (0, y * 2 + (spot[1] ^ other))),
-                pl.BlockSpec((rows, wide), lambda y, _: (0, 0)),
-            ],
-            out_specs=pl.BlockSpec((1, block, wide), lambda y, _: (y, 0, 0)),
+        stack_kernel,
+        grid=(total // count,),
+        in_specs=[pl.BlockSpec((count, rows, wide), lambda i: (i, 0, 0))],
+        out_specs=pl.BlockSpec((count * folds * rows, width), lambda i: (i, 0)),
+        out_shape=jax.ShapeDtypeStruct((total * folds * rows, width), bf16),
+        cost_estimate=pl.CostEstimate(
+            flops=0, bytes_accessed=4 * total * rows * wide, transcendentals=0
         ),
-        out_shape=jax.ShapeDtypeStruct((ny, block, wide), bf16),
+        name="stack",
+    )(gathered.reshape(total, rows, -1))
+
+
+STRIP = 512
+SLAB = 384
+
+
+def grad_down_kernel(left_ref, right_ref, out_ref, *, rows):
+    total = tn(left_ref[...], right_ref[...]).astype(bf16)
+    tall, width = total.shape
+    folds = out_ref.shape[1] // width
+    for k in range(tall // rows):
+        at = k // folds * rows
+        fold = k % folds
+        out_ref[at : at + rows, fold * width : (fold + 1) * width] = total[k * rows : (k + 1) * rows]
+
+
+def grad_down(grid, left, right):
+    count, tall = left.shape
+    width = right.shape[1]
+    rows = width // grid.total
+    return pl.pallas_call(
+        lambda *refs: grad_down_kernel(*refs, rows=rows),
+        grid=(tall // SLAB,),
+        in_specs=[
+            pl.BlockSpec((count, SLAB), lambda i: (0, i)),
+            pl.BlockSpec((count, width), lambda i: (0, 0)),
+        ],
+        out_specs=pl.BlockSpec((SLAB * width // tall, tall), lambda i: (i, 0)),
+        out_shape=jax.ShapeDtypeStruct((width, 2 * tall), bf16),
         cost_estimate=pl.CostEstimate(
-            flops=rows * tall * wide * 2, bytes_accessed=rows * tall * 2, transcendentals=0
+            flops=0, bytes_accessed=4 * width, transcendentals=0
         ),
-        name="grad_tall",
-    )(grid.spot(), left, right)
-
-
-STRIP = 384
-
-
-def grad_wide_kernel(spot, left_ref, right_ref, *refs):
-    own_ref, other_ref, turned, total = refs[-4:]
-
+        name="grad_down",
+    )(left, right)
+
+
+def grad_up_kernel(left_ref, right_ref, _, out_ref, turned):
     @pl.when(pl.program_id(0) == 0)
     def _():
         turned[...] = left_ref[...].T
 
-    total[...] = jnp.dot(turned[...], right_ref[...], preferred_element_type=f32)
-    ny, block = own_ref.shape[:2]
-    core = spot[1]
-    for y in range(ny):
-        at = pl.multiple_of((2 * y + core) * block, 16)
-        own_ref[y] = total[pl.ds(at, block), :].astype(bf16)
-        at = pl.multiple_of((2 * y + 1 - core) * block, 16)
-        other_ref[y] = total[pl.ds(at, block), :].astype(bf16)
-
-
-def grad_wide(grid, left, right, wide=None, first=0, base=None):
+    out_ref[...] = jnp.dot(turned[...], right_ref[...], preferred_element_type=f32).astype(bf16)
+
+
+def grad_up(left, right, base):
     rows, tall = left.shape
-    wide = wide or right.shape[1]
-    ny = grid.size["y"]
-    block = tall // (2 * ny)
-    at = first // STRIP
-    made = pl.BlockSpec((ny, block, STRIP), lambda j, _: (0, 0, j + at))
-    given = () if base is None else tuple(base)
+    wide = right.shape[1]
+    at = wide // STRIP
     return pl.pallas_call(
-        grad_wide_kernel,
-        grid_spec=pltpu.PrefetchScalarGridSpec(
-            num_scalar_prefetch=1,
-            grid=(right.shape[1] // STRIP,),
-            in_specs=[
-                pl.BlockSpec((rows, tall), lambda j, _: (0, 0)),
-                pl.BlockSpec((rows, STRIP), lambda j, _: (0, j)),
-            ]
-            + [pl.BlockSpec(memory_space=pl.ANY)] * len(given),
-            out_specs=[made, made],
-            scratch_shapes=[pltpu.VMEM((tall, rows), bf16), pltpu.VMEM((tall, STRIP), f32)],
+        grad_up_kernel,
+        grid=(wide // STRIP,),
+        in_specs=[
+            pl.BlockSpec((rows, tall), lambda j: (0, 0)),
+            pl.BlockSpec((rows, STRIP), lambda j: (0, j)),
+            pl.BlockSpec(memory_space=pl.ANY),
+        ],
+        out_specs=pl.BlockSpec((tall, STRIP), lambda j: (0, j + at)),
+        scratch_shapes=[pltpu.VMEM((tall, rows), bf16)],
+        out_shape=jax.ShapeDtypeStruct(base.shape, bf16),
+        input_output_aliases={2: 0},
+        cost_estimate=pl.CostEstimate(
+            flops=0, bytes_accessed=4 * wide, transcendentals=0
         ),
-        out_shape=[jax.ShapeDtypeStruct((ny, block, wide), bf16)] * 2,
-        input_output_aliases={3: 0, 4: 1} if given else {},
-        cost_estimate=pl.CostEstimate(
-            flops=rows * tall * right.shape[1] * 2,
-            bytes_accessed=2 * rows * (tall + right.shape[1]),
-            transcendentals=0,
-        ),
-        name="grad_wide",
-    )(grid.spot(), left, right, *given)
-
-
-def fold_plane_kernel(spot, own_ref, got_ref, *outs, keys):
+        name="grad_up",
+    )(left, right, base)
+
+
+def fold_plane_kernel(spot, *refs, keys, widths):
+    count = len(widths)
+    owns, gots, outs = refs[:count], refs[count : 2 * count], refs[2 * count :]
     for out, (y, x) in zip(outs, keys):
         at = (spot[0] ^ y, 0, spot[3] ^ x)
-        out[0] = (own_ref[at].astype(f32) + got_ref[at].astype(f32)).astype(bf16)
-
-
-def fold_line_kernel(spot, *refs):
-    parts, outs = refs[:-LINE], refs[-LINE:]
+        left = 0
+        for own, got, wide in zip(owns, gots, widths):
+            out[0, :, left : left + wide] = (
+                own[at].astype(f32) + got[at].astype(f32)
+            ).astype(bf16)
+            left += wide
+
+
+def fold_line_kernel(spot, *refs, counts):
+    outs = refs[-LINE:]
     for step, out in enumerate(outs):
-        total = parts[0][spot[2] ^ step].astype(f32)
-        for part in parts[1:]:
-            total = total + part[spot[2] ^ step].astype(f32)
-        out[...] = total.astype(bf16)
+        at = left = 0
+        for count in counts:
+            parts = refs[at : at + count]
+            total = parts[0][spot[2] ^ step].astype(f32)
+            for part in parts[1:]:
+                total = total + part[spot[2] ^ step].astype(f32)
+            wide = total.shape[1]
+            out[:, left : left + wide] = total.astype(bf16)
+            at += count
+            left += wide
 
 
 class Scatter:
@@ -238,43 +267,50 @@
         mask = sum(grid.stride[axis] * step for axis, step in steps.items())
         return lax.ppermute(array, BOTH, [(k, k ^ mask) for k in range(grid.total)])
 
-    def send_core(self, other):
-        return self.fetch(other, core=1)
-
-    def send_plane(self, own, got):
+    def send_core(self, others):
+        return [self.fetch(other, core=1) for other in others]
+
+    def send_plane(self, owns, gots):
         grid = self.grid
-        ny, block, wide = own.shape
-        nx = grid.size["x"]
-        rows = block // (LINE * nx)
-        shape = (ny, LINE, nx, rows, wide)
+        ny, nx = grid.size["y"], grid.size["x"]
+        rows = owns[0].shape[0] // (ny * LINE * nx)
+        widths = [own.shape[1] for own in owns]
+        wide = sum(widths)
         keys = [(y, x) for y in range(ny) for x in range(nx)]
-        whole = pl.BlockSpec((ny, 1, nx, rows, wide), lambda i, _: (0, i, 0, 0, 0))
+        blocks = [
+            pl.BlockSpec((ny, 1, nx, rows, one), lambda i, _: (0, i, 0, 0, 0)) for one in widths
+        ]
         parts = pl.pallas_call(
-            lambda *refs: fold_plane_kernel(*refs, keys=keys),
+            lambda *refs: fold_plane_kernel(*refs, keys=keys, widths=widths),
             grid_spec=pltpu.PrefetchScalarGridSpec(
                 num_scalar_prefetch=1,
                 grid=(LINE,),
-                in_specs=[whole, whole],
+                in_specs=blocks + blocks,
                 out_specs=[pl.BlockSpec((1, rows, wide), lambda i, _: (i, 0, 0))] * len(keys),
             ),
             out_shape=[jax.ShapeDtypeStruct((LINE, rows, wide), bf16)] * len(keys),
             cost_estimate=pl.CostEstimate(
-                flops=0, bytes_accessed=6 * ny * block * wide, transcendentals=0
+                flops=0, bytes_accessed=6 * owns[0].shape[0] * wide, transcendentals=0
             ),
             name="fold_plane",
-        )(grid.spot(), own.reshape(shape), got.reshape(shape))
-        self.own = parts[0]
-        return [self.fetch(part, y=y, x=x) for part, (y, x) in zip(parts[1:], keys[1:])]
-
-    def send_line(self, got):
-        rows, wide = self.own.shape[1:]
+        )(grid.spot(), *[one.reshape(ny, LINE, nx, rows, -1) for one in (*owns, *gots)])
+        return [parts[0]] + [self.fetch(part, y=y, x=x) for part, (y, x) in zip(parts[1:], keys[1:])]
+
+    def send_line(self, groups):
+        rows = groups[0][0].shape[1]
+        widths = [group[0].shape[2] for group in groups]
+        wide = sum(widths)
+        counts = [len(group) for group in groups]
         parts = pl.pallas_call(
-            fold_line_kernel,
+            lambda *refs: fold_line_kernel(*refs, counts=counts),
             grid_spec=pltpu.PrefetchScalarGridSpec(
                 num_scalar_prefetch=1,
                 grid=(1,),
-                in_specs=[pl.BlockSpec((LINE, rows, wide), lambda i, _: (0, 0, 0))]
-                * (1 + len(got)),
+                in_specs=[
+                    pl.BlockSpec((LINE, rows, one), lambda i, _: (0, 0, 0))
+                    for one, count in zip(widths, counts)
+                    for _ in range(count)
+                ],
                 out_specs=[pl.BlockSpec((rows, wide), lambda i, _: (0, 0))] * LINE,
             ),
             out_shape=[jax.ShapeDtypeStruct((rows, wide), bf16)] * LINE,
@@ -282,22 +318,31 @@
                 flops=0, bytes_accessed=8 * LINE * rows * wide, transcendentals=0
             ),
             name="fold_line",
-        )(self.grid.spot(), self.own, *got)
-        self.own = parts[0]
-        return [
+        )(self.grid.spot(), *[part for group in groups for part in group])
+        return [parts[0]] + [
             self.fetch(part, zl=step & 1, zh=step >> 1)
             for step, part in zip(range(1, LINE), parts[1:])
         ]
 
-    def finish(self, got):
-        total = self.own.astype(f32)
-        for one in got:
+    def finish(self, parts):
+        total = parts[0].astype(f32)
+        for one in parts[1:]:
             total = total + one.astype(f32)
         return total
 
 
-def tie(values, after):
-    return lax.optimization_barrier((values, after))
+def turn(grid, array):
+    rows, tall = array.shape
+    turned = array.T.reshape(grid.size["y"], 2, -1, rows)
+    core = grid.place("core")
+    return [
+        lax.dynamic_index_in_dim(turned, at, 1, keepdims=False).reshape(-1, rows)
+        for at in (core, 1 - core)
+    ]
+
+
+def gate(*values):
+    return lax.optimization_barrier(values)
 
 
 def standardize(values):
@@ -536,72 +581,64 @@
     )
 
     singles = (b_query, b_value, b_out, gain_one, shift_one, b_in, b_down, gain_two, shift_two)
-    own, up_own = join(w_query, w_key, w_value, w_out, w_in)
+    own, up_own = join(w_query, w_key, w_value, w_out, w_in, w_down)
     first = Gather(grid, own)
-    up_weights = Gather(grid, up_own)
-    down_weights = Gather(grid, w_down)
-
     got = first.send_line()
-    got_up = up_weights.send_line()
-    got_down = down_weights.send_line()
+    up_whole = lax.all_gather(up_own, BOTH, axis=0, tiled=True)
+    small = jnp.concatenate(singles)
+    small = jnp.broadcast_to(small[None, :], (grid.total, small.shape[0]))
+    cut = pieces_out(cotangent, lax.axis_size("fsdp"))
+
+    got, small, cut = gate(got, small, cut)
     first.take_line(got)
     got = first.send_plane()
-    singles, first.held = tie(singles, first.held)
-    small = jnp.concatenate(singles)
-    small = lax.all_to_all(
-        jnp.broadcast_to(small[None, :], (grid.total, small.shape[0])), BOTH, 0, 0, tiled=True
-    )
-    (cotangent, got), _ = tie((cotangent, got), ())
+    small = lax.all_to_all(small, BOTH, 0, 0, tiled=True)
+
+    tokens_own, tokens_other = turn(grid, tokens.reshape(slots * rows, width))
+    got, small, tokens_own, tokens_other = gate(got, small, tokens_own, tokens_other)
     first.take_plane(got)
-    up_weights.take_line(got_up)
-    down_weights.take_line(got_down)
-    (up_weights.held, down_weights.held), _ = tie(
-        (up_weights.held, down_weights.held), got
-    )
     got = first.send_core()
-    got_up = up_weights.send_plane()
-    up_spread = spread_out(cotangent)
-    qkv = first.whole(got)
-
+    up_spread = lax.all_to_all(cut, "fsdp", 0, 0, tiled=True)
     vectors = []
     at = 0
     for one in singles:
         vectors.append(small[:, at : at + one.shape[0]].reshape(-1).astype(f32))
         at += one.shape[0]
     bq, bv, bo, g1, s1, bi, bd, g2, s2 = vectors
+    bias = interleave(bq[None], jnp.zeros_like(bq)[None], bv[None])
+
+    got, bias, tokens = gate(got, bias, tokens)
+    qkv = first.whole(got)
 
     total_rows = slots * rows
     inputs = tokens.reshape(total_rows, width)
     valid = jnp.arange(rows)[None, :] < my_lengths[:, None]
     valid_row = valid.reshape(total_rows)[:, None]
 
-    bias = interleave(bq[None], jnp.zeros_like(bq)[None], bv[None])
     fused = (matmul(inputs, qkv) + bias).astype(bf16)
-    (down_weights.held, fused) = lax.optimization_barrier((down_weights.held, fused))
-    got_down = down_weights.send_plane()
-    halves = []
-    for slot in range(slots):
+    halves = [attend(fused, my_lengths, slots, 0, 1)]
+    for slot in range(1, slots):
         halves.append(attend(fused, my_lengths, slots, slot, 1))
-        (fused, halves), _ = tie((fused, halves), ())
-    (halves, up_spread), got_up = tie((halves, up_spread), got_up)
-    up_weights.take_plane(got_up)
-    got_up = up_weights.send_core()
-    upstream = bring_in(up_spread, deal_row)
+    halves, up_spread = gate(halves, up_spread)
     context = jnp.concatenate([half[0] for half in halves], axis=0)
     totals = jnp.concatenate([half[1] for half in halves], axis=0)
-    up_whole = up_weights.whole(got_up)
-    wo, wi = up_whole[:, :width], up_whole[:, width:]
+    context_own, context_other = turn(grid, context)
+    upstream = bring_in(up_spread, deal_row)
+    context, context_own, context_other, up_whole = gate(
+        context, context_own, context_other, up_whole
+    )
+    tall = w_in.shape[1]
+    wo, wi = up_whole[:, tall : tall + width], up_whole[:, tall + width :]
+    wd = stack(up_whole, grid.total, width)
 
     middle_norm, middle_spread = standardize(inputs.astype(f32) + matmul(context, wo) + bo)
     middle = middle_norm * g1 + s1
     middle_low = middle.astype(bf16)
     hidden = matmul(middle_low, wi) + bi
     active = gelu_value(hidden).astype(bf16)
-    active, got_down = tie(active, got_down)
-    down_weights.take_plane(got_down)
-    wd = down_weights.whole(down_weights.send_core())
     final_norm, final_spread = standardize(middle + matmul(active, wd) + bd)
     output = jnp.where(valid_row, final_norm * g2 + s2, 0.0).astype(bf16)
+    output, upstream = gate(output, upstream)
 
     upstream = joined(upstream).reshape(total_rows, width).astype(f32)
     d_result = jnp.where(valid_row, upstream, 0.0)
@@ -611,58 +648,61 @@
     d_branch = d_final.astype(bf16)
     grad_bd = jnp.sum(d_branch.astype(f32), axis=0)
 
-    plane, line = ("y", "x"), ("zh", "zl")
-    sum_down, sum_up, sum_first, sum_second = (Scatter(grid) for _ in range(4))
-    other = grad_tall(grid, active, d_branch, 1)
-    got_down = sum_down.send_core(other)
-    own_down = grad_tall(grid, active, d_branch, 0)
-    output, d_branch = tie(output, d_branch)
+    scatter = Scatter(grid)
     out_spread = spread_out(output.reshape(slots, rows, width))
+    d_branch, grad_g2, grad_s2, grad_bd = gate(d_branch, grad_g2, grad_s2, grad_bd)
     d_hidden = (right_times(d_branch, wd) * gelu_slope(hidden)).astype(bf16)
     grad_bi = jnp.sum(d_hidden.astype(f32), axis=0)
-    d_hidden, got_down = tie(d_hidden, got_down)
-    got_down = sum_down.send_plane(own_down, got_down)
-    own_up, other = grad_wide(grid, middle_low, d_hidden)
-    got_up = sum_up.send_core(other)
+    d_hidden, d_branch = gate(d_hidden, d_branch)
+    outer = grad_up(middle_low, d_hidden, grad_down(grid, active, d_branch))
+    outer, d_hidden, grad_bi, out_spread = gate(outer, d_hidden, grad_bi, out_spread)
+    out_pieces = bring_in(out_spread, inverse)
+    shard_outer = lax.psum_scatter(outer, BOTH, scatter_dimension=0, tiled=True)
     d_middle = d_final + right_times(d_hidden, wi)
     grad_g1 = jnp.sum(d_middle * middle_norm, axis=0)
     grad_s1 = jnp.sum(d_middle, axis=0)
     d_sum = norm_back(d_middle * g1, middle_norm, middle_spread)
     d_attended = d_sum.astype(bf16)
     grad_bo = jnp.sum(d_attended.astype(f32), axis=0)
-    d_attended, got_up = tie(d_attended, got_up)
-    got_up = sum_up.send_plane(own_up, got_up)
     half = pairs // 2
-    wide = width + half * 3 * WIDE
-    begun = grad_wide(grid, context, d_attended, wide)
     d_context = right_times(d_attended, wo).astype(bf16)
     d_first, sums_first = attend_back(fused, totals, d_context, my_lengths, slots, 0, half)
-    (d_first, d_context, out_spread), got_down = tie((d_first, d_context, out_spread), got_down)
-    got_down = sum_down.send_line(got_down)
-    out_pieces = bring_in(out_spread, inverse)
-    own_first, other = grad_wide(grid, inputs, d_first, wide, width, begun)
-    got_first = sum_first.send_core(other)
+    others = [
+        matmul(context_other, d_attended).astype(bf16),
+        matmul(tokens_other, d_first).astype(bf16),
+    ]
+    others, d_context, d_attended, d_first = gate(others, d_context, d_attended, d_first)
+    got_first = scatter.send_core(others)
+    own_first = [
+        matmul(context_own, d_attended).astype(bf16),
+        matmul(tokens_own, d_first).astype(bf16),
+    ]
+    own_first, got_first, d_context, out_pieces = gate(own_first, got_first, d_context, out_pieces)
+    got_first = scatter.send_plane(own_first, got_first)
+    d_context, got_first[0] = gate(d_context, got_first[0])
     d_second, sums_second = attend_back(
         fused, totals, d_context, my_lengths, slots, half, pairs - half
     )
-    (d_second, d_sum), (got_up, got_first) = tie((d_second, d_sum), (got_up, got_first))
-    got_first = sum_first.send_plane(own_first, got_first)
-    own_second, other = grad_wide(grid, inputs, d_second)
-    got_second = sum_second.send_core(other)
-    got_up = sum_up.send_line(got_up)
-    d_fused = jnp.concatenate([d_first, d_second], axis=1)
-    (d_fused, d_sum), got_second = tie((d_fused, d_sum), got_second)
-    got_second = sum_second.send_plane(own_second, got_second)
-    input_grad = (d_sum + right_times(d_fused, qkv)).astype(bf16).reshape(slots, rows, width)
-    input_grad, got_first = tie(input_grad, got_first)
-    got_first = sum_first.send_line(got_first)
-    got_second = sum_second.send_line(got_second)
-    shard_first = sum_first.finish(got_first)
-    shard_second = sum_second.finish(got_second)
+    other = matmul(tokens_other, d_second).astype(bf16)
+    partial = d_sum + right_times(d_first, qkv[:, : half * 3 * WIDE])
+    other, d_second, sums_second, partial, got_first = gate(
+        other, d_second, sums_second, partial, got_first
+    )
+    got_second = scatter.send_core([other])
+    own_second = matmul(tokens_own, d_second).astype(bf16)
+    own_second, d_second, got_second = gate(own_second, d_second, got_second)
+    got_second = scatter.send_plane([own_second], got_second)
+    got_second[0], d_second, sums_second = gate(got_second[0], d_second, sums_second)
+    input_grad = partial + right_times(d_second, qkv[:, half * 3 * WIDE :])
+    input_grad = input_grad.astype(bf16).reshape(slots, rows, width)
+    sums = jnp.sum(jnp.concatenate([sums_first, sums_second], axis=-1), axis=0)
+    input_grad, got_second, got_first = gate(input_grad, got_second, got_first)
+    got = scatter.send_line([got_first, got_second])
+    shard = scatter.finish(got)
     layer_out = joined(out_pieces)
-    shard_qkv = jnp.concatenate([shard_first[:, width:], shard_second], axis=1).reshape(-1, pairs, 3, WIDE)
+    shard_qkv = shard[:, width:].reshape(-1, pairs, 3, WIDE)
+    shard_down = shard_outer[:, :tall].reshape(shard_outer.shape[0], -1, width).transpose(1, 0, 2)
     shard_q, shard_k, shard_v = (shard_qkv[:, :, i].reshape(-1, width) for i in range(3))
-    sums = jnp.sum(jnp.concatenate([sums_first, sums_second], axis=-1), axis=0)
 
     grads = (sums[0], sums[1], grad_bo, grad_g1, grad_s1, grad_bi, grad_bd, grad_g2, grad_s2)
     small = jnp.concatenate([one.reshape(grid.total, -1) for one in grads], axis=1)
@@ -681,13 +721,13 @@
         shard_k,
         shard_v,
         pbv,
-        shard_first[:, :width],
+        shard[:, :width],
         pbo,
         pg1,
         ps1,
-        sum_up.finish(got_up),
+        shard_outer[:, tall:].astype(f32),
         pbi,
-        sum_down.finish(got_down),
+        shard_down.astype(f32).reshape(-1, width),
         pbd,
         pg2,
         ps2,

time: 477 us -> 401 us (0.84)
  Pallas kernels: 142 us -> 93.1 us
  starting transfers between devices: 94.3 us -> 53.1 us
  waiting for transfers between devices: 96.7 us -> 75.3 us
  matrix products: 64.9 us -> 83.1 us
  local copies, waits for them, and re-layouts: 33.7 us -> 47.2 us
  between operations: 2.13 us -> 15.2 us
  other arithmetic: 34.8 us -> 25.8 us
    ppermute x58 -> x22, starting transfers between devices: 66.1 us -> 22.2 us  [fetch(): return lax.ppermute(array, BOTH, [(k, k ^ mask) for k in range(grid.total)])]
    pallas_call x14 -> x6, Pallas kernels: 77.8 us -> 40.2 us  [the longest x1 10.9 us: grad_down(): pl.pallas_call(lambda *refs: grad_down_kernel(*refs, rows=rows), grid=(ta...]
    ppermute x58 -> x22, waiting for transfers between devices: 90.3 us -> 58.6 us  [fetch(): return lax.ppermute(array, BOTH, [(k, k ^ mask) for k in range(grid.total)])]
    dot_general x4 -> x10, matrix products: 30.9 us -> 46.2 us  [matmul(): return jnp.dot(left, right, preferred_element_type=f32)]
    pallas_call x3 -> x1, Pallas kernels: 17.2 us -> 5.29 us  [whole(): pl.pallas_call(lambda *refs: place_kernel(*refs, keys=keys), grid_spec=pl...]
    reduce_scatter x0 -> x1, waiting for transfers between devices: none -> 8.74 us  [per_device(): shard_outer = lax.psum_scatter(outer, BOTH, scatter_dimension=0, tiled=True)]
    reshape x7, local copies, waits for them, and re-layouts: 0.55 us -> 6.85 us  [per_device(): one.reshape(grid.total, -1)]
    unnamed x132 -> x82, local copies, waits for them, and re-layouts: 10.4 us -> 6.84 us
  transfers between devices with their start and end apart: 64 -> 30, of which waited for: 13 -> 14; matrix products, arithmetic and copies ran while one was open for 24% -> 35% of each run, Pallas kernels for 26% -> 23%
where the time goes in v3:
time: 401 us; the launch traced here: 393 us
  Pallas kernels  93.1 us (23%)
  matrix products  83.1 us (21%)
  waiting for transfers between devices  75.3 us (19%)
  starting transfers between devices  53.1 us (13%)
  local copies, waits for them, and re-layouts  47.2 us (12%)
  other arithmetic  25.8 us (6%)
  between operations  15.2 us (4%)
    ppermute x22, waiting for transfers between devices, fetch(): return lax.ppermute(array, BOTH, [(k, k ^ mask) for k in range(grid.total)])  58.6 us
    dot_general x10, matrix products, matmul(): return jnp.dot(left, right, preferred_element_type=f32)  46.2 us
    dot_general x5, matrix products, right_times(): return jnp.einsum('to,io->ti', grads, weight, preferred_element_type=f32)  37 us
    pallas_call x2, Pallas kernels, attend_back(): pl.pallas_call(attend_back_kernel, grid_spec=pltpu.PrefetchScalarGridSpec...  27.1 us
    ppermute x22, starting transfers between devices, fetch(): return lax.ppermute(array, BOTH, [(k, k ^ mask) for k in range(grid.total)])  22.2 us
    pallas_call x2, Pallas kernels, attend(): pl.pallas_call(lambda *refs: attend_kernel(*refs, first=first), grid_spec...  18.5 us
    pallas_call x1, Pallas kernels, grad_down(): pl.pallas_call(lambda *refs: grad_down_kernel(*refs, rows=rows), grid=(ta...  10.9 us
    pallas_call x1, Pallas kernels, grad_up(): pl.pallas_call(grad_up_kernel, grid=(wide // STRIP,), in_specs=[pl.BlockS...  10.3 us
  transfers between devices with their start and end apart: 30, of which 14 were waited for; matrix products, arithmetic and copies ran while one was open for 35% of the time, Pallas kernels for 23%

profile of v3, /device:TPU:0, one launch (start us, length us, event | category | flops | bytes accessed | tf_op | source)
XLA Modules:
  0.0 392.9 jit_solution(15605297630779098206)
XLA Ops:
  14.9 6.1 %concatenate.15 = bf16[288]{0:T(512)(128)(2,1)S(1)} concatenate(bf16[24]{0:T(256)(128)(2,1)} %param.24, bf16[24]{0:T(256)(128)(2,1)} %param.27, bf16[24]{0:T(256)(128)(2,1)} %param.29, bf16[24]{0:T(256)(128)(2,1)} %param.30, bf16[24]{0:T(256)(128)(2,1)} %param.31, bf16[96]{0:T(256)(128)(2,1)} %param.33, bf16[24]{0:T(256)(128)(2,1)} %param.35, bf16[24]{0:T(256)(128)(2,1)} %param.36, ...), dimensions={0} | concatenate | bytes 1152 | tf_op jit(solution)/shard_map/concatenate | solution.py:588
  25.8 5.2 %all-to-all-start = ((bf16[32,2,144]{2,1,0:T(2,128)(2,1)}), bf16[32,2,144]{2,1,0:T(2,128)(2,1)S(1)}, u32[]{:S(2)}, u32[]{:S(2)}) async-start(bf16[32,2,144]{2,1,0:T(2,128)(2,1)} %reshape.397), calls=%async_computation | async-start | bytes 65536 | tf_op jit(solution)/shard_map/all_to_all | solution.py:595
  49.2 29.9 %collective-permute-done.4.refs_2_ = bf16[4,24,2304]{2,1,0:T(8,128)(2,1)} collective-permute-done((bf16[4,24,2304]{2,1,0:T(8,128)(2,1)}, bf16[4,24,2304]{2,1,0:T(8,128)(2,1)}, u32[]{:S(2)}, u32[]{:S(2)}) %collective-permute-start.4) | collective-permute-done | bytes 442400 | tf_op jit(solution)/shard_map/ppermute | solution.py:65
  79.1 10.4 %collective-permute-done.6.refs_4_ = bf16[4,24,2304]{2,1,0:T(8,128)(2,1)} collective-permute-done((bf16[4,24,2304]{2,1,0:T(8,128)(2,1)}, bf16[4,24,2304]{2,1,0:T(8,128)(2,1)}, u32[]{:S(2)}, u32[]{:S(2)}) %collective-permute-start.6) | collective-permute-done | bytes 442400 | tf_op jit(solution)/shard_map/ppermute | solution.py:65
  94.3 5.3 %place.1 = bf16[2,2,4,2,24,2304]{5,4,3,2,1,0:T(8,128)(2,1)} custom-call(s32[4]{0:T(128)} %pad_add_fusion.refs_0_, bf16[4,24,2304]{2,1,0:T(8,128)(2,1)} %select_select_fusion.refs_1_, bf16[4,24,2304]{2,1,0:T(8,128)(2,1)} %collective-permute-done.4.refs_2_, bf16[4,24,2304]{2,1,0:T(8,128)(2,1)} %collective-permute-done.5.refs_3_, ...), custom_call_target="tpu_custom_call" | custom-call | bytes 7077888 | tf_op jit(solution)/shard_map/place/pallas_call | solution.py:96
  99.6 7.5 %add_convert_fusion.refs_1_.fused_ref = bf16[1024,2304]{1,0:T(8,128)(2,1)} fusion(bf16[1024,768]{1,0:T(8,128)(2,1)S(1)} %bitcast.115, bf16[768,2304]{1,0:T(8,128)(2,1)} %bitcast.108, f32[2304]{0:T(1024)S(1)} %reduce.3), kind=kOutput, calls=%fused_computation.12 | convolution fusion | flops 3628597248 | bytes 9839616 | tf_op jit(solution)/shard_map/dot_general | solution.py:374
  107.1 9.2 %attend.2 = (bf16[512,768]{1,0:T(8,128)(2,1)}, f32[1,6,2,512]{3,2,1,0:T(2,128)}) custom-call(s32[2]{0:T(128)} %copy-done.33, bf16[1024,2304]{1,0:T(8,128)(2,1)} %add_convert_fusion.refs_1_.fused_ref), custom_call_target="tpu_custom_call" | custom-call | flops 3221225472 | bytes 3145728 | tf_op jit(solution)/shard_map/attend/pallas_call | solution.py:434
  116.3 9.4 %attend.3 = (bf16[512,768]{1,0:T(8,128)(2,1)}, f32[1,6,2,512]{3,2,1,0:T(2,128)}) custom-call(s32[2]{0:T(128)} %copy-done.33, bf16[1024,2304]{1,0:T(8,128)(2,1)} %add_convert_fusion.refs_1_.fused_ref), custom_call_target="tpu_custom_call" | custom-call | flops 3221225472 | bytes 3145728 | tf_op jit(solution)/shard_map/attend/pallas_call | solution.py:434
  131.6 4.7 %all-to-all-start.2 = ((bf16[8,2,64,768]{3,2,1,0:T(8,128)(2,1)}), bf16[8,2,64,768]{3,2,1,0:T(8,128)(2,1)}, u32[]{:S(2)}, u32[]{:S(2)}) async-start(bf16[8,2,64,768]{3,2,1,0:T(8,128)(2,1)} %bitcast.105), calls=%async_computation.2 | async-start | bytes 3145728 | tf_op jit(solution)/shard_map/all_to_all | solution.py:543
  143.1 11.5 %multiply_convert_fusion = (bf16[1024,3072]{1,0:T(8,128)(2,1)}, f32[1024,3072]{1,0:T(8,128)}) fusion(f32[3072]{0:T(1024)S(1)} %reshape.361, bf16[1024,768]{1,0:T(8,128)(2,1)S(1)} %fusion.11.left_ref, bf16[768,6912]{1,0:T(8,128)(2,1)} %all-gather.2.cloned.1.call-done), kind=kOutput, calls=%fused_computation.10 | convolution fusion | flops 4850712576 | bytes 25178112 | tf_op jit(solution)/shard_map/dot_general | solution.py:374
  154.6 6.8 %stack.19 = bf16[3072,768]{1,0:T(8,128)(2,1)} custom-call(bf16[32,24,6912]{2,1,0:T(8,128)(2,1)} %bitcast.100), custom_call_target="tpu_custom_call" | custom-call | bytes 9437184 | tf_op jit(solution)/shard_map/stack/pallas_call | solution.py:155
  161.5 9.3 %fusion.30 = (f32[1024]{0:T(1024)S(1)}, f32[1024,768]{1,0:T(8,128)S(1)}) fusion(f32[768]{0:T(1024)S(1)} %reshape.362, bf16[1024,3072]{1,0:T(8,128)(2,1)} %get-tuple-element.252.refs_0_, bf16[3072,768]{1,0:T(8,128)(2,1)} %stack.19, f32[768]{0:T(1024)S(1)} %reshape.360, f32[768]{0:T(1024)S(1)} %reshape.359, f32[1024]{0:T(1024)S(1)} %add_rsqrt_fusion.1, ...), kind=kOutput, calls=%fused_computation.112 | convolution fusion | flops 4837342208 | bytes 17323008 | tf_op jit(solution)/shard_map/dot_general | solution.py:374
  185.4 5.5 %all-to-all-start.3 = ((bf16[8,2,64,768]{3,2,1,0:T(8,128)(2,1)}), bf16[8,2,64,768]{3,2,1,0:T(8,128)(2,1)S(1)}, u32[]{:S(2)}, u32[]{:S(2)}) async-start(bf16[8,2,64,768]{3,2,1,0:T(8,128)(2,1)} %bitcast.95), calls=%async_computation.3 | async-start | bytes 3145728 | tf_op jit(solution)/shard_map/all_to_all | solution.py:536
  190.9 14.1 %convert_reduce_fusion = (f32[3072]{0:T(1024)}, bf16[1024,3072]{1,0:T(8,128)(2,1)}) fusion(f32[1024,3072]{1,0:T(8,128)} %get-tuple-element.253, f32[3072]{0:T(1024)S(1)} %reshape.361, bf16[1024,768]{1,0:T(8,128)(2,1)S(1)} %copy-done.5, bf16[3072,768]{1,0:T(8,128)(2,1)} %stack.19), kind=kOutput, calls=%fused_computation.9 | convolution fusion | flops 4872729600 | bytes 25190400 | tf_op jit(solution)/shard_map/to,io->ti/dot_general | solution.py:382
  205.0 10.9 %grad_down.1._ = bf16[768,6144]{1,0:T(8,128)(2,1)} custom-call(bf16[1024,3072]{1,0:T(8,128)(2,1)} %get-tuple-element.252.refs_0_, bf16[1024,768]{1,0:T(8,128)(2,1)} %get-tuple-element.144.refs_1_), custom_call_target="tpu_custom_call" | custom-call | bytes 3072 | tf_op jit(solution)/shard_map/grad_down/pallas_call | solution.py:186
  215.9 10.3 %grad_up.1 = bf16[768,6144]{1,0:T(8,128)(2,1)} custom-call(bf16[1024,768]{1,0:T(8,128)(2,1)} %copy-done.6, bf16[1024,3072]{1,0:T(8,128)(2,1)} %get-tuple-element.146.right_ref, bf16[768,6144]{1,0:T(8,128)(2,1)} %grad_down.1._), custom_call_target="tpu_custom_call", output_to_operand_aliasing={{}: (2, {})} | custom-call | bytes 12288 | tf_op jit(solution)/shard_map/grad_up/pallas_call | solution.py:214
  232.4 4.8 %all-to-all-start.4 = ((bf16[8,2,64,768]{3,2,1,0:T(8,128)(2,1)}), bf16[8,2,64,768]{3,2,1,0:T(8,128)(2,1)}, u32[]{:S(2)}, u32[]{:S(2)}) async-start(bf16[8,2,64,768]{3,2,1,0:T(8,128)(2,1)} %bitcast.104), calls=%async_computation.4 | async-start | bytes 3145728 | tf_op jit(solution)/shard_map/all_to_all | solution.py:543
  237.2 11.0 %multiply_reduce_fusion = (f32[768]{0:T(1024)}, f32[1024]{0:T(1024)S(1)}, f32[1024]{0:T(1024)S(1)}, f32[768]{0:T(1024)}, f32[1024,768]{1,0:T(8,128)S(1)}) fusion(f32[1024,768]{1,0:T(8,128)S(1)} %copy-done.3, f32[1024]{0:T(1024)S(1)} %add_rsqrt_fusion.1, f32[1024]{0:T(1024)S(1)} %broadcast_multiply_fusion.4, f32[768]{0:T(1024)S(1)} %reshape.359, ...), kind=kOutput, calls=%fused_computation.19 | convolution fusion | flops 4839698432 | bytes 20472832 | tf_op jit(solution)/shard_map/to,io->ti/dot_general | solution.py:382
  256.1 13.5 %attend_back.2 = (bf16[1024,1152]{1,0:T(8,128)(2,1)}, f32[2,2,384]{2,1,0:T(2,128)}) custom-call(s32[2]{0:T(128)} %copy-done.33, bf16[1024,2304]{1,0:T(8,128)(2,1)} %add_convert_fusion.refs_1_.fused_ref, f32[2,6,2,512]{3,2,1,0:T(2,128)} %copy-done.31, bf16[1024,768]{1,0:T(8,128)(2,1)} %convolution_convert_fusion.4.up_ref), custom_call_target="tpu_custom_call" | custom-call | flops 8053063680 | bytes 6291456 | tf_op jit(solution)/shard_map/attend_back/pallas_call | solution.py:494
  281.5 4.5 %fold_plane.2 = (bf16[4,24,1920]{2,1,0:T(8,128)(2,1)}, bf16[4,24,1920]{2,1,0:T(8,128)(2,1)}, bf16[4,24,1920]{2,1,0:T(8,128)(2,1)}, bf16[4,24,1920]{2,1,0:T(8,128)(2,1)}) custom-call(s32[4]{0:T(128)} %pad_add_fusion.refs_0_, bf16[2,4,2,24,768]{4,3,2,1,0:T(8,128)(2,1)} %bitcast.127, bf16[2,4,2,24,1152]{4,3,2,1,0:T(8,128)(2,1)} %bitcast.119, ...), custom_call_target="tpu_custom_call" | custom-call | bytes 4423680 | tf_op jit(solution)/shard_map/fold_plane/pallas_call | solution.py:283
  289.6 13.6 %attend_back.3 = (bf16[1024,1152]{1,0:T(8,128)(2,1)}, f32[2,2,384]{2,1,0:T(2,128)}) custom-call(s32[2]{0:T(128)} %copy-done.33, bf16[1024,2304]{1,0:T(8,128)(2,1)} %add_convert_fusion.refs_1_.fused_ref, f32[2,6,2,512]{3,2,1,0:T(2,128)} %copy-done.31, bf16[1024,768]{1,0:T(8,128)(2,1)} %convolution_convert_fusion.4.up_ref), custom_call_target="tpu_custom_call" | custom-call | flops 8053063680 | bytes 6291456 | tf_op jit(solution)/shard_map/attend_back/pallas_call | solution.py:494
  333.0 7.1 %all-to-all-start.5 = ((f32[32,1,288]{2,1,0:T(1,128)}), f32[32,1,288]{2,1,0:T(1,128)}, u32[]{:S(2)}, u32[]{:S(2)}) async-start(f32[32,1,288]{2,1,0:T(1,128)} %all_to_all.33), calls=%async_computation.5 | async-start | bytes 98304 | tf_op jit(solution)/shard_map/all_to_all | solution.py:709
  361.3 8.6 %collective-permute-done.20 = bf16[24,3072]{1,0:T(8,128)(2,1)S(1)} collective-permute-done((bf16[24,3072]{1,0:T(8,128)(2,1)}, bf16[24,3072]{1,0:T(8,128)(2,1)S(1)}, u32[]{:S(2)}, u32[]{:S(2)}) %collective-permute-start.20) | collective-permute-done | bytes 147488 | tf_op jit(solution)/shard_map/ppermute | solution.py:268
  374.2 8.7 %reduce-scatter.2.cloned.1.call-done = bf16[24,6144]{1,0:T(8,128)(2,1)} async-done(((bf16[768,6144]{1,0:T(8,128)(2,1)}), bf16[24,6144]{1,0:T(8,128)(2,1)}) %reduce-scatter.2.cloned.1.call-update) | async-done | bytes 294928 | tf_op jit(solution)/shard_map/reduce_scatter | solution.py:660
  (233 shorter events, 149.8 us)
Async XLA Ops:
  7.2 130.4 %all-gather.2.cloned.1.call-start = ((), (), s32[]{:S(2)}) async-start(), calls=%async_computation.7 | async-start | bytes 10948608 | tf_op jit(solution)/shard_map/all_gather | solution.py:587
  9.2 12.6 %collective-permute-start = (bf16[24,2304]{1,0:T(8,128)(2,1)}, bf16[24,2304]{1,0:T(8,128)(2,1)S(1)}, u32[]{:S(2)}, u32[]{:S(2)}) collective-permute-start(bf16[24,2304]{1,0:T(8,128)(2,1)} %get-tuple-element.113), channel_id=1, source_target_pairs={{0,2},{1,3},{2,0},{3,1},{4,6},{5,7},{6,4},{7,5},{8,10},{9,11},{10,... | collective-permute-start | bytes 331784 | tf_op jit(solution)/shard_map/ppermute | solution.py:65
  12.4 11.6 %collective-permute-start.1 = (bf16[24,2304]{1,0:T(8,128)(2,1)}, bf16[24,2304]{1,0:T(8,128)(2,1)S(1)}, u32[]{:S(2)}, u32[]{:S(2)}) collective-permute-start(bf16[24,2304]{1,0:T(8,128)(2,1)} %get-tuple-element.113), channel_id=1, source_target_pairs={{0,4},{1,5},{2,6},{3,7},{4,0},{5,1},{6,2},{7,3},{8,12},{9,13},{10,... | collective-permute-start | bytes 331784 | tf_op jit(solution)/shard_map/ppermute | solution.py:65
  25.8 12.4 %all-to-all-start = ((bf16[32,2,144]{2,1,0:T(2,128)(2,1)}), bf16[32,2,144]{2,1,0:T(2,128)(2,1)S(1)}, u32[]{:S(2)}, u32[]{:S(2)}) async-start(bf16[32,2,144]{2,1,0:T(2,128)(2,1)} %reshape.397), calls=%async_computation | async-start | bytes 65536 | tf_op jit(solution)/shard_map/all_to_all | solution.py:595
  38.3 87.4 %all-to-all-start.1 = ((bf16[8,2,64,768]{3,2,1,0:T(8,128)(2,1)}), bf16[8,2,64,768]{3,2,1,0:T(8,128)(2,1)S(1)}, u32[]{:S(2)}, u32[]{:S(2)}) async-start(bf16[8,2,64,768]{3,2,1,0:T(8,128)(2,1)} %copy.89), calls=%async_computation.1 | async-start | bytes 3145728 | tf_op jit(solution)/shard_map/all_to_all | solution.py:601
  43.7 35.5 %collective-permute-start.4 = (bf16[4,24,2304]{2,1,0:T(8,128)(2,1)}, bf16[4,24,2304]{2,1,0:T(8,128)(2,1)}, u32[]{:S(2)}, u32[]{:S(2)}) collective-permute-start(bf16[4,24,2304]{2,1,0:T(8,128)(2,1)} %select_select_fusion.refs_1_), channel_id=1, source_target_pairs={{0,1},{1,0},{2,3},{3,2},{4,5},{5,4},{6,7},{7,6},{8,9},{9,8},{10,11... | collective-permute-start | bytes 1327112 | tf_op jit(solution)/shard_map/ppermute | solution.py:65
  45.6 33.6 %collective-permute-start.5 = (bf16[4,24,2304]{2,1,0:T(8,128)(2,1)}, bf16[4,24,2304]{2,1,0:T(8,128)(2,1)}, u32[]{:S(2)}, u32[]{:S(2)}) collective-permute-start(bf16[4,24,2304]{2,1,0:T(8,128)(2,1)} %select_select_fusion.refs_1_), channel_id=1, source_target_pairs={{0,16},{1,17},{2,18},{3,19},{4,20},{5,21},{6,22},{7,23},{8,24},{9,... | collective-permute-start | bytes 1327112 | tf_op jit(solution)/shard_map/ppermute | solution.py:65
  46.2 43.3 %collective-permute-start.6 = (bf16[4,24,2304]{2,1,0:T(8,128)(2,1)}, bf16[4,24,2304]{2,1,0:T(8,128)(2,1)}, u32[]{:S(2)}, u32[]{:S(2)}) collective-permute-start(bf16[4,24,2304]{2,1,0:T(8,128)(2,1)} %select_select_fusion.refs_1_), channel_id=1, source_target_pairs={{0,17},{1,16},{2,19},{3,18},{4,21},{5,20},{6,23},{7,22},{8,25},{9,... | collective-permute-start | bytes 1327112 | tf_op jit(solution)/shard_map/ppermute | solution.py:65
  49.1 42.0 %collective-permute-start.3 = (bf16[4,24,2304]{2,1,0:T(8,128)(2,1)}, bf16[4,24,2304]{2,1,0:T(8,128)(2,1)S(1)}, u32[]{:S(2)}, u32[]{:S(2)}) collective-permute-start(bf16[4,24,2304]{2,1,0:T(8,128)(2,1)} %select_select_fusion.refs_1_), channel_id=1, source_target_pairs={{0,8},{1,9},{2,10},{3,11},{4,12},{5,13},{6,14},{7,15},{8,0},{9,1},... | collective-permute-start | bytes 1327112 | tf_op jit(solution)/shard_map/ppermute | solution.py:65
  131.6 42.2 %all-to-all-start.2 = ((bf16[8,2,64,768]{3,2,1,0:T(8,128)(2,1)}), bf16[8,2,64,768]{3,2,1,0:T(8,128)(2,1)}, u32[]{:S(2)}, u32[]{:S(2)}) async-start(bf16[8,2,64,768]{3,2,1,0:T(8,128)(2,1)} %bitcast.105), calls=%async_computation.2 | async-start | bytes 3145728 | tf_op jit(solution)/shard_map/all_to_all | solution.py:543
  185.4 42.3 %all-to-all-start.3 = ((bf16[8,2,64,768]{3,2,1,0:T(8,128)(2,1)}), bf16[8,2,64,768]{3,2,1,0:T(8,128)(2,1)S(1)}, u32[]{:S(2)}, u32[]{:S(2)}) async-start(bf16[8,2,64,768]{3,2,1,0:T(8,128)(2,1)} %bitcast.95), calls=%async_computation.3 | async-start | bytes 3145728 | tf_op jit(solution)/shard_map/all_to_all | solution.py:536
  190.9 192.1 %reduce-scatter.2.cloned.1.call-start = ((), (), s32[]{:S(2)}) async-start(), calls=%async_computation.8 | async-start | bytes 9732096 | tf_op jit(solution)/shard_map/reduce_scatter | solution.py:660
  232.4 49.1 %all-to-all-start.4 = ((bf16[8,2,64,768]{3,2,1,0:T(8,128)(2,1)}), bf16[8,2,64,768]{3,2,1,0:T(8,128)(2,1)}, u32[]{:S(2)}, u32[]{:S(2)}) async-start(bf16[8,2,64,768]{3,2,1,0:T(8,128)(2,1)} %bitcast.104), calls=%async_computation.4 | async-start | bytes 3145728 | tf_op jit(solution)/shard_map/all_to_all | solution.py:543
  286.0 21.2 %collective-permute-start.12 = (bf16[4,24,1920]{2,1,0:T(8,128)(2,1)}, bf16[4,24,1920]{2,1,0:T(8,128)(2,1)}, u32[]{:S(2)}, u32[]{:S(2)}) collective-permute-start(bf16[4,24,1920]{2,1,0:T(8,128)(2,1)} %get-tuple-element.169), channel_id=1, source_target_pairs={{0,1},{1,0},{2,3},{3,2},{4,5},{5,4},{6,7},{7,6},{8,9},{9,8},{10,11... | collective-permute-start | bytes 1105928 | tf_op jit(solution)/shard_map/ppermute | solution.py:268
  288.1 19.2 %collective-permute-start.13 = (bf16[4,24,1920]{2,1,0:T(8,128)(2,1)}, bf16[4,24,1920]{2,1,0:T(8,128)(2,1)}, u32[]{:S(2)}, u32[]{:S(2)}) collective-permute-start(bf16[4,24,1920]{2,1,0:T(8,128)(2,1)} %get-tuple-element.170), channel_id=1, source_target_pairs={{0,16},{1,17},{2,18},{3,19},{4,20},{5,21},{6,22},{7,23},{8,24},{9,... | collective-permute-start | bytes 1105928 | tf_op jit(solution)/shard_map/ppermute | solution.py:268
  288.1 19.8 %collective-permute-start.14 = (bf16[4,24,1920]{2,1,0:T(8,128)(2,1)}, bf16[4,24,1920]{2,1,0:T(8,128)(2,1)}, u32[]{:S(2)}, u32[]{:S(2)}) collective-permute-start(bf16[4,24,1920]{2,1,0:T(8,128)(2,1)} %get-tuple-element.171), channel_id=1, source_target_pairs={{0,17},{1,16},{2,19},{3,18},{4,21},{5,20},{6,23},{7,22},{8,25},{9,... | collective-permute-start | bytes 1105928 | tf_op jit(solution)/shard_map/ppermute | solution.py:268
  307.8 11.8 %collective-permute-start.15 = (bf16[384,1152]{1,0:T(8,128)(2,1)}, bf16[384,1152]{1,0:T(8,128)(2,1)}, u32[]{:S(2)}, u32[]{:S(2)}) collective-permute-start(bf16[384,1152]{1,0:T(8,128)(2,1)} %convolution_convert_fusion.1), channel_id=1, source_target_pairs={{0,8},{1,9},{2,10},{3,11},{4,12},{5,13},{6,14},{7,15},{8,0},{9,1},... | collective-permute-start | bytes 2654216 | tf_op jit(solution)/shard_map/ppermute | solution.py:268
  323.8 25.1 %collective-permute-start.16 = (bf16[4,24,1152]{2,1,0:T(8,128)(2,1)}, bf16[4,24,1152]{2,1,0:T(8,128)(2,1)}, u32[]{:S(2)}, u32[]{:S(2)}) collective-permute-start(bf16[4,24,1152]{2,1,0:T(8,128)(2,1)} %get-tuple-element.182), channel_id=1, source_target_pairs={{0,1},{1,0},{2,3},{3,2},{4,5},{5,4},{6,7},{7,6},{8,9},{9,8},{10,11... | collective-permute-start | bytes 663560 | tf_op jit(solution)/shard_map/ppermute | solution.py:268
  325.5 23.4 %collective-permute-start.17 = (bf16[4,24,1152]{2,1,0:T(8,128)(2,1)}, bf16[4,24,1152]{2,1,0:T(8,128)(2,1)}, u32[]{:S(2)}, u32[]{:S(2)}) collective-permute-start(bf16[4,24,1152]{2,1,0:T(8,128)(2,1)} %get-tuple-element.183), channel_id=1, source_target_pairs={{0,16},{1,17},{2,18},{3,19},{4,20},{5,21},{6,22},{7,23},{8,24},{9,... | collective-permute-start | bytes 663560 | tf_op jit(solution)/shard_map/ppermute | solution.py:268
  327.8 21.1 %collective-permute-start.18 = (bf16[4,24,1152]{2,1,0:T(8,128)(2,1)}, bf16[4,24,1152]{2,1,0:T(8,128)(2,1)}, u32[]{:S(2)}, u32[]{:S(2)}) collective-permute-start(bf16[4,24,1152]{2,1,0:T(8,128)(2,1)} %get-tuple-element.184), channel_id=1, source_target_pairs={{0,17},{1,16},{2,19},{3,18},{4,21},{5,20},{6,23},{7,22},{8,25},{9,... | collective-permute-start | bytes 663560 | tf_op jit(solution)/shard_map/ppermute | solution.py:268
  333.0 14.5 %all-to-all-start.5 = ((f32[32,1,288]{2,1,0:T(1,128)}), f32[32,1,288]{2,1,0:T(1,128)}, u32[]{:S(2)}, u32[]{:S(2)}) async-start(f32[32,1,288]{2,1,0:T(1,128)} %all_to_all.33), calls=%async_computation.5 | async-start | bytes 98304 | tf_op jit(solution)/shard_map/all_to_all | solution.py:709
  352.3 9.0 %collective-permute-start.21 = (bf16[24,3072]{1,0:T(8,128)(2,1)}, bf16[24,3072]{1,0:T(8,128)(2,1)S(1)}, u32[]{:S(2)}, u32[]{:S(2)}) collective-permute-start(bf16[24,3072]{1,0:T(8,128)(2,1)} %get-tuple-element.201), channel_id=1, source_target_pairs={{0,6},{1,7},{2,4},{3,5},{4,2},{5,3},{6,0},{7,1},{8,14},{9,15},{10,... | collective-permute-start | bytes 442376 | tf_op jit(solution)/shard_map/ppermute | solution.py:268
  354.0 15.9 %collective-permute-start.20 = (bf16[24,3072]{1,0:T(8,128)(2,1)}, bf16[24,3072]{1,0:T(8,128)(2,1)S(1)}, u32[]{:S(2)}, u32[]{:S(2)}) collective-permute-start(bf16[24,3072]{1,0:T(8,128)(2,1)} %get-tuple-element.200), channel_id=1, source_target_pairs={{0,4},{1,5},{2,6},{3,7},{4,0},{5,1},{6,2},{7,3},{8,12},{9,13},{10,... | collective-permute-start | bytes 442376 | tf_op jit(solution)/shard_map/ppermute | solution.py:268
  354.2 15.7 %collective-permute-start.19 = (bf16[24,3072]{1,0:T(8,128)(2,1)}, bf16[24,3072]{1,0:T(8,128)(2,1)S(1)}, u32[]{:S(2)}, u32[]{:S(2)}) collective-permute-start(bf16[24,3072]{1,0:T(8,128)(2,1)} %get-tuple-element.199), channel_id=1, source_target_pairs={{0,2},{1,3},{2,0},{3,1},{4,6},{5,7},{6,4},{7,5},{8,10},{9,11},{10,... | collective-permute-start | bytes 442376 | tf_op jit(solution)/shard_map/ppermute | solution.py:268
  (43 other events, 278.9 us)
Sparse Core Ops, SparseCore 0:
  11.0 115.9 all-gather.1
  227.9 155.0 reduce-scatter.1
